TPU v7x, 32 devices: a whole 2x2x4 slice. The times are simulated.
32 devices in a mesh: fsdp: 32 (over z, y, x, core).
Axes of the slice: x: 2, y: 2, z: 4, core: 2. Of those that a mesh axis runs over, the one named last changes fastest.
Arguments:
- block_input: bfloat16 [32768, 768], P('fsdp'), may hold values from -6 to 6
- seg_ids: int32 [64, 512], P('fsdp'), may hold values from 0 to 3, never falling along the last dimension, each value on 1 to 256 neighbouring positions
- masked: int32 [64, 512], P('fsdp'), may hold values 0 or 1
- out_grad: bfloat16 [32768, 768], P('fsdp'), may hold values from -6 to 6
- att_master: float32 [18496, 128], P('fsdp'), may hold values from -3 to 3, as said below
- att_moment: float32 [18496, 128], P('fsdp'), as said below
- att_average: float32 [18496, 128], P('fsdp'), may hold values from -3 to 3, as said below
- ffn_master: float32 [36928, 128], P('fsdp'), may hold values from -1 to 2, as said below
- ffn_moment: float32 [36928, 128], P('fsdp'), as said below
- ffn_average: float32 [36928, 128], P('fsdp'), may hold values from -1 to 2, as said below
Outputs:
- block_output: bfloat16 [32768, 768], P('fsdp')
- input_grad: float32 [32768, 768], P('fsdp')
- att_master_new: float32 [18496, 128], P('fsdp')
- att_moment_new: float32 [18496, 128], P('fsdp')
- att_average_new: float32 [18496, 128], P('fsdp')
- att_master_low: bfloat16 [18496, 128], P('fsdp')
- ffn_master_new: float32 [36928, 128], P('fsdp')
- ffn_moment_new: float32 [36928, 128], P('fsdp')
- ffn_average_new: float32 [36928, 128], P('fsdp')
- ffn_master_low: bfloat16 [36928, 128], P('fsdp')
Inputs may be any that keep to these rules, and one draw needn't show every extreme that they name: `att_master`: entries after the first 2363904 of the vector are zero. `att_average`: entries after the first 2363904 of the vector are zero. `att_moment`: entries after the first 2363904 of the vector are zero; the others have a spread of the order of the root of 32768. `ffn_master`: entries after the first 4723968 of the vector are zero. `ffn_average`: entries after the first 4723968 of the vector are zero. `ffn_moment`: entries after the first 4723968 of the vector are zero; the others have a spread of the order of the root of 32768.
All inputs are finite; a program needn't handle non-finite values. No bound on the sum of `masked` on one device may be relied on, other than what follows from the above.
Results may differ from a plain program's by a relative error of at most 0.012.
The roundings to bfloat16 on the way count: a program that leaves them out, or rounds other values in their place, can miss the bound.
Values may be sent and summed in bfloat16 or wider, within the bound.
No kernel may reach another device: no remote copies, remote signals or barrier semaphores. Data moves between devices by JAX's collectives and lax.ppermute only.
A program may use at most 192 MiB of HBM per device.

v0:
```python
import math

import jax
import jax.numpy as jnp
from jax import lax
from jax.sharding import PartitionSpec as P

HEAD_DIM = 64
FF = 3072


EPSILON = 1e-05
MASKED_SCORE = -1e30


def layer_norm(pre_norm, gain, shift):
    center = pre_norm - jnp.mean(pre_norm, axis=-1, keepdims=True)
    spread = jnp.mean(center * center, axis=-1, keepdims=True)
    return center * lax.rsqrt(spread + EPSILON) * gain + shift


def gelu_exact(inputs):
    return jax.nn.gelu(inputs, approximate=False)


def unpack_attention(flat_att, model_width):
    square = model_width * model_width
    att_mats = flat_att[: 4 * square].reshape(4, model_width, model_width)
    small_params = flat_att[4 * square : 4 * square + 6 * model_width].reshape(6, model_width)
    return (att_mats, small_params)


def unpack_ffn(flat_ffn, model_width, hidden):
    size_in = model_width * hidden
    weight_in = flat_ffn[:size_in].reshape(model_width, hidden)
    weight_out = flat_ffn[size_in : 2 * size_in].reshape(hidden, model_width)
    offset = 2 * size_in
    bias_in = flat_ffn[offset : offset + hidden]
    small_params = flat_ffn[offset + hidden : offset + hidden + 3 * model_width].reshape(
        3, model_width
    )
    return (weight_in, weight_out, bias_in, small_params)


def pack_rows(pieces, row_count):
    filled = sum((piece.shape[0] for piece in pieces))
    padding = jnp.zeros((row_count * 128 - filled,), jnp.float32)
    return jnp.concatenate(list(pieces) + [padding]).reshape(row_count, 128)


def attend_forward(block_items):
    query_block, key_block, value_block, doc_block = block_items
    scores = jnp.einsum("qhd,khd->hqk", query_block, key_block, preferred_element_type=jnp.float32)
    same_doc = doc_block[:, None] == doc_block[None, :]
    scores = jnp.where(same_doc[None], scores, MASKED_SCORE)
    row_max = jnp.max(scores, axis=-1, keepdims=True)
    exponent = jnp.exp(scores - row_max)
    row_total = jnp.sum(exponent, axis=-1, keepdims=True)
    attn_probs = (exponent / row_total).astype(jnp.bfloat16)
    context = jnp.einsum(
        "hqk,khd->qhd", attn_probs, value_block, preferred_element_type=jnp.float32
    )
    return (context.astype(jnp.bfloat16), (row_max + jnp.log(row_total))[..., 0])


def attend_backward(block_items):
    query_block, key_block, value_block, doc_block, log_total, grad_context = block_items
    scores = jnp.einsum("qhd,khd->hqk", query_block, key_block, preferred_element_type=jnp.float32)
    same_doc = doc_block[:, None] == doc_block[None, :]
    scores = jnp.where(same_doc[None], scores, MASKED_SCORE)
    attn_probs = jnp.exp(scores - log_total[..., None])
    probs_low = attn_probs.astype(jnp.bfloat16)
    grad_probs = jnp.einsum(
        "qhd,khd->hqk", grad_context, value_block, preferred_element_type=jnp.float32
    )
    row_inner = jnp.sum(grad_probs * attn_probs, axis=-1, keepdims=True)
    grad_scores = (attn_probs * (grad_probs - row_inner)).astype(jnp.bfloat16)
    grad_query = jnp.einsum(
        "hqk,khd->qhd", grad_scores, key_block, preferred_element_type=jnp.float32
    ).astype(jnp.bfloat16)
    grad_key = jnp.einsum(
        "hqk,qhd->khd", grad_scores, query_block, preferred_element_type=jnp.float32
    ).astype(jnp.bfloat16)
    grad_value = jnp.einsum(
        "hqk,qhd->khd", probs_low, grad_context, preferred_element_type=jnp.float32
    ).astype(jnp.bfloat16)
    return (grad_query, grad_key, grad_value)


def nesterov(master, moment, average, gradient, step_rate):
    moment_new = 0.5 * moment + gradient
    master_new = master - step_rate * (gradient + 0.5 * moment_new)
    average_new = 0.5 * average + 0.5 * master_new
    return (master_new, moment_new, average_new, master_new.astype(jnp.bfloat16))


def local(
    block_input,
    seg_ids,
    masked,
    out_grad,
    att_master,
    att_moment,
    att_average,
    ffn_master,
    ffn_moment,
    ffn_average,
):
    tok_rows, model_width = block_input.shape
    seq_count, seq_length = seg_ids.shape
    head_count = model_width // HEAD_DIM
    devices = lax.axis_size("fsdp")
    att_rows = att_master.shape[0] * devices
    ffn_rows = ffn_master.shape[0] * devices
    head_shape = (seq_count, seq_length, head_count, HEAD_DIM)
    att_whole = lax.all_gather(att_master.astype(jnp.bfloat16), "fsdp", axis=0, tiled=True)
    att_mats, att_small_low = unpack_attention(att_whole.reshape(-1), model_width)
    att_small = att_small_low.astype(jnp.float32)
    masked_rows = masked.reshape(tok_rows, 1) == 1
    stream_in = jnp.where(masked_rows, att_small[5][None, :], block_input.astype(jnp.float32))
    stream_low = stream_in.astype(jnp.bfloat16)
    projected = jnp.einsum(
        "td,cde->cte", stream_low, att_mats[:3], preferred_element_type=jnp.float32
    )
    queries = ((projected[0] + att_small[0]) * 0.125).astype(jnp.bfloat16).reshape(head_shape)
    key_rows = projected[1].astype(jnp.bfloat16).reshape(head_shape)
    values = (projected[2] + att_small[1]).astype(jnp.bfloat16).reshape(head_shape)
    context, log_total = lax.map(attend_forward, (queries, key_rows, values, seg_ids))
    context_flat = context.reshape(tok_rows, model_width)
    pre_one = (
        stream_in
        + jnp.dot(context_flat, att_mats[3], preferred_element_type=jnp.float32)
        + att_small[2]
    )
    normed_one = layer_norm(pre_one, att_small[3], att_small[4])
    normed_low = normed_one.astype(jnp.bfloat16)
    ffn_whole = lax.all_gather(ffn_master.astype(jnp.bfloat16), "fsdp", axis=0, tiled=True)
    weight_in, weight_out, bias_in_low, ffn_small_low = unpack_ffn(
        ffn_whole.reshape(-1), model_width, FF
    )
    bias_in = bias_in_low.astype(jnp.float32)
    ffn_small = ffn_small_low.astype(jnp.float32)
    hid_pre = jnp.dot(normed_low, weight_in, preferred_element_type=jnp.float32) + bias_in
    hid_act = gelu_exact(hid_pre).astype(jnp.bfloat16)
    pre_two = (
        normed_one + jnp.dot(hid_act, weight_out, preferred_element_type=jnp.float32) + ffn_small[0]
    )
    normed_two, norm_two_pull = jax.vjp(layer_norm, pre_two, ffn_small[1], ffn_small[2])
    block_output = normed_two.astype(jnp.bfloat16)
    ffn_back = lax.all_gather(ffn_master.astype(jnp.bfloat16), "fsdp", axis=0, tiled=True)
    back_in, back_out, bias_unused, small_unused = unpack_ffn(ffn_back.reshape(-1), model_width, FF)
    grad_pre_two, grad_gain_two, grad_shift_two = norm_two_pull(out_grad.astype(jnp.float32))
    grad_branch_two = grad_pre_two.astype(jnp.bfloat16)
    grad_w_out = jnp.einsum(
        "tf,td->fd", hid_act, grad_branch_two, preferred_element_type=jnp.float32
    )
    grad_b_out = jnp.sum(grad_branch_two, axis=0, dtype=jnp.float32)
    grad_act = jnp.einsum(
        "td,fd->tf", grad_branch_two, back_out, preferred_element_type=jnp.float32
    )
    hid_unused, gelu_pull = jax.vjp(gelu_exact, hid_pre)
    grad_hidden = gelu_pull(grad_act)[0].astype(jnp.bfloat16)
    grad_w_in = jnp.einsum("td,tf->df", normed_low, grad_hidden, preferred_element_type=jnp.float32)
    grad_b_in = jnp.sum(grad_hidden, axis=0, dtype=jnp.float32)
    grad_normed_one = grad_pre_two + jnp.einsum(
        "tf,df->td", grad_hidden, back_in, preferred_element_type=jnp.float32
    )
    ffn_flat_grad = pack_rows(
        (
            grad_w_in.reshape(-1),
            grad_w_out.reshape(-1),
            grad_b_in,
            grad_b_out,
            grad_gain_two,
            grad_shift_two,
        ),
        ffn_rows,
    )
    ffn_grad = lax.psum_scatter(ffn_flat_grad, "fsdp", scatter_dimension=0, tiled=True)
    att_back = lax.all_gather(att_master.astype(jnp.bfloat16), "fsdp", axis=0, tiled=True)
    back_mats, small_back = unpack_attention(att_back.reshape(-1), model_width)
    pre_unused, norm_one_pull = jax.vjp(layer_norm, pre_one, att_small[3], att_small[4])
    grad_pre_one, grad_gain_one, grad_shift_one = norm_one_pull(grad_normed_one)
    grad_branch_one = grad_pre_one.astype(jnp.bfloat16)
    grad_w_o = jnp.einsum(
        "td,te->de", context_flat, grad_branch_one, preferred_element_type=jnp.float32
    )
    grad_b_o = jnp.sum(grad_branch_one, axis=0, dtype=jnp.float32)
    grad_context = jnp.einsum(
        "te,de->td", grad_branch_one, back_mats[3], preferred_element_type=jnp.float32
    ).astype(jnp.bfloat16)
    grad_q4, grad_k4, grad_v4 = lax.map(
        attend_backward,
        (queries, key_rows, values, seg_ids, log_total, grad_context.reshape(head_shape)),
    )
    grad_queries = grad_q4.reshape(tok_rows, model_width) * 0.125
    grad_keys = grad_k4.reshape(tok_rows, model_width)
    grad_values = grad_v4.reshape(tok_rows, model_width)
    grad_projected = jnp.stack([grad_queries, grad_keys, grad_values])
    grad_w_qkv = jnp.einsum(
        "td,cte->cde", stream_low, grad_projected, preferred_element_type=jnp.float32
    )
    grad_b_q = jnp.sum(grad_queries, axis=0, dtype=jnp.float32)
    grad_b_v = jnp.sum(grad_values, axis=0, dtype=jnp.float32)
    grad_stream = grad_pre_one + jnp.einsum(
        "cte,cde->td", grad_projected, back_mats[:3], preferred_element_type=jnp.float32
    )
    grad_mask_vector = jnp.sum(jnp.where(masked_rows, grad_stream, 0.0), axis=0)
    input_grad = jnp.where(masked_rows, 0.0, grad_stream)
    att_flat_grad = pack_rows(
        (
            grad_w_qkv.reshape(-1),
            grad_w_o.reshape(-1),
            grad_b_q,
            grad_b_v,
            grad_b_o,
            grad_gain_one,
            grad_shift_one,
            grad_mask_vector,
        ),
        att_rows,
    )
    att_grad = lax.psum_scatter(att_flat_grad, "fsdp", scatter_dimension=0, tiled=True)
    step_rate = 0.05 / math.sqrt(tok_rows * devices)
    att_new = nesterov(att_master, att_moment, att_average, att_grad, step_rate)
    ffn_new = nesterov(ffn_master, ffn_moment, ffn_average, ffn_grad, step_rate)
    return (
        block_output,
        input_grad,
        att_new[0],
        att_new[1],
        att_new[2],
        att_new[3],
        ffn_new[0],
        ffn_new[1],
        ffn_new[2],
        ffn_new[3],
    )


def solution(mesh):
    in_specs = (
        P("fsdp", None),
        P("fsdp", None),
        P("fsdp", None),
        P("fsdp", None),
        P("fsdp", None),
        P("fsdp", None),
        P("fsdp", None),
        P("fsdp", None),
        P("fsdp", None),
        P("fsdp", None),
    )
    out_specs = (
        P("fsdp", None),
        P("fsdp", None),
        P("fsdp", None),
        P("fsdp", None),
        P("fsdp", None),
        P("fsdp", None),
        P("fsdp", None),
        P("fsdp", None),
        P("fsdp", None),
        P("fsdp", None),
    )
    return jax.shard_map(local, mesh=mesh, in_specs=in_specs, out_specs=out_specs, check_vma=False)
```

profile of v0, /device:TPU:7, one launch (start us, length us, event | category | flops | bytes accessed | tf_op | source)
XLA Modules:
  0.0 812.6 jit_solution(7425068839208217309)
XLA Ops:
  10.9 2.6 copy.89
  15.2 61.0 %all-gather.5.cloned.1.call-done = bf16[32,578,128]{2,1,0:T(8,128)(2,1)} async-done(((bf16[1,578,128]{2,1,0:T(8,128)(2,1)}), bf16[32,578,128]{2,1,0:T(8,128)(2,1)}) %all-gather.5.cloned.1.call-update) | async-done | bytes 4734992 | tf_op jit(solution)/shard_map/all_gather | solution.py:116
  76.1 7.3 reshape.304
  83.4 2.3 copy-done.8
  86.9 4.5 slice.89
  92.8 6.6 convolution_bitcast_fusion.1
  100.7 2.1 fusion.89
  102.7 2.4 copy.81
  105.2 4.2 squeeze.39
  113.3 2.4 copy.82
  115.7 4.3 squeeze.40
  124.8 3.9 convert_element_type.131
  128.7 2.2 copy.86
  132.2 20.8 %while.26 = (s32[]{:T(128)}, bf16[2,512,12,64]{1,3,2,0:T(8,128)(2,1)}, f32[2,12,512]{2,1,0:T(8,128)}, bf16[2,512,12,64]{1,3,2,0:T(8,128)(2,1)}, s32[2,512]{1,0:T...) while((s32[]{:T(128)}, ...), condition=%wide.region_3.4_spmd, body=%wide.region_0.3_spmd.sunk | while | flops 834267136 | bytes 42156132 | solution.py:128
  134.8 2.2 fusion.130
  137.0 5.1 fusion.131
  143.0 1.9 select_reduce_fusion.3
  145.0 2.2 fusion.130
  147.1 5.2 fusion.131
  153.0 4.2 copy.87
  158.8 3.3 squeeze.41
  162.1 3.9 fusion.90
  166.5 11.0 %reshape.306 = bf16[36928,128]{1,0:T(8,128)(2,1)} reshape(bf16[32,1154,128]{2,1,0:T(8,128)(2,1)} %all-gather.7.cloned.1.call-done) | data formatting | bytes 18907136
  178.9 8.3 %fusion.88 = (bf16[18432,128]{1,0:T(8,128)(2,1)}, bf16[18432,128]{1,0:T(8,128)(2,1)}) fusion(bf16[36928,128]{1,0:T(8,128)(2,1)} %reshape.306), kind=kLoop, calls=%fused_computation.175 | loop fusion | bytes 18874368 | tf_op jit(solution)/shard_map/slice | solution.py:36
  187.3 8.2 %reshape.293 = bf16[768,3072]{1,0:T(8,128)(2,1)} reshape(bf16[18432,128]{1,0:T(8,128)(2,1)} %get-tuple-element.253) | data formatting | bytes 9437184 | tf_op jit(solution)/shard_map/reshape | solution.py:35
  195.5 9.4 %reshape.294 = bf16[3072,768]{1,0:T(8,128)(2,1)} reshape(bf16[18432,128]{1,0:T(8,128)(2,1)} %get-tuple-element.252) | data formatting | bytes 9437184 | tf_op jit(solution)/shard_map/reshape | solution.py:36
  205.0 37.3 %multiply_convert_fusion.1 = (bf16[1024,3072]{1,0:T(8,128)(2,1)S(1)}, f32[1024,3072]{1,0:T(8,128)}, f32[1024,3072]{1,0:T(8,128)}) fusion(f32[3072]{0:T(1024)S(1)} %fusion.74, bf16[768,3072]{1,0:T(8,128)(2,1)} %reshape.293, f32[1024,768]{0,1:T(8,128)S(1)} %get-tuple-element.271, f32[768]{0:T(1024)S(1)} %copy-done.59, f32[768]{0:T(1024)S(1)} %copy-done.48, ...), kind=kOutput, calls=%fused_computation.67 | convolution fusion | flops 5043388416 | bytes 39348224 | tf_op jit(solution)/shard_map/dot_general | solution.py:143
  242.3 10.1 %fusion.91 = (f32[1024]{0:T(1024)S(1)}, f32[1024,768]{0,1:T(8,128)S(1)}) fusion(f32[768]{0:T(1024)S(1)} %get-tuple-element.267, bf16[1024,3072]{1,0:T(8,128)(2,1)S(1)} %get-tuple-element.246, bf16[3072,768]{1,0:T(8,128)(2,1)S(1)} %copy-done.23, f32[768]{0:T(1024)S(1)} %copy-done.59, f32[768]{0:T(1024)S(1)} %copy-done.48, f32[1024]{0:T(1024)S(1)} %fusion.75, ...), kind=kOutput, calls=%fused_computation.178 | convolution fusion | flops 4837342208 | bytes 17323008 | tf_op jit(solution)/shard_map/dot_general | solution.py:146
  254.1 2.2 fusion.67
  256.4 3.3 convert_reduce_fusion.2
  259.6 18.1 %convert_reduce_fusion = (f32[3072]{0:T(1024)}, bf16[1024,3072]{1,0:T(8,128)(2,1)}) fusion(f32[1024,3072]{1,0:T(8,128)} %get-tuple-element.247, bf16[1024,768]{0,1:T(8,128)(2,1)S(1)} %get-tuple-element.241, bf16[3072,768]{1,0:T(8,128)(2,1)} %reshape.294, f32[1024,3072]{1,0:T(8,128)} %get-tuple-element.272, f32[3072]{0:T(1024)S(1)} %fusion.74), kind=kOutput, calls=%fused_computation.65 | convolution fusion | flops 4885312512 | bytes 37773312 | tf_op jit(solution)/shard_map/td,fd->tf/dot_general | solution.py:158
  277.8 11.4 %multiply_reduce_fusion.1 = (f32[768]{0:T(1024)}, f32[1024]{0:T(1024)S(1)}, f32[768]{0:T(1024)}, f32[1024,768]{0,1:T(8,128)S(1)}) fusion(f32[1024,768]{0,1:T(8,128)} %copy-done.13, f32[1024]{0:T(1024)S(1)} %fusion.75, f32[1024]{0:T(1024)S(1)} %broadcast_multiply_fusion.2, f32[768]{0:T(1024)S(1)} %copy-done.48, bf16[1024,3072]{1,0:T(8,128)(2,1)} %get-tuple-element.277, ...), kind=kOutput, calls=%fused_computation.97 | convolution fusion | flops 4845204480 | bytes 22061056 | tf_op jit(solution)/shard_map/tf,df->td/dot_general | solution.py:165
  302.7 48.2 %while.27 = (s32[]{:T(128)}, bf16[2,512,12,64]{1,3,2,0:T(8,128)(2,1)}, bf16[2,512,12,64]{1,3,2,0:T(8,128)(2,1)}, bf16[2,512,12,64]{1,3,2,0:T(8,128)(2,1)}, bf16[...) while((s32[]{:T(128)}, ...), condition=%wide.region_14.15_spmd, body=%wide.region_12.14_spmd.sunk | while | flops 2052450304 | bytes 147524944 | solution.py:192
  305.1 6.6 multiply_reduce_fusion.6
  311.6 7.1 multiply_convert_fusion.4
  320.1 2.0 fusion.142
  323.3 3.6 fusion.143
  329.1 6.6 multiply_reduce_fusion.6
  335.6 7.1 multiply_convert_fusion.4
  344.2 2.0 fusion.142
  347.3 3.6 fusion.143
  351.0 4.2 copy.98
  355.2 2.9 stack_reshape.7
  361.4 2.6 stack_reshape.6
  363.9 2.6 copy.100
  368.3 2.4 mul.247
  372.4 9.7 %select_reduce_fusion.1 = (f32[768]{0:T(1024)S(1)}, f32[1024,768]{0,1:T(8,128)}) fusion(pred[1024]{0:T(1024)(128)(4,1)S(1)} %copy-done.67, bf16[3,768,768]{2,1,0:T(8,128)(2,1)} %slice.89, bf16[1,1024,768]{2,1,0:T(8,128)(2,1)} %copy.101, bf16[1,1024,768]{2,1,0:T(8,128)(2,1)} %copy.100, bf16[1,1024,768]{2,1,0:T(8,128)(2,1)S(1)} %copy.99, ...), kind=kOutput, calls=%fused_computation.96 | convolution fusion | flops 3632528640 | bytes 14557184 | tf_op jit(solution)/shard_map/cte,cde->td/dot_general | solution.py:205
  382.1 6.2 convolution_bitcast_fusion.2
  388.4 2.8 fusion.92
  393.1 8.2 %convolution_bitcast_fusion = f32[96,24,8,128]{3,2,1,0:T(8,128)} fusion(bf16[1024,3072]{1,0:T(8,128)(2,1)S(1)} %bitcast.192, f32[1024,768]{0,1:T(8,128)S(1)} %copy-done.15, f32[768]{0:T(1024)S(1)} %copy-done.60, f32[768]{0:T(1024)S(1)} %copy-done.49, f32[1024]{0:T(1024)S(1)} %copy-done.53, f32[1024]{0:T(1024)S(1)} %copy-done.45), kind=kOutput, calls=%fused_computation.89 | convolution fusion | flops 4835770368 | bytes 18888704 | tf_op jit(solution)/shard_map/td,tf->df/dot_general | solution.py:163
  401.4 7.7 fusion.93
  409.1 8.1 copy.105
  417.2 8.2 %reshape.296 = f32[1769472]{0:T(1024)} reshape(f32[3,768,768]{2,1,0:T(8,128)} %copy.105) | data formatting | bytes 14155776 | tf_op jit(solution)/shard_map/reshape | solution.py:212
  425.4 5.2 constant_dynamic-update-slice_fusion.2
  430.6 2.3 reshape.297
  443.7 5.9 copy.122
  449.6 3.9 constant_dynamic-update-slice_fusion.3
  453.4 10.7 %reshape.300 = f32[2359296]{0:T(1024)} reshape(f32[3072,768]{1,0:T(8,128)} %fusion.93) | data formatting | bytes 18874368 | tf_op jit(solution)/shard_map/reshape | solution.py:171
  464.2 8.3 %constant_dynamic-update-slice_fusion.1 = f32[4726784]{0:T(1024)} fusion(f32[4726784]{0:T(1024)} %constant_dynamic-update-slice_fusion.3, f32[2359296]{0:T(1024)} %reshape.300), kind=kLoop, calls=%fused_computation.136 | loop fusion | bytes 18874368
  478.3 305.5 %fusion.83 = (f32[592,128]{1,0:T(8,128)S(1)}, f32[1168,128]{1,0:T(8,128)S(1)}) fusion(f32[18496,128]{1,0:T(8,128)} %bitcast.185, f32[36928,128]{1,0:T(8,128)} %bitcast.183), kind=kCustom, calls=%all-reduce-scatter.2 | all-reduce-scatter fusion | flops 7208962 | bytes 29278208
  788.1 3.6 copy.107
  791.7 3.1 collective-permute-start.1
  798.2 2.1 collective-permute-done.1
  802.1 2.2 fusion.84
  (256 shorter events, 86.0 us)
Async XLA Ops:
  7.2 6.3 copy-start.26
  7.2 68.9 %all-gather.5.cloned.1.call-start = ((), (), s32[]{:S(2)}) async-start(), calls=%async_computation | async-start | bytes 4933632 | tf_op jit(solution)/shard_map/all_gather | solution.py:116
  9.0 157.5 %all-gather.7.cloned.1.call-start = ((), (), s32[]{:S(2)}) async-start(), calls=%async_computation.1 | async-start | bytes 9799680 | tf_op jit(solution)/shard_map/all_gather | solution.py:137
  10.9 4.2 copy-start.63
  15.1 147.0 %copy-start.66 = (pred[1024]{0:T(1024)(128)(4,1)}, pred[1024]{0:T(1024)(128)(4,1)S(1)}, u32[]{:S(2)}) copy-start(pred[1024]{0:T(1024)(128)(4,1)S(1)} %eq.54) | copy-start | bytes 3076
  83.4 3.5 slice-start
  92.8 69.4 %copy-start.61 = (f32[768]{0:T(1024)}, f32[768]{0:T(1024)S(1)}, u32[]{:S(2)}) copy-start(f32[768]{0:T(1024)S(1)} %get-tuple-element.264) | copy-start | bytes 9220
  128.7 3.5 copy-start.42
  153.0 5.8 copy-start
  153.0 5.8 copy-start.2
  166.1 38.9 %copy-start.13 = (f32[1024,768]{0,1:T(8,128)}, f32[1024,768]{0,1:T(8,128)S(1)}, u32[]{:S(2)}) copy-start(f32[1024,768]{0,1:T(8,128)S(1)} %get-tuple-element.271) | copy-start | bytes 9437188
  166.1 123.1 %copy-start.44 = (f32[1024]{0:T(1024)}, f32[1024]{0:T(1024)S(1)}, u32[]{:S(2)}) copy-start(f32[1024]{0:T(1024)S(1)} %broadcast_multiply_fusion.2) | copy-start | bytes 12292
  166.5 11.1 %copy-start.46 = (f32[1024]{0:T(1024)}, f32[1024]{0:T(1024)S(1)}, u32[]{:S(2)}) copy-start(f32[1024]{0:T(1024)S(1)} %multiply_reduce_fusion.4) | copy-start | bytes 12292
  166.5 122.7 %copy-start.52 = (f32[1024]{0:T(1024)}, f32[1024]{0:T(1024)S(1)}, u32[]{:S(2)}) copy-start(f32[1024]{0:T(1024)S(1)} %fusion.75) | copy-start | bytes 12292
  195.5 9.5 %copy-start.48 = (f32[768]{0:T(1024)S(1)}, f32[768]{0:T(1024)}, u32[]{:S(2)}) copy-start(f32[768]{0:T(1024)} %get-tuple-element.259) | copy-start | bytes 9220
  195.5 9.5 %copy-start.59 = (f32[768]{0:T(1024)S(1)}, f32[768]{0:T(1024)}, u32[]{:S(2)}) copy-start(f32[768]{0:T(1024)} %get-tuple-element.260) | copy-start | bytes 9220
  205.0 37.3 %copy-start.23 = (bf16[3072,768]{1,0:T(8,128)(2,1)S(1)}, bf16[3072,768]{1,0:T(8,128)(2,1)}, u32[]{:S(2)}) copy-start(bf16[3072,768]{1,0:T(8,128)(2,1)} %reshape.294) | copy-start | bytes 14155780
  242.3 10.2 %copy-start.68 = (bf16[1024,3072]{1,0:T(8,128)(2,1)}, bf16[1024,3072]{1,0:T(8,128)(2,1)S(1)}, u32[]{:S(2)}) copy-start(bf16[1024,3072]{1,0:T(8,128)(2,1)S(1)} %get-tuple-element.246) | copy-start | bytes 18874372
  242.3 10.2 %copy-start.4 = (bf16[1024,768]{0,1:T(8,128)(2,1)S(1)}, bf16[1024,768]{0,1:T(8,128)(2,1)}, u32[]{:S(2)}) copy-start(bf16[1024,768]{0,1:T(8,128)(2,1)} %copy.89) | copy-start | bytes 4718596
  259.6 18.1 %copy-start.31 = (bf16[1024,768]{0,1:T(8,128)(2,1)}, bf16[1024,768]{0,1:T(8,128)(2,1)S(1)}, u32[]{:S(2)}) copy-start(bf16[1024,768]{0,1:T(8,128)(2,1)S(1)} %get-tuple-element.241) | copy-start | bytes 4718596
  277.8 11.4 %copy-start.47 = (f32[1024]{0:T(1024)S(1)}, f32[1024]{0:T(1024)}, u32[]{:S(2)}) copy-start(f32[1024]{0:T(1024)} %copy-done.46) | copy-start | bytes 12292
  277.8 11.5 %copy-start.14 = (f32[1024,768]{0,1:T(8,128)S(1)}, f32[1024,768]{0,1:T(8,128)}, u32[]{:S(2)}) copy-start(f32[1024,768]{0,1:T(8,128)} %copy-done.13) | copy-start | bytes 9437188
  290.0 3.7 copy-start.37
  290.1 2.5 copy-start.55
  298.7 4.0 copy-start.1
  298.7 4.0 copy-start.3
  298.7 4.0 copy-start.39
  298.7 4.0 copy-start.43
  311.6 7.1 copy-start.9
  320.1 3.2 copy-start.7
  335.6 7.1 copy-start.9
  344.2 3.2 copy-start.7
  355.2 4.5 copy-start.21
  361.4 5.1 copy-start.11
  368.3 4.1 copy-start.56
  368.3 4.1 copy-start.67
  372.4 9.7 %copy-start.27 = (bf16[1024,768]{0,1:T(8,128)(2,1)S(1)}, bf16[1024,768]{0,1:T(8,128)(2,1)}, u32[]{:S(2)}) copy-start(bf16[1024,768]{0,1:T(8,128)(2,1)} %copy.79) | copy-start | bytes 4718596
  372.4 9.7 %copy-start.29 = (bf16[1,1024,768]{2,1,0:T(8,128)(2,1)S(1)}, bf16[1,1024,768]{2,1,0:T(8,128)(2,1)}, u32[]{:S(2)}) copy-start(bf16[1,1024,768]{2,1,0:T(8,128)(2,1)} %copy.101) | copy-start | bytes 4718596
  372.4 9.7 %copy-start.30 = (bf16[1,1024,768]{2,1,0:T(8,128)(2,1)S(1)}, bf16[1,1024,768]{2,1,0:T(8,128)(2,1)}, u32[]{:S(2)}) copy-start(bf16[1,1024,768]{2,1,0:T(8,128)(2,1)} %copy.100) | copy-start | bytes 4718596
  372.4 9.7 %copy-start.62 = (f32[768]{0:T(1024)S(1)}, f32[768]{0:T(1024)}, u32[]{:S(2)}) copy-start(f32[768]{0:T(1024)} %copy-done.61) | copy-start | bytes 9220
  372.4 19.4 %slice-start.1 = ((s8[6291456]{0:T(1024)(128)(4,1)}), s8[4194304]{0:T(1024)(128)(4,1)S(1)}, s32[]{:S(2)}) async-start(s8[6291456]{0:T(1024)(128)(4,1)} %bitcast.191), calls=%async_computation.3 | async-start | bytes 8388608
  382.1 6.3 copy-start.28
  382.1 6.3 copy-start.34
  382.1 9.7 %slice-start.2 = ((s8[6291456]{0:T(1024)(128)(4,1)}), s8[2097152]{0:T(1024)(128)(4,1)S(1)}, s32[]{:S(2)}) async-start(s8[6291456]{0:T(1024)(128)(4,1)} %bitcast.191), calls=%async_computation.4 | async-start | bytes 4194304
  388.4 2.8 copy-start.12
  391.2 10.1 %slice-start.3 = ((s8[6291456]{0:T(1024)(128)(4,1)}), s8[4194304]{0:T(1024)(128)(4,1)S(1)}, s32[]{:S(2)}) async-start(s8[6291456]{0:T(1024)(128)(4,1)} %bitcast.193), calls=%async_computation.5 | async-start | bytes 8388608
  393.1 8.2 %copy-start.32 = (bf16[1024,768]{0,1:T(8,128)(2,1)S(1)}, bf16[1024,768]{0,1:T(8,128)(2,1)}, u32[]{:S(2)}) copy-start(bf16[1024,768]{0,1:T(8,128)(2,1)} %copy-done.31) | copy-start | bytes 4718596
  393.1 8.2 %slice-start.4 = ((s8[6291456]{0:T(1024)(128)(4,1)}), s8[2097152]{0:T(1024)(128)(4,1)S(1)}, s32[]{:S(2)}) async-start(s8[6291456]{0:T(1024)(128)(4,1)} %bitcast.193), calls=%async_computation.6 | async-start | bytes 4194304
  432.9 4.3 copy-start.54
  432.9 5.6 copy-start.65
  432.9 6.9 copy-start.64
  464.2 8.4 %copy-start.58 = (f32[3072]{0:T(1024)S(1)}, f32[3072]{0:T(1024)}, u32[]{:S(2)}) copy-start(f32[3072]{0:T(1024)} %get-tuple-element.276) | copy-start | bytes 36868
  464.2 9.0 %copy-start.51 = (f32[768]{0:T(1024)S(1)}, f32[768]{0:T(1024)}, u32[]{:S(2)}) copy-start(f32[768]{0:T(1024)} %get-tuple-element.240) | copy-start | bytes 9220
  464.2 10.2 %copy-start.50 = (f32[768]{0:T(1024)S(1)}, f32[768]{0:T(1024)}, u32[]{:S(2)}) copy-start(f32[768]{0:T(1024)} %get-tuple-element.190) | copy-start | bytes 9220
  464.2 11.5 %copy-start.57 = (f32[768]{0:T(1024)S(1)}, f32[768]{0:T(1024)}, u32[]{:S(2)}) copy-start(f32[768]{0:T(1024)} %get-tuple-element.195) | copy-start | bytes 9220
  478.3 308.2 %copy-start.22 = (bf16[1024,768]{0,1:T(8,128)(2,1)S(1)}, bf16[1024,768]{0,1:T(8,128)(2,1)}, u32[]{:S(2)}) copy-start(bf16[1024,768]{0,1:T(8,128)(2,1)} %get-tuple-element.256) | copy-start | bytes 4718596
  784.6 10.3 %collective-permute-start = (f32[434,128]{1,0:T(8,128)}, f32[434,128]{1,0:T(8,128)}, u32[]{:S(2)}, u32[]{:S(2)}) collective-permute-start(f32[434,128]{1,0:T(8,128)} %slice.125), channel_id=1, source_target_pairs={{0,1},{1,2},{2,3},{3,4},{4,5},{5,6},{6,7},{7,8},{8,9},{9,10},{10,1... | collective-permute-start | bytes 666632
  788.1 8.5 %copy-start.35 = (f32[578,128]{1,0:T(8,128)S(1)}, f32[578,128]{1,0:T(8,128)}, u32[]{:S(2)}) copy-start(f32[578,128]{1,0:T(8,128)} %param.18) | copy-start | bytes 887812
  788.1 8.5 %copy-start.40 = (f32[578,128]{1,0:T(8,128)S(1)}, f32[578,128]{1,0:T(8,128)}, u32[]{:S(2)}) copy-start(f32[578,128]{1,0:T(8,128)} %param.19) | copy-start | bytes 887812
  791.7 5.8 copy-start.41
  791.7 10.4 %copy-start.24 = (f32[1154,128]{1,0:T(8,128)S(1)}, f32[1154,128]{1,0:T(8,128)}, u32[]{:S(2)}) copy-start(f32[1154,128]{1,0:T(8,128)} %param.21) | copy-start | bytes 1772548
  791.7 8.7 %collective-permute-start.1 = (f32[434,128]{1,0:T(8,128)S(1)}, f32[434,128]{1,0:T(8,128)}, u32[]{:S(2)}, u32[]{:S(2)}) collective-permute-start(f32[434,128]{1,0:T(8,128)S(1)} %slice.126), channel_id=1, source_target_pairs={{0,1},{1,2},{2,3},{3,4},{4,5},{5,6},{6,7},{7,8},{8,9},{9,10},{10,1... | collective-permute-start | bytes 666632
  797.5 7.8 copy-start.36
  797.5 6.8 copy-start.38
  (21 other events, 37.6 us)
Sparse Core Ops, SparseCore 0:
  11.5 64.5 all-gather.4
  79.6 80.8 all-gather.6
where the time goes:
time: 828 us; the launch traced here: 813 us
  blocking collectives  306 us (37%)
  local copies, waits for them, and re-layouts  210 us (25%)
  matrix products  168 us (20%)
  waiting for transfers between devices  63.1 us (8%)
  other arithmetic  44.2 us (5%)
  between operations  15.3 us (2%)
    unnamed x1, blocking collectives  306 us
    unnamed x158, local copies, waits for them, and re-layouts  79.1 us
    all_gather x1, waiting for transfers between devices, local(): lax.all_gather(att_master.astype(jnp.bfloat16), 'fsdp', axis=0, tiled=True)  61 us
    dot_general x1, matrix products, local(): jnp.dot(normed_low, weight_in, preferred_element_type=jnp.float32) + bias_in  37.3 us
    dot_general x1, matrix products, local(): jnp.einsum('td,fd->tf', grad_branch_two, back_out, preferred_element_type...  18.1 us
  transfers between devices with their start and end apart: 4, of which 2 were waited for; matrix products, arithmetic and copies ran while one was open for 12% of the time, Pallas kernels for 0%

commit v1 on v0

--- a/solution.py
+++ b/solution.py
@@ -1,8 +1,11 @@
+import functools
 import math
 
 import jax
 import jax.numpy as jnp
 from jax import lax
+from jax.experimental import pallas as pl
+from jax.experimental.pallas import tpu as pltpu
 from jax.sharding import PartitionSpec as P
 
 HEAD_DIM = 64
@@ -238,6 +241,846 @@
     )
 
 
+BF = jnp.bfloat16
+F32 = jnp.float32
+LANES = 128
+SLOT = 96
+TILE = 256
+EXTRA = 16
+MIB = 1 << 20
+
+
+def params(limit):
+    return pltpu.CompilerParams(vmem_limit_bytes=limit * MIB)
+
+
+def spec_any():
+    return pl.BlockSpec(memory_space=pl.ANY)
+
+
+def spec_vmem():
+    return pl.BlockSpec(memory_space=pltpu.VMEM)
+
+
+def spec_whole(shape):
+    return pl.BlockSpec(shape, lambda *ids: (0,) * len(shape))
+
+
+def dot_nn(left, right):
+    return lax.dot_general(left, right, (((1,), (0,)), ((), ())), preferred_element_type=F32)
+
+
+def dot_nt(left, right):
+    return lax.dot_general(left, right, (((1,), (1,)), ((), ())), preferred_element_type=F32)
+
+
+def dot_tn(left, right):
+    return lax.dot_general(left, right, (((0,), (0,)), ((), ())), preferred_element_type=F32)
+
+
+def slot_of(chunk, me):
+    diff = lax.bitwise_xor(me, chunk)
+    far_core = lax.bitwise_and(diff, 1)
+    x_bit = lax.bitwise_and(lax.shift_right_logical(diff, 1), 1)
+    y_bit = lax.bitwise_and(lax.shift_right_logical(diff, 2), 1)
+    z_low = lax.bitwise_and(lax.shift_right_logical(diff, 3), 1)
+    z_high = lax.shift_right_logical(diff, 4)
+    core = lax.bitwise_xor(lax.bitwise_and(me, 1), far_core)
+    third = x_bit + core * (y_bit - x_bit)
+    fourth = y_bit + core * (x_bit - y_bit)
+    return far_core, z_high + 2 * z_low + 4 * third + 8 * fourth
+
+
+def stage_perm(stage):
+    if stage == 0:
+        return [(i, i ^ 16) for i in range(32)]
+    if stage == 1:
+        return [(i, i ^ 8) for i in range(32)]
+    if stage == 2:
+        return [(i, i ^ (4 if i & 1 else 2)) for i in range(32)]
+    if stage == 3:
+        return [(i, i ^ (2 if i & 1 else 4)) for i in range(32)]
+    return [(i, i ^ 1) for i in range(32)]
+
+
+def exchange(array, stage):
+    return lax.ppermute(array, "fsdp", stage_perm(stage))
+
+
+def gather_chunks(chunk, small=None):
+    held = chunk
+    for stage in range(4):
+        rows = held.shape[0]
+        sent = held if small is None else jnp.concatenate([held, small])
+        got = exchange(sent, stage)
+        held = jnp.concatenate([held, got[:rows]])
+        if small is not None:
+            small = small + got[rows:]
+    if small is not None:
+        held = jnp.concatenate([held, small])
+    return held, exchange(held, 4)
+
+
+def scatter_chunks(sent, kept, small=None):
+    rows = 16 * SLOT
+    got = exchange(sent, 4)
+    for stage in (3, 2, 1, 0):
+        half = rows // 2
+        total_high = kept[half:].astype(F32) + got[half:rows].astype(F32)
+        kept = kept[:half].astype(F32) + got[:half].astype(F32)
+        high = total_high.astype(BF)
+        if small is not None:
+            small = small + got[rows:].astype(F32)
+            high = jnp.concatenate([high, small.astype(BF)])
+        if stage > 0:
+            kept = kept.astype(BF)
+        got = exchange(high, stage)
+        rows = half
+    total = kept.astype(F32) + got[:rows].astype(F32)
+    if small is not None:
+        return total, small + got[rows:].astype(F32)
+    return total
+
+
+def prep_kernel(last, att_mats, ffn_mats, att_ref, ffn_ref, tail_ref, att_out, small_out, ffn_a, ffn_b, att_buf, ffn_buf):
+    me = lax.axis_index("fsdp")
+    att_rows = att_ref.shape[0]
+    ffn_rows = ffn_ref.shape[0]
+    att_buf[0:64, :] = tail_ref[0:64, :]
+    att_buf[64 : 64 + att_rows, :] = att_ref[...]
+    ffn_buf[0:64, :] = tail_ref[64:128, :]
+    ffn_buf[64 : 64 + ffn_rows, :] = ffn_ref[...]
+    start = 64 - 2 * me
+    for part in range(6):
+        cols = slice(part * LANES, (part + 1) * LANES)
+        att_out[:, cols] = att_buf[pl.ds(start + part, SLOT, stride=6), :].astype(BF)
+    first = me < 16
+
+    @pl.when(first)
+    def _():
+        for block in range(4):
+            out = ffn_a if block < 2 else ffn_b
+            rows = slice((block % 2) * 48, (block % 2) * 48 + 48)
+            for part in range(6):
+                cols = slice(part * LANES, (part + 1) * LANES)
+                piece = ffn_buf[pl.ds(start + 6 * block + part, 48, stride=24), :]
+                out[rows, cols] = piece.astype(BF)
+
+    @pl.when(jnp.logical_not(first))
+    def _():
+        for part in range(6):
+            cols = slice(part * LANES, (part + 1) * LANES)
+            ffn_a[:, cols] = ffn_buf[pl.ds(start + part, SLOT, stride=6), :].astype(BF)
+            ffn_b[:, cols] = ffn_buf[pl.ds(start + 6 * SLOT + part, SLOT, stride=6), :].astype(BF)
+
+    small_out[...] = jnp.zeros_like(small_out)
+
+    @pl.when(me == last)
+    def _():
+        att_at = 64 + att_mats - last * att_rows
+        ffn_at = 64 + ffn_mats - last * ffn_rows
+        for part in range(6):
+            cols = slice(part * LANES, (part + 1) * LANES)
+            upper = att_buf[pl.ds(att_at + part, 6, stride=6), :]
+            lower = ffn_buf[pl.ds(ffn_at + part, 7, stride=6), :]
+            both = jnp.concatenate([upper, lower, jnp.zeros((3, LANES), F32)])
+            small_out[:, cols] = both.astype(BF)
+
+
+def prepare(att_master, ffn_master, tails, devices, width):
+    att_mats = 4 * width * width // LANES
+    ffn_mats = 2 * width * FF // LANES
+    att_rows, ffn_rows = att_master.shape[0], ffn_master.shape[0]
+    body = functools.partial(prep_kernel, devices - 1, att_mats, ffn_mats)
+    return pl.pallas_call(
+        body,
+        out_shape=(
+            jax.ShapeDtypeStruct((SLOT, width), BF),
+            jax.ShapeDtypeStruct((EXTRA, width), BF),
+            jax.ShapeDtypeStruct((SLOT, width), BF),
+            jax.ShapeDtypeStruct((SLOT, width), BF),
+        ),
+        in_specs=[spec_vmem()] * 3,
+        out_specs=(spec_vmem(),) * 4,
+        scratch_shapes=[
+            pltpu.VMEM((64 + att_rows + 6, LANES), F32),
+            pltpu.VMEM((64 + ffn_rows + 6, LANES), F32),
+        ],
+        compiler_params=params(16),
+        name="prep",
+    )(att_master, ffn_master, tails)
+
+
+def start_copy(lo, hi, far_core, src_rows, dst, sem):
+    @pl.when(far_core == 0)
+    def _():
+        pltpu.make_async_copy(lo.at[src_rows, :], dst, sem).start()
+
+    @pl.when(far_core == 1)
+    def _():
+        pltpu.make_async_copy(hi.at[src_rows, :], dst, sem).start()
+
+
+def load_att(lo, hi, dst, sem, first, last):
+    me = lax.axis_index("fsdp")
+
+    def body(chunk, carry):
+        far_core, slot = slot_of(chunk, me)
+        src = pl.ds(pl.multiple_of(slot * SLOT, 32), SLOT)
+        at = pl.multiple_of((chunk - first) * SLOT, 32)
+        start_copy(lo, hi, far_core, src, dst.at[pl.ds(at, SLOT), :], sem)
+        return carry
+
+    lax.fori_loop(first, last, body, 0)
+
+
+def load_ffn(units, w_in, w_out, sem_in, sem_out):
+    me = lax.axis_index("fsdp")
+
+    def body_in(chunk, carry):
+        far_core, slot = slot_of(chunk, me)
+        at = pl.multiple_of(chunk * 48, 16)
+        for unit in range(2):
+            lo, hi = units[unit]
+            for part in range(2):
+                src = pl.ds(pl.multiple_of(slot * SLOT + part * 48, 16), 48)
+                dst = w_in.at[2 * unit + part, pl.ds(at, 48), :]
+                start_copy(lo, hi, far_core, src, dst, sem_in)
+        return carry
+
+    def body_out(chunk, carry):
+        far_core, slot = slot_of(chunk, me)
+        for unit in range(2):
+            lo, hi = units[unit]
+            src = pl.ds(pl.multiple_of(slot * SLOT, 32), SLOT)
+            at = pl.multiple_of((chunk - 16) * 192 + unit * SLOT, 32)
+            start_copy(lo, hi, far_core, src, w_out.at[pl.ds(at, SLOT), :], sem_out)
+        return carry
+
+    lax.fori_loop(0, 16, body_in, 0)
+    lax.fori_loop(16, 32, body_out, 0)
+
+
+def wait_whole(ref, sem):
+    pltpu.make_async_copy(ref, ref, sem).wait()
+
+
+def head_mask(rows):
+    lane = lax.broadcasted_iota(jnp.int32, (rows, LANES), 1)
+    return lane < HEAD_DIM
+
+
+def forward_kernel(
+    x_ref,
+    masked_ref,
+    seg_col_ref,
+    seg_row_ref,
+    lo_ref,
+    hi_ref,
+    stream_ref,
+    q_ref,
+    k_ref,
+    v_ref,
+    ctx_ref,
+    lse_ref,
+    pre_ref,
+    small_ref,
+    weights,
+    small_lo,
+    small_hi,
+    sem,
+    small_sem,
+):
+    width = x_ref.shape[1]
+    seq = x_ref.shape[0]
+
+    @pl.when(pl.program_id(0) == 0)
+    def _():
+        load_att(lo_ref, hi_ref, weights, sem, 0, 32)
+        one = pltpu.make_async_copy(lo_ref.at[pl.ds(16 * SLOT, EXTRA), :], small_lo, small_sem.at[0])
+        two = pltpu.make_async_copy(hi_ref.at[pl.ds(16 * SLOT, EXTRA), :], small_hi, small_sem.at[1])
+        one.start()
+        two.start()
+        one.wait()
+        two.wait()
+        small_ref[...] = small_lo[...].astype(F32) + small_hi[...].astype(F32)
+        wait_whole(weights, sem)
+
+    small = small_ref[...]
+    stream = jnp.where(masked_ref[...] == 1, small[5:6], x_ref[...].astype(F32)).astype(BF)
+    stream_ref[...] = stream
+    q_ref[...] = ((dot_nn(stream, weights[0:width]) + small[0:1]) * 0.125).astype(BF)
+    k_ref[...] = dot_nn(stream, weights[width : 2 * width]).astype(BF)
+    v_ref[...] = (dot_nn(stream, weights[2 * width : 3 * width]) + small[1:2]).astype(BF)
+    left = head_mask(seq)
+    same = seg_col_ref[...] == seg_row_ref[0]
+
+    def pair(index, carry):
+        cols = pl.ds(pl.multiple_of(index * LANES, LANES), LANES)
+        queries = q_ref[:, cols]
+        keys = k_ref[:, cols]
+        values_t = v_ref[:, cols].T
+        outs = []
+        for head in range(2):
+            keep = left if head == 0 else jnp.logical_not(left)
+            own = jnp.where(keep, queries, jnp.zeros_like(queries))
+            scores = jnp.where(same, dot_nt(keys, own), MASKED_SCORE)
+            top = jnp.max(scores, axis=0, keepdims=True)
+            exponent = jnp.exp(scores - top)
+            total = jnp.sum(exponent, axis=0, keepdims=True)
+            probs = (exponent * (1.0 / total)).astype(BF)
+            lse_ref[0, pl.ds(2 * index + head, 1), :] = top + jnp.log(total)
+            outs.append(dot_nn(values_t[head * HEAD_DIM : (head + 1) * HEAD_DIM], probs))
+        ctx_ref[:, cols] = jnp.concatenate(outs).T.astype(BF)
+        return carry
+
+    lax.fori_loop(0, width // LANES, pair, 0)
+    out = dot_nn(ctx_ref[...], weights[3 * width :])
+    pre_ref[...] = stream_ref[...].astype(F32) + out + small[2:3]
+
+
+def attention_forward(block_input, masked_col, seg_col, seg_row, lo, hi):
+    tok, width = block_input.shape
+    seq_count, seq = seg_row.shape[0], seg_row.shape[2]
+    heads = width // HEAD_DIM
+    tile = lambda: pl.BlockSpec((seq, width), lambda s: (s, 0))
+    col = lambda: pl.BlockSpec((seq, 1), lambda s: (s, 0))
+    bf = jax.ShapeDtypeStruct((tok, width), BF)
+    return pl.pallas_call(
+        forward_kernel,
+        grid=(seq_count,),
+        out_shape=(
+            bf,
+            bf,
+            bf,
+            bf,
+            bf,
+            jax.ShapeDtypeStruct((seq_count, 16, seq), F32),
+            jax.ShapeDtypeStruct((tok, width), F32),
+            jax.ShapeDtypeStruct((EXTRA, width), F32),
+        ),
+        in_specs=[
+            tile(),
+            col(),
+            col(),
+            pl.BlockSpec((1, 1, seq), lambda s: (s, 0, 0)),
+            spec_any(),
+            spec_any(),
+        ],
+        out_specs=(
+            tile(),
+            tile(),
+            tile(),
+            tile(),
+            tile(),
+            pl.BlockSpec((1, 16, seq), lambda s: (s, 0, 0)),
+            tile(),
+            spec_whole((EXTRA, width)),
+        ),
+        scratch_shapes=[
+            pltpu.VMEM((4 * width, width), BF),
+            pltpu.VMEM((EXTRA, width), BF),
+            pltpu.VMEM((EXTRA, width), BF),
+            pltpu.SemaphoreType.DMA,
+            pltpu.SemaphoreType.DMA((2,)),
+        ],
+        compiler_params=params(40),
+        cost_estimate=pl.CostEstimate(
+            flops=2 * tok * width * width * 4 + 4 * tok * seq * width,
+            bytes_accessed=40 * MIB,
+            transcendentals=tok * seq * heads,
+        ),
+        name="attention_forward",
+    )(block_input, masked_col, seg_col, seg_row, lo, hi)
+
+
+def norm_stats(pre_norm):
+    center = pre_norm - jnp.mean(pre_norm, axis=-1, keepdims=True)
+    scale = lax.rsqrt(jnp.mean(center * center, axis=-1, keepdims=True) + EPSILON)
+    return center * scale, scale
+
+
+def norm_back(grad, gain, normed, scale):
+    scaled = grad * gain
+    mean_one = jnp.mean(scaled, axis=-1, keepdims=True)
+    mean_two = jnp.mean(scaled * normed, axis=-1, keepdims=True)
+    return scale * (scaled - mean_one - normed * mean_two)
+
+
+def column_sum(array):
+    return jnp.sum(array, axis=0, keepdims=True)
+
+
+def gelu_pair(inputs):
+    phi_cdf = 0.5 + 0.5 * lax.erf(inputs * math.sqrt(0.5))
+    density = jnp.exp(inputs * inputs * -0.5) * (1.0 / math.sqrt(2.0 * math.pi))
+    return inputs * phi_cdf, phi_cdf + inputs * density
+
+
+def ffn_kernel(
+    pre_ref,
+    grad_ref,
+    small_ref,
+    att_lo,
+    att_hi,
+    lo_a,
+    hi_a,
+    lo_b,
+    hi_b,
+    y_ref,
+    x1_ref,
+    hid_ref,
+    dhid_ref,
+    dfb_ref,
+    dpre_ref,
+    dob_ref,
+    dctx_ref,
+    sums_ref,
+    w_in,
+    w_out,
+    w_o,
+    slope,
+    sem_in,
+    sem_out,
+    sem_o,
+):
+    width = pre_ref.shape[1]
+    blocks = FF // width
+    step = pl.program_id(0)
+
+    @pl.when(step == 0)
+    def _():
+        load_ffn(((lo_a, hi_a), (lo_b, hi_b)), w_in, w_out, sem_in, sem_out)
+        load_att(att_lo, att_hi, w_o, sem_o, 24, 32)
+        sums_ref[...] = jnp.zeros_like(sums_ref)
+
+    small = small_ref[...]
+    normed_one, scale_one = norm_stats(pre_ref[...])
+    x_one = normed_one * small[3:4] + small[4:5]
+    x_low = x_one.astype(BF)
+    x1_ref[...] = x_low
+
+    @pl.when(step == 0)
+    def _():
+        wait_whole(w_in, sem_in)
+        wait_whole(w_out, sem_out)
+        wait_whole(w_o, sem_o)
+
+    total = x_one + small[10:11]
+    for block in range(blocks):
+        cols = slice(block * width, (block + 1) * width)
+        hidden, gate = gelu_pair(dot_nn(x_low, w_in[block]) + small[6 + block : 7 + block])
+        hidden = hidden.astype(BF)
+        hid_ref[:, cols] = hidden
+        slope[block] = gate
+        total = total + dot_nn(hidden, w_out[cols, :])
+    normed_two, scale_two = norm_stats(total)
+    y_ref[...] = (normed_two * small[11:12] + small[12:13]).astype(BF)
+    grad_out = grad_ref[...].astype(F32)
+    grad_two = norm_back(grad_out, small[11:12], normed_two, scale_two)
+    grad_low = grad_two.astype(BF)
+    dfb_ref[...] = grad_low
+    sums_ref[10:11] += column_sum(grad_low.astype(F32))
+    sums_ref[11:12] += column_sum(grad_out * normed_two)
+    sums_ref[12:13] += column_sum(grad_out)
+    grad_one = grad_two
+    for block in range(blocks):
+        cols = slice(block * width, (block + 1) * width)
+        dhid = (dot_nt(grad_low, w_out[cols, :]) * slope[block]).astype(BF)
+        dhid_ref[:, cols] = dhid
+        sums_ref[6 + block : 7 + block] += column_sum(dhid.astype(F32))
+        grad_one = grad_one + dot_nt(dhid, w_in[block])
+    sums_ref[3:4] += column_sum(grad_one * normed_one)
+    sums_ref[4:5] += column_sum(grad_one)
+    grad_pre = norm_back(grad_one, small[3:4], normed_one, scale_one)
+    dpre_ref[...] = grad_pre
+    dob = grad_pre.astype(BF)
+    dob_ref[...] = dob
+    sums_ref[2:3] += column_sum(dob.astype(F32))
+    dctx_ref[...] = dot_nt(dob, w_o[...]).astype(BF)
+
+
+def feed_forward(pre_one, out_grad, small, att, unit_a, unit_b):
+    tok, width = pre_one.shape
+    tile = lambda cols: pl.BlockSpec((TILE, cols), lambda i: (i, 0))
+    bf = lambda cols: jax.ShapeDtypeStruct((tok, cols), BF)
+    return pl.pallas_call(
+        ffn_kernel,
+        grid=(tok // TILE,),
+        out_shape=(
+            bf(width),
+            bf(width),
+            bf(FF),
+            bf(FF),
+            bf(width),
+            jax.ShapeDtypeStruct((tok, width), F32),
+            bf(width),
+            bf(width),
+            jax.ShapeDtypeStruct((EXTRA, width), F32),
+        ),
+        in_specs=[tile(width), tile(width), spec_whole((EXTRA, width))] + [spec_any()] * 6,
+        out_specs=(
+            tile(width),
+            tile(width),
+            tile(FF),
+            tile(FF),
+            tile(width),
+            tile(width),
+            tile(width),
+            tile(width),
+            spec_whole((EXTRA, width)),
+        ),
+        scratch_shapes=[
+            pltpu.VMEM((FF // width, width, width), BF),
+            pltpu.VMEM((FF, width), BF),
+            pltpu.VMEM((width, width), BF),
+            pltpu.VMEM((FF // width, TILE, width), F32),
+            pltpu.SemaphoreType.DMA,
+            pltpu.SemaphoreType.DMA,
+            pltpu.SemaphoreType.DMA,
+        ],
+        compiler_params=params(48),
+        cost_estimate=pl.CostEstimate(
+            flops=8 * tok * width * FF, bytes_accessed=40 * MIB, transcendentals=2 * tok * FF
+        ),
+        name="feed_forward",
+    )(pre_one, out_grad, small, *att, *unit_a, *unit_b)
+
+
+def put_slot(sent, kept, far_core, row, value):
+    rows = value.shape[0]
+    at = pl.ds(pl.multiple_of(row, 16), rows)
+
+    @pl.when(far_core == 1)
+    def _():
+        sent[at, :] = value
+
+    @pl.when(far_core == 0)
+    def _():
+        kept[at, :] = value
+
+
+def ffn_grad_kernel(x_ref, hid_ref, dhid_ref, dfb_ref, sent_a, kept_a, sent_b, kept_b):
+    width = x_ref.shape[1]
+    me = lax.axis_index("fsdp")
+    step = pl.program_id(0)
+    units = ((sent_a, kept_a), (sent_b, kept_b))
+
+    @pl.when(step < 4)
+    def _():
+        product = dot_tn(hid_ref[...], dfb_ref[...]).astype(BF)
+        for piece in range(8):
+            chunk = 16 + 4 * step + piece // 2
+            far_core, slot = slot_of(chunk, me)
+            sent, kept = units[piece % 2]
+            put_slot(sent, kept, far_core, slot * SLOT, product[piece * SLOT : (piece + 1) * SLOT])
+
+    for block in range(4):
+
+        @pl.when(step == 4 + block)
+        def _():
+            product = dot_tn(x_ref[...], dhid_ref[...]).astype(BF)
+            sent, kept = units[block // 2]
+            for chunk in range(16):
+                far_core, slot = slot_of(chunk, me)
+                row = slot * SLOT + (block % 2) * 48
+                put_slot(sent, kept, far_core, row, product[chunk * 48 : (chunk + 1) * 48])
+
+
+def ffn_grads(x_low, hidden, dhid, dfb):
+    tok, width = x_low.shape
+    out = jax.ShapeDtypeStruct((16 * SLOT, width), BF)
+    return pl.pallas_call(
+        ffn_grad_kernel,
+        grid=(8,),
+        out_shape=(out,) * 4,
+        in_specs=[
+            spec_whole((tok, width)),
+            pl.BlockSpec((tok, width), lambda i: (0, jnp.minimum(i, 3))),
+            pl.BlockSpec((tok, width), lambda i: (0, jnp.maximum(i - 4, 0))),
+            spec_whole((tok, width)),
+        ],
+        out_specs=(spec_whole((16 * SLOT, width)),) * 4,
+        compiler_params=params(48),
+        cost_estimate=pl.CostEstimate(
+            flops=4 * tok * width * FF, bytes_accessed=30 * MIB, transcendentals=0
+        ),
+        name="ffn_grads",
+    )(x_low, hidden, dhid, dfb)
+
+
+def backward_kernel(q_ref, k_ref, v_ref, dctx_ref, lse_ref, seg_col_ref, seg_row_ref, dq_ref, dk_ref, dv_ref):
+    seq, width = q_ref.shape
+    left = head_mask(seq)
+    same = seg_col_ref[...] == seg_row_ref[0]
+
+    def pair(index, carry):
+        cols = pl.ds(pl.multiple_of(index * LANES, LANES), LANES)
+        queries = q_ref[:, cols]
+        keys = k_ref[:, cols]
+        values = v_ref[:, cols]
+        grads = dctx_ref[:, cols]
+        keys_t = keys.T
+        grad_q = []
+        grad_k = jnp.zeros((seq, LANES), F32)
+        grad_v = jnp.zeros((seq, LANES), F32)
+        for head in range(2):
+            keep = left if head == 0 else jnp.logical_not(left)
+            own = jnp.where(keep, queries, jnp.zeros_like(queries))
+            own_grad = jnp.where(keep, grads, jnp.zeros_like(grads))
+            log_total = lse_ref[0, pl.ds(2 * index + head, 1), :]
+            scores = jnp.where(same, dot_nt(keys, own), MASKED_SCORE)
+            probs = jnp.exp(scores - log_total)
+            grad_probs = dot_nt(values, own_grad)
+            inner = jnp.sum(grad_probs * probs, axis=0, keepdims=True)
+            grad_scores = (probs * (grad_probs - inner)).astype(BF)
+            grad_v = grad_v + dot_nn(probs.astype(BF), own_grad)
+            grad_k = grad_k + dot_nn(grad_scores, own)
+            grad_q.append(dot_nn(keys_t[head * HEAD_DIM : (head + 1) * HEAD_DIM], grad_scores))
+        dq_ref[:, cols] = (jnp.concatenate(grad_q).T.astype(BF) * 0.125).astype(BF)
+        dk_ref[:, cols] = grad_k.astype(BF)
+        dv_ref[:, cols] = grad_v.astype(BF)
+        return carry
+
+    lax.fori_loop(0, width // LANES, pair, 0)
+
+
+def attention_backward(q, k, v, dctx, lse, seg_col, seg_row):
+    tok, width = q.shape
+    seq_count, seq = seg_row.shape[0], seg_row.shape[2]
+    heads = width // HEAD_DIM
+    tile = lambda: pl.BlockSpec((seq, width), lambda s: (s, 0))
+    return pl.pallas_call(
+        backward_kernel,
+        grid=(seq_count,),
+        out_shape=(jax.ShapeDtypeStruct((tok, width), BF),) * 3,
+        in_specs=[
+            tile(),
+            tile(),
+            tile(),
+            tile(),
+            pl.BlockSpec((1, 16, seq), lambda s: (s, 0, 0)),
+            pl.BlockSpec((seq, 1), lambda s: (s, 0)),
+            pl.BlockSpec((1, 1, seq), lambda s: (s, 0, 0)),
+        ],
+        out_specs=(tile(), tile(), tile()),
+        compiler_params=params(40),
+        cost_estimate=pl.CostEstimate(
+            flops=10 * tok * seq * width,
+            bytes_accessed=12 * MIB,
+            transcendentals=tok * seq * heads,
+        ),
+        name="attention_backward",
+    )(q, k, v, dctx, lse, seg_col, seg_row)
+
+
+def att_grad_kernel(
+    stream_ref,
+    dq_ref,
+    dk_ref,
+    dv_ref,
+    ctx_ref,
+    dob_ref,
+    dpre_ref,
+    masked_ref,
+    sums_ref,
+    lo_ref,
+    hi_ref,
+    sent_ref,
+    kept_ref,
+    small_ref,
+    dx_ref,
+    weights,
+    sem,
+):
+    tok, width = stream_ref.shape
+    me = lax.axis_index("fsdp")
+    load_att(lo_ref, hi_ref, weights, sem, 0, 24)
+    for matrix in range(4):
+        source = (dq_ref, dk_ref, dv_ref, dob_ref)[matrix]
+        inputs = ctx_ref if matrix == 3 else stream_ref
+        product = dot_tn(inputs[...], source[...]).astype(BF)
+        for piece in range(8):
+            far_core, slot = slot_of(8 * matrix + piece, me)
+            put_slot(
+                sent_ref, kept_ref, far_core, slot * SLOT, product[piece * SLOT : (piece + 1) * SLOT]
+            )
+    wait_whole(weights, sem)
+    small_ref[...] = sums_ref[...]
+
+    def tile(index, carry):
+        rows = pl.ds(pl.multiple_of(index * TILE, TILE), TILE)
+        dq = dq_ref[rows, :]
+        dv = dv_ref[rows, :]
+        grad = dpre_ref[rows, :] + dot_nt(dq, weights[0:width])
+        grad = grad + dot_nt(dk_ref[rows, :], weights[width : 2 * width])
+        grad = grad + dot_nt(dv, weights[2 * width : 3 * width])
+        chosen = masked_ref[rows, :] == 1
+        dx_ref[rows, :] = jnp.where(chosen, 0.0, grad)
+        small_ref[0:1] += column_sum(dq.astype(F32))
+        small_ref[1:2] += column_sum(dv.astype(F32))
+        small_ref[5:6] += column_sum(jnp.where(chosen, grad, 0.0))
+        return carry
+
+    lax.fori_loop(0, tok // TILE, tile, 0)
+    sent_ref[pl.ds(16 * SLOT, EXTRA), :] = small_ref[...].astype(BF)
+
+
+def att_grads(stream, dq, dk, dv, ctx, dob, dpre, masked_col, sums, lo, hi):
+    tok, width = stream.shape
+    return pl.pallas_call(
+        att_grad_kernel,
+        out_shape=(
+            jax.ShapeDtypeStruct((16 * SLOT + EXTRA, width), BF),
+            jax.ShapeDtypeStruct((16 * SLOT, width), BF),
+            jax.ShapeDtypeStruct((EXTRA, width), F32),
+            jax.ShapeDtypeStruct((tok, width), F32),
+        ),
+        in_specs=[spec_vmem()] * 9 + [spec_any()] * 2,
+        out_specs=(spec_vmem(),) * 4,
+        scratch_shapes=[pltpu.VMEM((3 * width, width), BF), pltpu.SemaphoreType.DMA],
+        compiler_params=params(48),
+        cost_estimate=pl.CostEstimate(
+            flops=14 * tok * width * width, bytes_accessed=30 * MIB, transcendentals=0
+        ),
+        name="att_grads",
+    )(stream, dq, dk, dv, ctx, dob, dpre, masked_col, sums, lo, hi)
+
+
+def flat_att_kernel(grad_ref, out_ref):
+    for part in range(6):
+        out_ref[pl.ds(part, SLOT, stride=6), :] = grad_ref[:, part * LANES : (part + 1) * LANES]
+
+
+def flat_ffn_kernel(a_ref, b_ref, out_ref):
+    first = lax.axis_index("fsdp") < 16
+
+    @pl.when(first)
+    def _():
+        for block in range(4):
+            source = a_ref if block < 2 else b_ref
+            rows = slice((block % 2) * 48, (block % 2) * 48 + 48)
+            for part in range(6):
+                cols = slice(part * LANES, (part + 1) * LANES)
+                out_ref[pl.ds(6 * block + part, 48, stride=24), :] = source[rows, cols]
+
+    @pl.when(jnp.logical_not(first))
+    def _():
+        for part in range(6):
+            cols = slice(part * LANES, (part + 1) * LANES)
+            out_ref[pl.ds(part, SLOT, stride=6), :] = a_ref[:, cols]
+            out_ref[pl.ds(6 * SLOT + part, SLOT, stride=6), :] = b_ref[:, cols]
+
+
+def flatten(kernel, rows, *pieces):
+    return pl.pallas_call(
+        kernel,
+        out_shape=jax.ShapeDtypeStruct((rows, LANES), F32),
+        in_specs=[spec_vmem()] * len(pieces),
+        out_specs=spec_vmem(),
+        compiler_params=params(16),
+        name="flatten",
+    )(*pieces)
+
+
+def update_kernel(last, small_at, rate, flat_ref, head_ref, small_ref, w_ref, m_ref, a_ref, w_out, m_out, a_out, low_out, buf):
+    me = lax.axis_index("fsdp")
+    aligned = flat_ref.shape[0]
+    own = w_ref.shape[0]
+    count = small_at[1]
+    buf[0:aligned, :] = flat_ref[...]
+    buf[aligned : aligned + 64, :] = head_ref[...]
+
+    @pl.when(me == last)
+    def _():
+        buf[aligned : aligned + 64, :] = jnp.zeros((64, LANES), F32)
+        for part in range(6):
+            cols = slice(part * LANES, (part + 1) * LANES)
+            buf[pl.ds(aligned + part, count, stride=6), :] = small_ref[
+                small_at[0] : small_at[0] + count, cols
+            ]
+
+    grad = buf[pl.ds(2 * me, own), :]
+    moment = 0.5 * m_ref[...] + grad
+    master = w_ref[...] - rate * (grad + 0.5 * moment)
+    m_out[...] = moment
+    w_out[...] = master
+    a_out[...] = 0.5 * a_ref[...] + 0.5 * master
+    low_out[...] = master.astype(BF)
+
+
+def update(flat, head, small, small_at, rate, devices, master, moment, average):
+    own = master.shape[0]
+    f32 = jax.ShapeDtypeStruct((own, LANES), F32)
+    body = functools.partial(update_kernel, devices - 1, small_at, rate)
+    return pl.pallas_call(
+        body,
+        out_shape=(f32, f32, f32, jax.ShapeDtypeStruct((own, LANES), BF)),
+        in_specs=[spec_vmem()] * 6,
+        out_specs=(spec_vmem(),) * 4,
+        scratch_shapes=[pltpu.VMEM((flat.shape[0] + 64, LANES), F32)],
+        compiler_params=params(16),
+        name="update",
+    )(flat, head, small, master, moment, average)
+
+
+def local_exchange(
+    block_input,
+    seg_ids,
+    masked,
+    out_grad,
+    att_master,
+    att_moment,
+    att_average,
+    ffn_master,
+    ffn_moment,
+    ffn_average,
+):
+    tok, width = block_input.shape
+    seq_count, seq = seg_ids.shape
+    devices = lax.axis_size("fsdp")
+    up = [(i, i + 1) for i in range(devices - 1)]
+    down = [(i + 1, i) for i in range(devices - 1)]
+    tails = lax.ppermute(jnp.concatenate([att_master[-64:], ffn_master[-64:]]), "fsdp", up)
+    masked_col = masked.reshape(tok, 1)
+    seg_col = seg_ids.reshape(tok, 1)
+    seg_row = seg_ids.reshape(seq_count, 1, seq)
+    att_chunk, small_chunk, chunk_a, chunk_b = prepare(att_master, ffn_master, tails, devices, width)
+    att = gather_chunks(att_chunk, small_chunk)
+    unit_a = gather_chunks(chunk_a)
+    unit_b = gather_chunks(chunk_b)
+    stream, q, k, v, ctx, lse, pre_one, small = attention_forward(
+        block_input, masked_col, seg_col, seg_row, *att
+    )
+    block_output, x_low, hidden, dhid, dfb, dpre, dob, dctx, sums = feed_forward(
+        pre_one, out_grad, small, att, unit_a, unit_b
+    )
+    sent_a, kept_a, sent_b, kept_b = ffn_grads(x_low, hidden, dhid, dfb)
+    grad_a = scatter_chunks(sent_a, kept_a)
+    grad_b = scatter_chunks(sent_b, kept_b)
+    dq, dk, dv = attention_backward(q, k, v, dctx, lse, seg_col, seg_row)
+    sent, kept, small_grads, input_grad = att_grads(
+        stream, dq, dk, dv, ctx, dob, dpre, masked_col, sums, *att
+    )
+    grad_att, small_total = scatter_chunks(sent, kept, small_grads)
+    rate = 0.05 / math.sqrt(tok * devices)
+    ffn_flat = flatten(flat_ffn_kernel, 12 * SLOT, grad_a, grad_b)
+    ffn_head = lax.ppermute(ffn_flat[:64], "fsdp", down)
+    att_flat = flatten(flat_att_kernel, 6 * SLOT, grad_att)
+    att_head = lax.ppermute(att_flat[:64], "fsdp", down)
+    ffn_new = update(
+        ffn_flat, ffn_head, small_total, (6, 7), rate, devices, ffn_master, ffn_moment, ffn_average
+    )
+    att_new = update(
+        att_flat, att_head, small_total, (0, 6), rate, devices, att_master, att_moment, att_average
+    )
+    return (block_output, input_grad) + tuple(att_new) + tuple(ffn_new)
+
+
+def chunked(mesh):
+    return mesh.shape["fsdp"] == 32
+
+
 def solution(mesh):
     in_specs = (
         P("fsdp", None),
@@ -263,4 +1106,5 @@
         P("fsdp", None),
         P("fsdp", None),
     )
-    return jax.shard_map(local, mesh=mesh, in_specs=in_specs, out_specs=out_specs, check_vma=False)
+    body = local_exchange if chunked(mesh) else local
+    return jax.shard_map(body, mesh=mesh, in_specs=in_specs, out_specs=out_specs, check_vma=False)

time: 828 us -> 345 us (0.42); the launches traced: 813 us -> 345 us
  blocking collectives: 306 us -> 0 us
  local copies, waits for them, and re-layouts: 210 us -> 18.3 us
  matrix products: 168 us -> 0 us
  Pallas kernels: 0 us -> 132 us
  waiting for transfers between devices: 63.1 us -> 140 us
  starting transfers between devices: 5.12 us -> 46.1 us
  other arithmetic: 44.2 us -> 7.52 us
  between operations: 15.3 us -> 1.29 us
    unnamed x1 -> x0, blocking collectives: 306 us -> none
    dot_general x26 -> x0, matrix products: 168 us -> none  [the longest x1 37.3 us: local(): jnp.dot(normed_low, weight_in, preferred_element_type=jnp.float32) + bias_in]
    ppermute x0 -> x33, waiting for transfers between devices: none -> 140 us  [the longest x30 135 us: exchange(): return lax.ppermute(array, 'fsdp', stage_perm(stage))]
    pallas_call x0 -> x10, Pallas kernels: none -> 132 us  [the longest x1 36.4 us: feed_forward(): pl.pallas_call(ffn_kernel, grid=(tok // TILE,), out_shape=(bf(width), bf(...]
    unnamed x158 -> x62, local copies, waits for them, and re-layouts: 79.1 us -> 14.6 us
    all_gather x2 -> x0, waiting for transfers between devices: 61 us -> none  [the longest x1 61 us: local(): lax.all_gather(att_master.astype(jnp.bfloat16), 'fsdp', axis=0, tiled=True)]
    ppermute x0 -> x33, starting transfers between devices: none -> 46.1 us  [the longest x30 26.9 us: exchange(): return lax.ppermute(array, 'fsdp', stage_perm(stage))]
    reshape x6 -> x1, local copies, waits for them, and re-layouts: 40.2 us -> 0.01 us  [local_exchange(): seg_row = seg_ids.reshape(seq_count, 1, seq)]
  transfers between devices with their start and end apart: 4 -> 33, of which waited for: 2 -> 17; matrix products, arithmetic and copies ran while one was open for 12% -> 5% of each run, Pallas kernels for 0% -> 22%
where the time goes in v1:
time: 345 us
  waiting for transfers between devices  140 us (41%)
  Pallas kernels  132 us (38%)
  starting transfers between devices  46.1 us (13%)
  local copies, waits for them, and re-layouts  18.3 us (5%)
  other arithmetic  7.52 us (2%)
    ppermute x30, waiting for transfers between devices, exchange(): return lax.ppermute(array, 'fsdp', stage_perm(stage))  135 us
    pallas_call x1, Pallas kernels, feed_forward(): pl.pallas_call(ffn_kernel, grid=(tok // TILE,), out_shape=(bf(width), bf(...  36.4 us
    pallas_call x1, Pallas kernels, attention_forward(): pl.pallas_call(forward_kernel, grid=(seq_count,), out_shape=(bf, bf, bf,...  28.3 us
    ppermute x30, starting transfers between devices, exchange(): return lax.ppermute(array, 'fsdp', stage_perm(stage))  26.9 us
    pallas_call x1, Pallas kernels, attention_backward(): pl.pallas_call(backward_kernel, grid=(seq_count,), out_shape=(jax.ShapeDt...  25.4 us
    pallas_call x1, Pallas kernels, att_grads(): pl.pallas_call(att_grad_kernel, out_shape=(jax.ShapeDtypeStruct((16 * SLO...  19.8 us
    pallas_call x1, Pallas kernels, ffn_grads(): pl.pallas_call(ffn_grad_kernel, grid=(8,), out_shape=(out,) * 4, in_specs...  18.8 us
    unnamed x62, local copies, waits for them, and re-layouts  14.6 us
  transfers between devices with their start and end apart: 33, of which 17 were waited for; matrix products, arithmetic and copies ran while one was open for 5% of the time, Pallas kernels for 22%

profile of v1, /device:TPU:7, one launch (start us, length us, event | category | flops | bytes accessed | tf_op | source)
XLA Modules:
  0.0 344.5 jit_solution(12563276493257323016)
XLA Ops:
  0.6 0.8 slice.198
  1.4 0.8 slice.199
  2.2 3.7 %collective-permute-start = (f32[128,128]{1,0:T(8,128)S(1)}, f32[128,128]{1,0:T(8,128)S(1)}, u32[]{:S(2)}, u32[]{:S(2)}) collective-permute-start(f32[128,128]{1,0:T(8,128)S(1)} %pad_maximum_fusion.13), channel_id=1, source_target_pairs={{0,1},{1,2},{2,3},{3,4},{4,5},{5,6},{6,7},{7,8},{8,9},{9,10},{10,1... | collective-permute-start | bytes 196616 | tf_op jit(solution)/shard_map/ppermute | solution.py:1044
  5.9 1.3 collective-permute-done.tail_ref
  7.2 1.1 copy-done
  8.3 1.0 copy-done.2
  9.5 2.3 collective-permute-start.1
  11.8 7.6 %collective-permute-done.1 = bf16[112,768]{1,0:T(8,128)(2,1)S(1)} collective-permute-done((bf16[112,768]{1,0:T(8,128)(2,1)S(1)}, bf16[112,768]{1,0:T(8,128)(2,1)S(1)}, u32[]{:S(2)}, u32[]{:S(2)}) %collective-permute-start.1) | collective-permute-done | bytes 172064 | tf_op jit(solution)/shard_map/ppermute | solution.py:307
  19.5 7.4 %collective-permute-done.2 = bf16[208,768]{1,0:T(8,128)(2,1)S(1)} collective-permute-done((bf16[208,768]{1,0:T(8,128)(2,1)S(1)}, bf16[208,768]{1,0:T(8,128)(2,1)S(1)}, u32[]{:S(2)}, u32[]{:S(2)}) %collective-permute-start.2) | collective-permute-done | bytes 319520 | tf_op jit(solution)/shard_map/ppermute | solution.py:307
  27.1 0.6 collective-permute-start.3
  27.7 4.2 %collective-permute-start.6 = (bf16[96,768]{1,0:T(8,128)(2,1)S(1)}, bf16[96,768]{1,0:T(8,128)(2,1)S(1)}, u32[]{:S(2)}, u32[]{:S(2)}) collective-permute-start(bf16[96,768]{1,0:T(8,128)(2,1)S(1)} %get-tuple-element.54), channel_id=1, source_target_pairs={{0,16},{1,17},{2,18},{3,19},{4,20},{5,21},{6,22},{7,23},{8,24},{9,... | collective-permute-start | bytes 442376 | tf_op jit(solution)/shard_map/ppermute | solution.py:307
  31.9 9.7 %collective-permute-done.6 = bf16[96,768]{1,0:T(8,128)(2,1)S(1)} collective-permute-done((bf16[96,768]{1,0:T(8,128)(2,1)S(1)}, bf16[96,768]{1,0:T(8,128)(2,1)S(1)}, u32[]{:S(2)}, u32[]{:S(2)}) %collective-permute-start.6) | collective-permute-done | bytes 147488 | tf_op jit(solution)/shard_map/ppermute | solution.py:307
  41.6 1.3 collective-permute-start.7
  42.9 1.8 collective-permute-done.11
  44.8 1.3 collective-permute-start.12
  46.3 10.6 %collective-permute-done.12 = bf16[192,768]{1,0:T(8,128)(2,1)S(1)} collective-permute-done((bf16[192,768]{1,0:T(8,128)(2,1)S(1)}, bf16[192,768]{1,0:T(8,128)(2,1)S(1)}, u32[]{:S(2)}, u32[]{:S(2)}) %collective-permute-start.12) | collective-permute-done | bytes 294944 | tf_op jit(solution)/shard_map/ppermute | solution.py:307
  57.1 1.5 collective-permute-start.8
  58.5 0.7 constant_dynamic-update-slice_fusion.12
  59.3 0.7 constant_dynamic-update-slice_fusion.11
  59.9 9.5 %collective-permute-done.13 = bf16[384,768]{1,0:T(8,128)(2,1)S(1)} collective-permute-done((bf16[384,768]{1,0:T(8,128)(2,1)S(1)}, bf16[384,768]{1,0:T(8,128)(2,1)S(1)}, u32[]{:S(2)}, u32[]{:S(2)}) %collective-permute-start.13) | collective-permute-done | bytes 589856 | tf_op jit(solution)/shard_map/ppermute | solution.py:307
  69.6 9.8 %collective-permute-done.8 = bf16[384,768]{1,0:T(8,128)(2,1)S(1)} collective-permute-done((bf16[384,768]{1,0:T(8,128)(2,1)S(1)}, bf16[384,768]{1,0:T(8,128)(2,1)S(1)}, u32[]{:S(2)}, u32[]{:S(2)}) %collective-permute-start.8) | collective-permute-done | bytes 589856 | tf_op jit(solution)/shard_map/ppermute | solution.py:307
  79.6 0.7 constant_dynamic-update-slice_fusion.16
  80.3 0.7 constant_dynamic-update-slice_fusion.10
  81.2 0.9 constant_dynamic-update-slice_fusion.15
  82.1 0.9 constant_dynamic-update-slice_fusion.9
  82.9 0.9 constant_dynamic-update-slice_fusion.14
  83.8 3.5 %collective-permute-done.14 = bf16[768,768]{1,0:T(8,128)(2,1)S(1)} collective-permute-done((bf16[768,768]{1,0:T(8,128)(2,1)S(1)}, bf16[768,768]{1,0:T(8,128)(2,1)S(1)}, u32[]{:S(2)}, u32[]{:S(2)}) %collective-permute-start.14) | collective-permute-done | bytes 1179680 | tf_op jit(solution)/shard_map/ppermute | solution.py:307
  87.3 1.1 constant_dynamic-update-slice_fusion.13.lo_b
  88.4 1.5 collective-permute-start.15
  89.9 10.0 %collective-permute-done.9 = bf16[768,768]{1,0:T(8,128)(2,1)S(1)} collective-permute-done((bf16[768,768]{1,0:T(8,128)(2,1)S(1)}, bf16[768,768]{1,0:T(8,128)(2,1)S(1)}, u32[]{:S(2)}, u32[]{:S(2)}) %collective-permute-start.9) | collective-permute-done | bytes 1179680 | tf_op jit(solution)/shard_map/ppermute | solution.py:307
  100.0 1.1 constant_dynamic-update-slice_fusion.8.lo_a
  101.1 1.5 collective-permute-start.10
  103.1 1.4 copy-done.9
  104.5 28.3 %attention_forward.1 = (bf16[1024,768]{1,0:T(8,128)(2,1)S(1)}, bf16[1024,768]{1,0:T(8,128)(2,1)S(1)}, bf16[1024,768]{1,0:T(8,128)(2,1)S(1)}, bf16[1024,768]{1,0:...) custom-call(bf16[1024,768]{1,0:T(8,128)(2,1)S(1)} %copy-done.9, ...), custom_call_target="tpu_custom_call" | custom-call | flops 6442450944 | bytes 41943040 | tf_op jit(solution)/shard_map/attention_forward/pallas_call | solution.py:549
  132.8 36.4 %feed_forward.1 = (bf16[1024,768]{1,0:T(8,128)(2,1)}, bf16[1024,768]{1,0:T(8,128)(2,1)S(1)}, bf16[1024,3072]{1,0:T(8,128)(2,1)}, bf16[1024,3072]{1,0:T(8,128)(2,...) custom-call(f32[1024,768]{1,0:T(8,128)} %get-tuple-element.52.pre_re, ...), custom_call_target="tpu_custom_call" | custom-call | flops 19327352832 | bytes 41943040 | tf_op jit(solution)/shard_map/feed_forward/pallas_call | solution.py:707
  169.3 1.2 copy-done.15
  170.5 1.1 copy-done.16
  171.7 1.4 copy-done.17
  173.1 18.8 %ffn_grads.1 = (bf16[1536,768]{1,0:T(8,128)(2,1)S(1)}, bf16[1536,768]{1,0:T(8,128)(2,1)}, bf16[1536,768]{1,0:T(8,128)(2,1)}, bf16[1536,768]{1,0:T(8,128)(2,1)}) custom-call(bf16[1024,768]{1,0:T(8,128)(2,1)S(1)} %copy-done.17, bf16[1024,3072]{1,0:T(8,128)(2,1)} %get-tuple-element.79.hid_ref, bf16[1024,3072]{1,0:T(8,128)(2,1)} %get-tuple-element.80.dhid_ref, ...), custom_call_target="tpu_custom_call" | custom-call | flops 9663676416 | bytes 31457280 | tf_op jit(solution)/shard_map/ffn_grads/pallas_call | solution.py:793
  192.1 0.3 collective-permute-start.27
  192.4 25.4 %attention_backward.1 = (bf16[1024,768]{1,0:T(8,128)(2,1)S(1)}, bf16[1024,768]{1,0:T(8,128)(2,1)S(1)}, bf16[1024,768]{1,0:T(8,128)(2,1)S(1)}) custom-call(bf16[1024,768]{1,0:T(8,128)(2,1)S(1)} %get-tuple-element.58.q_ref, bf16[1024,768]{1,0:T(8,128)(2,1)S(1)} %get-tuple-element.59.k_ref, bf16[1024,768]{1,0:T(8,128)(2,1)S(1)} %get-tuple-element.60.v_ref, ...), custom_call_target="tpu_custom_call" | custom-call | flops 4026531840 | bytes 12582912 | tf_op jit(solution)/shard_map/attention_backward/pallas_call | solution.py:853
  217.8 1.1 copy-done.11
  218.9 19.8 %att_grads.1 = (bf16[1552,768]{1,0:T(8,128)(2,1)}, bf16[1536,768]{1,0:T(8,128)(2,1)}, f32[16,768]{1,0:T(8,128)S(1)}, f32[1024,768]{1,0:T(8,128)}) custom-call(bf16[1024,768]{1,0:T(8,128)(2,1)S(1)} %copy-done.13, bf16[1024,768]{1,0:T(8,128)(2,1)S(1)} %get-tuple-element.63.dq_ref, bf16[1024,768]{1,0:T(8,128)(2,1)S(1)} %get-tuple-element.64.dk_ref, ...), custom_call_target="tpu_custom_call" | custom-call | flops 8455716864 | bytes 31457280 | tf_op jit(solution)/shard_map/att_grads/pallas_call | solution.py:931
  239.0 2.4 add_convert_fusion.3
  241.5 2.3 add_convert_fusion.1
  243.9 1.5 collective-permute-start.28
  245.4 0.6 add_convert_fusion.5
  246.1 10.7 %collective-permute-done.23 = bf16[768,768]{1,0:T(8,128)(2,1)S(1)} collective-permute-done((bf16[768,768]{1,0:T(8,128)(2,1)S(1)}, bf16[768,768]{1,0:T(8,128)(2,1)S(1)}, u32[]{:S(2)}, u32[]{:S(2)}) %collective-permute-start.23) | collective-permute-done | bytes 1179680 | tf_op jit(solution)/shard_map/ppermute | solution.py:307
  257.3 18.5 %collective-permute-done.28 = bf16[768,768]{1,0:T(8,128)(2,1)S(1)} collective-permute-done((bf16[768,768]{1,0:T(8,128)(2,1)S(1)}, bf16[768,768]{1,0:T(8,128)(2,1)S(1)}, u32[]{:S(2)}, u32[]{:S(2)}) %collective-permute-start.28) | collective-permute-done | bytes 1179680 | tf_op jit(solution)/shard_map/ppermute | solution.py:307
  276.2 18.8 %collective-permute-done.17 = bf16[784,768]{1,0:T(8,128)(2,1)S(1)} collective-permute-done((bf16[784,768]{1,0:T(8,128)(2,1)S(1)}, bf16[784,768]{1,0:T(8,128)(2,1)S(1)}, u32[]{:S(2)}, u32[]{:S(2)}) %collective-permute-start.17) | collective-permute-done | bytes 1204256 | tf_op jit(solution)/shard_map/ppermute | solution.py:307
  295.7 1.2 collective-permute-start.25
  297.1 0.4 collective-permute-start.30
  297.5 7.3 %collective-permute-done.18 = bf16[400,768]{1,0:T(8,128)(2,1)S(1)} collective-permute-done((bf16[400,768]{1,0:T(8,128)(2,1)S(1)}, bf16[400,768]{1,0:T(8,128)(2,1)S(1)}, u32[]{:S(2)}, u32[]{:S(2)}) %collective-permute-start.18) | collective-permute-done | bytes 614432 | tf_op jit(solution)/shard_map/ppermute | solution.py:307
  305.0 1.2 collective-permute-start.19
  306.2 2.1 collective-permute-start.26
  308.3 1.2 collective-permute-done.30
  309.5 3.2 collective-permute-start.31
  312.7 8.3 %collective-permute-done.19 = bf16[208,768]{1,0:T(8,128)(2,1)S(1)} collective-permute-done((bf16[208,768]{1,0:T(8,128)(2,1)S(1)}, bf16[208,768]{1,0:T(8,128)(2,1)S(1)}, u32[]{:S(2)}, u32[]{:S(2)}) %collective-permute-start.19) | collective-permute-done | bytes 319520 | tf_op jit(solution)/shard_map/ppermute | solution.py:307
  321.1 1.3 collective-permute-start.20
  322.7 13.4 %collective-permute-start.32 = (f32[64,128]{1,0:T(8,128)S(1)}, f32[64,128]{1,0:T(8,128)S(1)}, u32[]{:S(2)}, u32[]{:S(2)}) collective-permute-start(f32[64,128]{1,0:T(8,128)S(1)} %slice.321), channel_id=1, source_target_pairs={{1,0},{2,1},{3,2},{4,3},{5,4},{6,5},{7,6},{8,7},{9,8},{10,9},{11,1... | collective-permute-start | bytes 98312 | tf_op jit(solution)/shard_map/ppermute | solution.py:1068
  336.3 2.2 collective-permute-start.21
  338.5 1.5 update.3
  340.0 3.5 %collective-permute-done.21.head_ref = f32[64,128]{1,0:T(8,128)S(1)} collective-permute-done((f32[64,128]{1,0:T(8,128)S(1)}, f32[64,128]{1,0:T(8,128)S(1)}, u32[]{:S(2)}, u32[]{:S(2)}) %collective-permute-start.21) | collective-permute-done | bytes 32800 | tf_op jit(solution)/shard_map/ppermute | solution.py:1070
  343.5 1.0 update.2
  (119 shorter events, 5.0 us)
Async XLA Ops:
  2.2 5.0 %collective-permute-start = (f32[128,128]{1,0:T(8,128)S(1)}, f32[128,128]{1,0:T(8,128)S(1)}, u32[]{:S(2)}, u32[]{:S(2)}) collective-permute-start(f32[128,128]{1,0:T(8,128)S(1)} %pad_maximum_fusion.13), channel_id=1, source_target_pairs={{0,1},{1,2},{2,3},{3,4},{4,5},{5,6},{6,7},{7,8},{8,9},{9,10},{10,1... | collective-permute-start | bytes 196616 | tf_op jit(solution)/shard_map/ppermute | solution.py:1044
  7.2 1.1 copy-start
  8.3 1.0 copy-start.2
  9.5 9.9 %collective-permute-start.1 = (bf16[112,768]{1,0:T(8,128)(2,1)S(1)}, bf16[112,768]{1,0:T(8,128)(2,1)S(1)}, u32[]{:S(2)}, u32[]{:S(2)}) collective-permute-start(bf16[112,768]{1,0:T(8,128)(2,1)S(1)} %pad_maximum_fusion.11), channel_id=1, source_target_pairs={{0,16},{1,17},{2,18},{3,19},{4,20},{5,21},{6,22},{7,23},{8,24},{9,... | collective-permute-start | bytes 516104 | tf_op jit(solution)/shard_map/ppermute | solution.py:307
  19.4 7.5 %collective-permute-start.2 = (bf16[208,768]{1,0:T(8,128)(2,1)S(1)}, bf16[208,768]{1,0:T(8,128)(2,1)S(1)}, u32[]{:S(2)}, u32[]{:S(2)}) collective-permute-start(bf16[208,768]{1,0:T(8,128)(2,1)S(1)} %pad_maximum_fusion.7), channel_id=1, source_target_pairs={{0,8},{1,9},{2,10},{3,11},{4,12},{5,13},{6,14},{7,15},{8,0},{9,1},... | collective-permute-start | bytes 958472 | tf_op jit(solution)/shard_map/ppermute | solution.py:307
  27.1 19.0 %collective-permute-start.3 = (bf16[400,768]{1,0:T(8,128)(2,1)S(1)}, bf16[400,768]{1,0:T(8,128)(2,1)S(1)}, u32[]{:S(2)}, u32[]{:S(2)}) collective-permute-start(bf16[400,768]{1,0:T(8,128)(2,1)S(1)} %pad_maximum_fusion.3), channel_id=1, source_target_pairs={{0,2},{1,5},{2,0},{3,7},{4,6},{5,1},{6,4},{7,3},{8,10},{9,13},{10,... | collective-permute-start | bytes 1843208 | tf_op jit(solution)/shard_map/ppermute | solution.py:307
  27.7 13.9 %collective-permute-start.6 = (bf16[96,768]{1,0:T(8,128)(2,1)S(1)}, bf16[96,768]{1,0:T(8,128)(2,1)S(1)}, u32[]{:S(2)}, u32[]{:S(2)}) collective-permute-start(bf16[96,768]{1,0:T(8,128)(2,1)S(1)} %get-tuple-element.54), channel_id=1, source_target_pairs={{0,16},{1,17},{2,18},{3,19},{4,20},{5,21},{6,22},{7,23},{8,24},{9,... | collective-permute-start | bytes 442376 | tf_op jit(solution)/shard_map/ppermute | solution.py:307
  31.9 12.9 %collective-permute-start.11 = (bf16[96,768]{1,0:T(8,128)(2,1)S(1)}, bf16[96,768]{1,0:T(8,128)(2,1)S(1)}, u32[]{:S(2)}, u32[]{:S(2)}) collective-permute-start(bf16[96,768]{1,0:T(8,128)(2,1)S(1)} %get-tuple-element.55), channel_id=1, source_target_pairs={{0,16},{1,17},{2,18},{3,19},{4,20},{5,21},{6,22},{7,23},{8,24},{9,... | collective-permute-start | bytes 442376 | tf_op jit(solution)/shard_map/ppermute | solution.py:307
  41.6 15.4 %collective-permute-start.7 = (bf16[192,768]{1,0:T(8,128)(2,1)S(1)}, bf16[192,768]{1,0:T(8,128)(2,1)S(1)}, u32[]{:S(2)}, u32[]{:S(2)}) collective-permute-start(bf16[192,768]{1,0:T(8,128)(2,1)S(1)} %pad_maximum_fusion.9), channel_id=1, source_target_pairs={{0,8},{1,9},{2,10},{3,11},{4,12},{5,13},{6,14},{7,15},{8,0},{9,1},... | collective-permute-start | bytes 884744 | tf_op jit(solution)/shard_map/ppermute | solution.py:307
  44.8 12.1 %collective-permute-start.12 = (bf16[192,768]{1,0:T(8,128)(2,1)S(1)}, bf16[192,768]{1,0:T(8,128)(2,1)S(1)}, u32[]{:S(2)}, u32[]{:S(2)}) collective-permute-start(bf16[192,768]{1,0:T(8,128)(2,1)S(1)} %pad_maximum_fusion.10), channel_id=1, source_target_pairs={{0,8},{1,9},{2,10},{3,11},{4,12},{5,13},{6,14},{7,15},{8,0},{9,1},... | collective-permute-start | bytes 884744 | tf_op jit(solution)/shard_map/ppermute | solution.py:307
  46.2 34.8 %collective-permute-start.4 = (bf16[784,768]{1,0:T(8,128)(2,1)S(1)}, bf16[784,768]{1,0:T(8,128)(2,1)S(1)}, u32[]{:S(2)}, u32[]{:S(2)}) collective-permute-start(bf16[784,768]{1,0:T(8,128)(2,1)S(1)} %constant_dynamic-update-slice_fusion), channel_id=1, source_target_pairs={{0,4},{1,3},{2,6},{3,1},{4,0},{5,7},{6,2},{7,5},{8,12},{9,11},{10,... | collective-permute-start | bytes 3612680 | tf_op jit(solution)/shard_map/ppermute | solution.py:307
  56.9 12.6 %collective-permute-start.13 = (bf16[384,768]{1,0:T(8,128)(2,1)S(1)}, bf16[384,768]{1,0:T(8,128)(2,1)S(1)}, u32[]{:S(2)}, u32[]{:S(2)}) collective-permute-start(bf16[384,768]{1,0:T(8,128)(2,1)S(1)} %pad_maximum_fusion.6), channel_id=1, source_target_pairs={{0,2},{1,5},{2,0},{3,7},{4,6},{5,1},{6,4},{7,3},{8,10},{9,13},{10,... | collective-permute-start | bytes 1769480 | tf_op jit(solution)/shard_map/ppermute | solution.py:307
  57.1 22.3 %collective-permute-start.8 = (bf16[384,768]{1,0:T(8,128)(2,1)S(1)}, bf16[384,768]{1,0:T(8,128)(2,1)S(1)}, u32[]{:S(2)}, u32[]{:S(2)}) collective-permute-start(bf16[384,768]{1,0:T(8,128)(2,1)S(1)} %pad_maximum_fusion.5), channel_id=1, source_target_pairs={{0,2},{1,5},{2,0},{3,7},{4,6},{5,1},{6,4},{7,3},{8,10},{9,13},{10,... | collective-permute-start | bytes 1769480 | tf_op jit(solution)/shard_map/ppermute | solution.py:307
  69.5 17.8 %collective-permute-start.14 = (bf16[768,768]{1,0:T(8,128)(2,1)S(1)}, bf16[768,768]{1,0:T(8,128)(2,1)S(1)}, u32[]{:S(2)}, u32[]{:S(2)}) collective-permute-start(bf16[768,768]{1,0:T(8,128)(2,1)S(1)} %pad_maximum_fusion.2), channel_id=1, source_target_pairs={{0,4},{1,3},{2,6},{3,1},{4,0},{5,7},{6,2},{7,5},{8,12},{9,11},{10,... | collective-permute-start | bytes 3538952 | tf_op jit(solution)/shard_map/ppermute | solution.py:307
  79.5 20.5 %collective-permute-start.9 = (bf16[768,768]{1,0:T(8,128)(2,1)S(1)}, bf16[768,768]{1,0:T(8,128)(2,1)S(1)}, u32[]{:S(2)}, u32[]{:S(2)}) collective-permute-start(bf16[768,768]{1,0:T(8,128)(2,1)S(1)} %pad_maximum_fusion.1), channel_id=1, source_target_pairs={{0,4},{1,3},{2,6},{3,1},{4,0},{5,7},{6,2},{7,5},{8,12},{9,11},{10,... | collective-permute-start | bytes 3538952 | tf_op jit(solution)/shard_map/ppermute | solution.py:307
  81.1 22.0 %copy-start.8 = (bf16[1552,768]{1,0:T(8,128)(2,1)}, bf16[1552,768]{1,0:T(8,128)(2,1)S(1)}, u32[]{:S(2)}) copy-start(bf16[1552,768]{1,0:T(8,128)(2,1)S(1)} %constant_dynamic-update-slice_fusion.4.lo_ref.att_lo) | copy-start | bytes 7151620
  81.1 22.0 %collective-permute-start.5 = (bf16[1552,768]{1,0:T(8,128)(2,1)S(1)}, bf16[1552,768]{1,0:T(8,128)(2,1)}, u32[]{:S(2)}, u32[]{:S(2)}) collective-permute-start(bf16[1552,768]{1,0:T(8,128)(2,1)S(1)} %constant_dynamic-update-slice_fusion.4.lo_ref.att_lo), channel_id=1, source_target_pairs={{0,1},{1,0},{2,3},{3,2},{4,5},{5,4},{6,7},{7,6},{8,9},{9,8},{10,11... | collective-permute-start | bytes 7151624 | tf_op jit(solution)/shard_map/ppermute | solution.py:307
  88.4 14.1 %copy-start.21 = (s32[2,512]{1,0:T(2,128)S(1)}, s32[2,512]{1,0:T(2,128)}, u32[]{:S(2)}) copy-start(s32[2,512]{1,0:T(2,128)} %param.11) | copy-start | bytes 12292
  88.4 14.1 %copy-start.22 = (s32[2,512]{1,0:T(2,128)S(1)}, s32[2,512]{1,0:T(2,128)}, u32[]{:S(2)}) copy-start(s32[2,512]{1,0:T(2,128)} %param.12) | copy-start | bytes 12292
  88.4 44.4 %collective-permute-start.15 = (bf16[1536,768]{1,0:T(8,128)(2,1)}, bf16[1536,768]{1,0:T(8,128)(2,1)}, u32[]{:S(2)}, u32[]{:S(2)}) collective-permute-start(bf16[1536,768]{1,0:T(8,128)(2,1)} %constant_dynamic-update-slice_fusion.13.lo_b), channel_id=1, source_target_pairs={{0,1},{1,0},{2,3},{3,2},{4,5},{5,4},{6,7},{7,6},{8,9},{9,8},{10,11... | collective-permute-start | bytes 7077896 | tf_op jit(solution)/shard_map/ppermute | solution.py:307
  101.1 31.8 %collective-permute-start.10 = (bf16[1536,768]{1,0:T(8,128)(2,1)}, bf16[1536,768]{1,0:T(8,128)(2,1)}, u32[]{:S(2)}, u32[]{:S(2)}) collective-permute-start(bf16[1536,768]{1,0:T(8,128)(2,1)} %constant_dynamic-update-slice_fusion.8.lo_a), channel_id=1, source_target_pairs={{0,1},{1,0},{2,3},{3,2},{4,5},{5,4},{6,7},{7,6},{8,9},{9,8},{10,11... | collective-permute-start | bytes 7077896 | tf_op jit(solution)/shard_map/ppermute | solution.py:307
  103.1 1.4 copy-start.9
  132.8 36.5 %copy-start.12 = (bf16[1024,768]{1,0:T(8,128)(2,1)}, bf16[1024,768]{1,0:T(8,128)(2,1)S(1)}, u32[]{:S(2)}) copy-start(bf16[1024,768]{1,0:T(8,128)(2,1)S(1)} %get-tuple-element.57.stream_ref) | copy-start | bytes 4718596
  132.8 36.5 %copy-start.14 = (bf16[1024,768]{1,0:T(8,128)(2,1)}, bf16[1024,768]{1,0:T(8,128)(2,1)S(1)}, u32[]{:S(2)}) copy-start(bf16[1024,768]{1,0:T(8,128)(2,1)S(1)} %get-tuple-element.66.ctx_ref) | copy-start | bytes 4718596
  169.3 1.2 copy-start.15
  170.5 1.1 copy-start.16
  171.7 1.4 copy-start.17
  173.1 19.3 %copy-start.10 = (bf16[1024,768]{1,0:T(8,128)(2,1)S(1)}, bf16[1024,768]{1,0:T(8,128)(2,1)}, u32[]{:S(2)}) copy-start(bf16[1024,768]{1,0:T(8,128)(2,1)} %get-tuple-element.61.dctx_ref) | copy-start | bytes 4718596
  191.9 47.1 %collective-permute-start.22 = (bf16[1536,768]{1,0:T(8,128)(2,1)S(1)}, bf16[1536,768]{1,0:T(8,128)(2,1)}, u32[]{:S(2)}, u32[]{:S(2)}) collective-permute-start(bf16[1536,768]{1,0:T(8,128)(2,1)S(1)} %get-tuple-element.83), channel_id=1, source_target_pairs={{0,1},{1,0},{2,3},{3,2},{4,5},{5,4},{6,7},{7,6},{8,9},{9,8},{10,11... | collective-permute-start | bytes 7077896 | tf_op jit(solution)/shard_map/ppermute | solution.py:307
  192.1 49.4 %collective-permute-start.27 = (bf16[1536,768]{1,0:T(8,128)(2,1)}, bf16[1536,768]{1,0:T(8,128)(2,1)}, u32[]{:S(2)}, u32[]{:S(2)}) collective-permute-start(bf16[1536,768]{1,0:T(8,128)(2,1)} %get-tuple-element.85), channel_id=1, source_target_pairs={{0,1},{1,0},{2,3},{3,2},{4,5},{5,4},{6,7},{7,6},{8,9},{9,8},{10,11... | collective-permute-start | bytes 7077896 | tf_op jit(solution)/shard_map/ppermute | solution.py:307
  192.4 26.5 %copy-start.13 = (bf16[1024,768]{1,0:T(8,128)(2,1)S(1)}, bf16[1024,768]{1,0:T(8,128)(2,1)}, u32[]{:S(2)}) copy-start(bf16[1024,768]{1,0:T(8,128)(2,1)} %copy-done.12) | copy-start | bytes 4718596
  217.8 1.1 copy-start.11
  218.9 20.1 %copy-start.19 = (bf16[1536,768]{1,0:T(8,128)(2,1)S(1)}, bf16[1536,768]{1,0:T(8,128)(2,1)}, u32[]{:S(2)}) copy-start(bf16[1536,768]{1,0:T(8,128)(2,1)} %get-tuple-element.82) | copy-start | bytes 7077892
  238.7 6.6 %collective-permute-start.16 = (bf16[1552,768]{1,0:T(8,128)(2,1)}, bf16[1552,768]{1,0:T(8,128)(2,1)S(1)}, u32[]{:S(2)}, u32[]{:S(2)}) collective-permute-start(bf16[1552,768]{1,0:T(8,128)(2,1)} %get-tuple-element.72), channel_id=1, source_target_pairs={{0,1},{1,0},{2,3},{3,2},{4,5},{5,4},{6,7},{7,6},{8,9},{9,8},{10,11... | collective-permute-start | bytes 7151624 | tf_op jit(solution)/shard_map/ppermute | solution.py:307
  239.0 2.5 copy-start.18
  241.4 15.4 %collective-permute-start.23 = (bf16[768,768]{1,0:T(8,128)(2,1)S(1)}, bf16[768,768]{1,0:T(8,128)(2,1)S(1)}, u32[]{:S(2)}, u32[]{:S(2)}) collective-permute-start(bf16[768,768]{1,0:T(8,128)(2,1)S(1)} %get-tuple-element.97), channel_id=1, source_target_pairs={{0,4},{1,3},{2,6},{3,1},{4,0},{5,7},{6,2},{7,5},{8,12},{9,11},{10,... | collective-permute-start | bytes 3538952 | tf_op jit(solution)/shard_map/ppermute | solution.py:307
  241.5 3.8 %copy-start.20 = (bf16[1536,768]{1,0:T(8,128)(2,1)S(1)}, bf16[1536,768]{1,0:T(8,128)(2,1)}, u32[]{:S(2)}) copy-start(bf16[1536,768]{1,0:T(8,128)(2,1)} %get-tuple-element.71) | copy-start | bytes 7077892
  243.9 31.9 %collective-permute-start.28 = (bf16[768,768]{1,0:T(8,128)(2,1)S(1)}, bf16[768,768]{1,0:T(8,128)(2,1)S(1)}, u32[]{:S(2)}, u32[]{:S(2)}) collective-permute-start(bf16[768,768]{1,0:T(8,128)(2,1)S(1)} %get-tuple-element.95), channel_id=1, source_target_pairs={{0,4},{1,3},{2,6},{3,1},{4,0},{5,7},{6,2},{7,5},{8,12},{9,11},{10,... | collective-permute-start | bytes 3538952 | tf_op jit(solution)/shard_map/ppermute | solution.py:307
  246.0 49.0 %collective-permute-start.17 = (bf16[784,768]{1,0:T(8,128)(2,1)S(1)}, bf16[784,768]{1,0:T(8,128)(2,1)S(1)}, u32[]{:S(2)}, u32[]{:S(2)}) collective-permute-start(bf16[784,768]{1,0:T(8,128)(2,1)S(1)} %pad_maximum_fusion), channel_id=1, source_target_pairs={{0,4},{1,3},{2,6},{3,1},{4,0},{5,7},{6,2},{7,5},{8,12},{9,11},{10,... | collective-permute-start | bytes 3612680 | tf_op jit(solution)/shard_map/ppermute | solution.py:307
  257.1 38.4 %collective-permute-start.24 = (bf16[384,768]{1,0:T(8,128)(2,1)S(1)}, bf16[384,768]{1,0:T(8,128)(2,1)S(1)}, u32[]{:S(2)}, u32[]{:S(2)}) collective-permute-start(bf16[384,768]{1,0:T(8,128)(2,1)S(1)} %get-tuple-element.103), channel_id=1, source_target_pairs={{0,2},{1,5},{2,0},{3,7},{4,6},{5,1},{6,4},{7,3},{8,10},{9,13},{10,... | collective-permute-start | bytes 1769480 | tf_op jit(solution)/shard_map/ppermute | solution.py:307
  276.1 20.9 %collective-permute-start.29 = (bf16[384,768]{1,0:T(8,128)(2,1)S(1)}, bf16[384,768]{1,0:T(8,128)(2,1)S(1)}, u32[]{:S(2)}, u32[]{:S(2)}) collective-permute-start(bf16[384,768]{1,0:T(8,128)(2,1)S(1)} %get-tuple-element.101), channel_id=1, source_target_pairs={{0,2},{1,5},{2,0},{3,7},{4,6},{5,1},{6,4},{7,3},{8,10},{9,13},{10,... | collective-permute-start | bytes 1769480 | tf_op jit(solution)/shard_map/ppermute | solution.py:307
  295.4 9.4 %collective-permute-start.18 = (bf16[400,768]{1,0:T(8,128)(2,1)S(1)}, bf16[400,768]{1,0:T(8,128)(2,1)S(1)}, u32[]{:S(2)}, u32[]{:S(2)}) collective-permute-start(bf16[400,768]{1,0:T(8,128)(2,1)S(1)} %pad_maximum_fusion.4), channel_id=1, source_target_pairs={{0,2},{1,5},{2,0},{3,7},{4,6},{5,1},{6,4},{7,3},{8,10},{9,13},{10,... | collective-permute-start | bytes 1843208 | tf_op jit(solution)/shard_map/ppermute | solution.py:307
  295.7 10.5 %collective-permute-start.25 = (bf16[192,768]{1,0:T(8,128)(2,1)S(1)}, bf16[192,768]{1,0:T(8,128)(2,1)S(1)}, u32[]{:S(2)}, u32[]{:S(2)}) collective-permute-start(bf16[192,768]{1,0:T(8,128)(2,1)S(1)} %get-tuple-element.109), channel_id=1, source_target_pairs={{0,8},{1,9},{2,10},{3,11},{4,12},{5,13},{6,14},{7,15},{8,0},{9,1},... | collective-permute-start | bytes 884744 | tf_op jit(solution)/shard_map/ppermute | solution.py:307
  297.1 12.4 %collective-permute-start.30 = (bf16[192,768]{1,0:T(8,128)(2,1)S(1)}, bf16[192,768]{1,0:T(8,128)(2,1)S(1)}, u32[]{:S(2)}, u32[]{:S(2)}) collective-permute-start(bf16[192,768]{1,0:T(8,128)(2,1)S(1)} %get-tuple-element.107), channel_id=1, source_target_pairs={{0,8},{1,9},{2,10},{3,11},{4,12},{5,13},{6,14},{7,15},{8,0},{9,1},... | collective-permute-start | bytes 884744 | tf_op jit(solution)/shard_map/ppermute | solution.py:307
  305.0 16.1 %collective-permute-start.19 = (bf16[208,768]{1,0:T(8,128)(2,1)S(1)}, bf16[208,768]{1,0:T(8,128)(2,1)S(1)}, u32[]{:S(2)}, u32[]{:S(2)}) collective-permute-start(bf16[208,768]{1,0:T(8,128)(2,1)S(1)} %pad_maximum_fusion.8), channel_id=1, source_target_pairs={{0,8},{1,9},{2,10},{3,11},{4,12},{5,13},{6,14},{7,15},{8,0},{9,1},... | collective-permute-start | bytes 958472 | tf_op jit(solution)/shard_map/ppermute | solution.py:307
  306.2 16.2 %collective-permute-start.26 = (bf16[96,768]{1,0:T(8,128)(2,1)S(1)}, bf16[96,768]{1,0:T(8,128)(2,1)S(1)}, u32[]{:S(2)}, u32[]{:S(2)}) collective-permute-start(bf16[96,768]{1,0:T(8,128)(2,1)S(1)} %add_convert_fusion.19), channel_id=1, source_target_pairs={{0,16},{1,17},{2,18},{3,19},{4,20},{5,21},{6,22},{7,23},{8,24},{9,... | collective-permute-start | bytes 442376 | tf_op jit(solution)/shard_map/ppermute | solution.py:307
  309.5 13.0 %collective-permute-start.31 = (bf16[96,768]{1,0:T(8,128)(2,1)S(1)}, bf16[96,768]{1,0:T(8,128)(2,1)S(1)}, u32[]{:S(2)}, u32[]{:S(2)}) collective-permute-start(bf16[96,768]{1,0:T(8,128)(2,1)S(1)} %add_convert_fusion.18), channel_id=1, source_target_pairs={{0,16},{1,17},{2,18},{3,19},{4,20},{5,21},{6,22},{7,23},{8,24},{9,... | collective-permute-start | bytes 442376 | tf_op jit(solution)/shard_map/ppermute | solution.py:307
  321.1 15.0 %collective-permute-start.20 = (bf16[112,768]{1,0:T(8,128)(2,1)S(1)}, bf16[112,768]{1,0:T(8,128)(2,1)S(1)}, u32[]{:S(2)}, u32[]{:S(2)}) collective-permute-start(bf16[112,768]{1,0:T(8,128)(2,1)S(1)} %pad_maximum_fusion.12), channel_id=1, source_target_pairs={{0,16},{1,17},{2,18},{3,19},{4,20},{5,21},{6,22},{7,23},{8,24},{9,... | collective-permute-start | bytes 516104 | tf_op jit(solution)/shard_map/ppermute | solution.py:307
  322.6 15.9 %copy-start.1 = (f32[1154,128]{1,0:T(8,128)S(1)}, f32[1154,128]{1,0:T(8,128)}, u32[]{:S(2)}) copy-start(f32[1154,128]{1,0:T(8,128)} %w_ref.3) | copy-start | bytes 1772548
  322.6 15.9 %copy-start.4 = (f32[1154,128]{1,0:T(8,128)S(1)}, f32[1154,128]{1,0:T(8,128)}, u32[]{:S(2)}) copy-start(f32[1154,128]{1,0:T(8,128)} %m_ref.3) | copy-start | bytes 1772548
  322.6 15.9 %copy-start.5 = (f32[1154,128]{1,0:T(8,128)S(1)}, f32[1154,128]{1,0:T(8,128)}, u32[]{:S(2)}) copy-start(f32[1154,128]{1,0:T(8,128)} %a_ref.3) | copy-start | bytes 1772548
  322.7 15.8 %collective-permute-start.32 = (f32[64,128]{1,0:T(8,128)S(1)}, f32[64,128]{1,0:T(8,128)S(1)}, u32[]{:S(2)}, u32[]{:S(2)}) collective-permute-start(f32[64,128]{1,0:T(8,128)S(1)} %slice.321), channel_id=1, source_target_pairs={{1,0},{2,1},{3,2},{4,3},{5,4},{6,5},{7,6},{8,7},{9,8},{10,9},{11,1... | collective-permute-start | bytes 98312 | tf_op jit(solution)/shard_map/ppermute | solution.py:1068
  336.2 7.2 %copy-start.3 = (f32[578,128]{1,0:T(8,128)S(1)}, f32[578,128]{1,0:T(8,128)}, u32[]{:S(2)}) copy-start(f32[578,128]{1,0:T(8,128)} %w_ref.2) | copy-start | bytes 887812
  336.2 7.2 %copy-start.6 = (f32[578,128]{1,0:T(8,128)S(1)}, f32[578,128]{1,0:T(8,128)}, u32[]{:S(2)}) copy-start(f32[578,128]{1,0:T(8,128)} %m_ref.2) | copy-start | bytes 887812
  336.3 7.2 %copy-start.7 = (f32[578,128]{1,0:T(8,128)S(1)}, f32[578,128]{1,0:T(8,128)}, u32[]{:S(2)}) copy-start(f32[578,128]{1,0:T(8,128)} %a_ref.2) | copy-start | bytes 887812
  336.3 7.2 %collective-permute-start.21 = (f32[64,128]{1,0:T(8,128)S(1)}, f32[64,128]{1,0:T(8,128)S(1)}, u32[]{:S(2)}, u32[]{:S(2)}) collective-permute-start(f32[64,128]{1,0:T(8,128)S(1)} %slice.291), channel_id=1, source_target_pairs={{1,0},{2,1},{3,2},{4,3},{5,4},{6,5},{7,6},{8,7},{9,8},{10,9},{11,1... | collective-permute-start | bytes 98312 | tf_op jit(solution)/shard_map/ppermute | solution.py:1070

commit v2 on v0

--- a/solution.py
+++ b/solution.py
@@ -1,8 +1,11 @@
+import functools
 import math
 
 import jax
 import jax.numpy as jnp
 from jax import lax
+from jax.experimental import pallas as pl
+from jax.experimental.pallas import tpu as pltpu
 from jax.sharding import PartitionSpec as P
 
 HEAD_DIM = 64
@@ -238,6 +241,990 @@
     )
 
 
+BF = jnp.bfloat16
+F32 = jnp.float32
+LANES = 128
+SLOT = 96
+TILE = 256
+EXTRA = 16
+MIB = 1 << 20
+BIG = 58
+
+
+def params(limit):
+    return pltpu.CompilerParams(vmem_limit_bytes=limit * MIB)
+
+
+def spec_any():
+    return pl.BlockSpec(memory_space=pl.ANY)
+
+
+def spec_vmem():
+    return pl.BlockSpec(memory_space=pltpu.VMEM)
+
+
+def spec_whole(shape):
+    return pl.BlockSpec(shape, lambda *ids: (0,) * len(shape))
+
+
+def dot_nn(left, right):
+    return lax.dot_general(left, right, (((1,), (0,)), ((), ())), preferred_element_type=F32)
+
+
+def dot_nt(left, right):
+    return lax.dot_general(left, right, (((1,), (1,)), ((), ())), preferred_element_type=F32)
+
+
+def dot_tn(left, right):
+    return lax.dot_general(left, right, (((0,), (0,)), ((), ())), preferred_element_type=F32)
+
+
+def slot_of(chunk, me, late=False):
+    diff = lax.bitwise_xor(me, chunk)
+    far_core = lax.bitwise_and(diff, 1)
+    x_bit = lax.bitwise_and(lax.shift_right_logical(diff, 1), 1)
+    y_bit = lax.bitwise_and(lax.shift_right_logical(diff, 2), 1)
+    z_low = lax.bitwise_and(lax.shift_right_logical(diff, 3), 1)
+    z_high = lax.shift_right_logical(diff, 4)
+    core = lax.bitwise_xor(lax.bitwise_and(me, 1), far_core)
+    third = x_bit + core * (y_bit - x_bit)
+    fourth = y_bit + core * (x_bit - y_bit)
+    if late:
+        return far_core, z_high + 2 * third + 4 * z_low + 8 * fourth
+    return far_core, z_high + 2 * z_low + 4 * third + 8 * fourth
+
+
+def stage_perm(stage):
+    if stage == 0:
+        return [(i, i ^ 16) for i in range(32)]
+    if stage == 1:
+        return [(i, i ^ 8) for i in range(32)]
+    if stage == 2:
+        return [(i, i ^ (4 if i & 1 else 2)) for i in range(32)]
+    if stage == 3:
+        return [(i, i ^ (2 if i & 1 else 4)) for i in range(32)]
+    return [(i, i ^ 1) for i in range(32)]
+
+
+def exchange(array, stage):
+    return lax.ppermute(array, "fsdp", stage_perm(stage))
+
+
+def widen(held, got):
+    return jnp.concatenate([held, got])
+
+
+def widen_small(held, got):
+    low = held.shape[0] - EXTRA
+    small = held[low:] + got[low:]
+    return jnp.concatenate([held[:low], got[:low], small])
+
+
+def total_of(arrays, first, last):
+    total = arrays[0][first:last].astype(F32)
+    for array in arrays[1:]:
+        total = total + array[first:last].astype(F32)
+    return total
+
+
+def halve(*arrays):
+    rows = arrays[0].shape[0]
+    low = total_of(arrays, 0, rows // 2).astype(BF)
+    return low, total_of(arrays, rows // 2, rows).astype(BF)
+
+
+def add_small(values, small):
+    return jnp.concatenate([values, small.astype(BF)])
+
+
+def phase(*values):
+    return lax.optimization_barrier(values)
+
+
+def prep_kernel(last, att_mats, ffn_mats, att_ref, ffn_ref, tail_ref, att_out, small_out, ffn_a, ffn_b, att_buf, ffn_buf):
+    me = lax.axis_index("fsdp")
+    att_rows = att_ref.shape[0]
+    ffn_rows = ffn_ref.shape[0]
+    att_buf[0:64, :] = tail_ref[0:64, :]
+    att_buf[64 : 64 + att_rows, :] = att_ref[...]
+    ffn_buf[0:64, :] = tail_ref[64:128, :]
+    ffn_buf[64 : 64 + ffn_rows, :] = ffn_ref[...]
+    start = 64 - 2 * me
+    for part in range(6):
+        cols = slice(part * LANES, (part + 1) * LANES)
+        att_out[:, cols] = att_buf[pl.ds(start + part, SLOT, stride=6), :].astype(BF)
+    first = me < 16
+
+    @pl.when(first)
+    def _():
+        for block in range(4):
+            out = ffn_a if block < 2 else ffn_b
+            rows = slice((block % 2) * 48, (block % 2) * 48 + 48)
+            for part in range(6):
+                cols = slice(part * LANES, (part + 1) * LANES)
+                piece = ffn_buf[pl.ds(start + 6 * block + part, 48, stride=24), :]
+                out[rows, cols] = piece.astype(BF)
+
+    @pl.when(jnp.logical_not(first))
+    def _():
+        for part in range(6):
+            cols = slice(part * LANES, (part + 1) * LANES)
+            ffn_a[:, cols] = ffn_buf[pl.ds(start + part, SLOT, stride=6), :].astype(BF)
+            ffn_b[:, cols] = ffn_buf[pl.ds(start + 6 * SLOT + part, SLOT, stride=6), :].astype(BF)
+
+    small_out[...] = jnp.zeros_like(small_out)
+
+    @pl.when(me == last)
+    def _():
+        att_at = 64 + att_mats - last * att_rows
+        ffn_at = 64 + ffn_mats - last * ffn_rows
+        for part in range(6):
+            cols = slice(part * LANES, (part + 1) * LANES)
+            upper = att_buf[pl.ds(att_at + part, 6, stride=6), :]
+            lower = ffn_buf[pl.ds(ffn_at + part, 7, stride=6), :]
+            both = jnp.concatenate([upper, lower, jnp.zeros((3, LANES), F32)])
+            small_out[:, cols] = both.astype(BF)
+
+
+def prepare(att_master, ffn_master, tails, devices, width):
+    att_mats = 4 * width * width // LANES
+    ffn_mats = 2 * width * FF // LANES
+    att_rows, ffn_rows = att_master.shape[0], ffn_master.shape[0]
+    body = functools.partial(prep_kernel, devices - 1, att_mats, ffn_mats)
+    return pl.pallas_call(
+        body,
+        out_shape=(
+            jax.ShapeDtypeStruct((SLOT, width), BF),
+            jax.ShapeDtypeStruct((EXTRA, width), BF),
+            jax.ShapeDtypeStruct((SLOT, width), BF),
+            jax.ShapeDtypeStruct((SLOT, width), BF),
+        ),
+        in_specs=[spec_vmem()] * 3,
+        out_specs=(spec_vmem(),) * 4,
+        scratch_shapes=[
+            pltpu.VMEM((64 + att_rows + 6, LANES), F32),
+            pltpu.VMEM((64 + ffn_rows + 6, LANES), F32),
+        ],
+        compiler_params=params(16),
+        name="prep",
+    )(att_master, ffn_master, tails)
+
+
+def pick(index, refs, use):
+    for number in range(len(refs)):
+
+        @pl.when(index == number)
+        def _():
+            use(refs[number])
+
+
+def start_copy(quad, far_core, slot, offset, rows, dst, sem):
+    at = pl.multiple_of(lax.bitwise_and(slot, 7) * SLOT + offset, 16)
+
+    def copy(ref):
+        pltpu.make_async_copy(ref.at[pl.ds(at, rows), :], dst, sem).start()
+
+    pick(2 * far_core + lax.shift_right_logical(slot, 3), quad, copy)
+
+
+def load_att(quad, dst, sem, first, last):
+    me = lax.axis_index("fsdp")
+
+    def body(chunk, carry):
+        far_core, slot = slot_of(chunk, me)
+        at = pl.multiple_of((chunk - first) * SLOT, 32)
+        start_copy(quad, far_core, slot, 0, SLOT, dst.at[pl.ds(at, SLOT), :], sem)
+        return carry
+
+    lax.fori_loop(first, last, body, 0)
+
+
+def load_ffn(quads, w_in, w_out, sem_in, sem_out):
+    me = lax.axis_index("fsdp")
+    for block in range(4):
+        unit = block // 2
+
+        def body_in(chunk, carry):
+            far_core, slot = slot_of(chunk, me, unit == 1)
+            dst = w_in.at[block, pl.ds(pl.multiple_of(chunk * 48, 16), 48), :]
+            start_copy(quads[unit], far_core, slot, (block % 2) * 48, 48, dst, sem_in.at[block])
+            return carry
+
+        def body_out(chunk, carry):
+            for which in range(2):
+                far_core, slot = slot_of(chunk, me, which == 1)
+                at = pl.multiple_of((chunk - 16) * 192 + which * SLOT, 32)
+                dst = w_out.at[pl.ds(at, SLOT), :]
+                start_copy(quads[which], far_core, slot, 0, SLOT, dst, sem_out.at[block])
+            return carry
+
+        lax.fori_loop(0, 16, body_in, 0)
+        lax.fori_loop(16 + 4 * block, 20 + 4 * block, body_out, 0)
+
+
+def wait_whole(ref, sem):
+    pltpu.make_async_copy(ref, ref, sem).wait()
+
+
+def head_mask(rows):
+    lane = lax.broadcasted_iota(jnp.int32, (rows, LANES), 1)
+    return lane < HEAD_DIM
+
+
+def project_kernel(x_ref, masked_ref, *refs):
+    quad = refs[0:4]
+    stream_ref, q_ref, k_ref, v_ref, small_ref, weights, smalls, sems, small_sem = refs[4:]
+    width = x_ref.shape[1]
+
+    @pl.when(pl.program_id(0) == 0)
+    def _():
+        for part in range(4):
+            src = quad[part].at[pl.ds(8 * SLOT, EXTRA), :]
+            pltpu.make_async_copy(src, smalls.at[part], small_sem).start()
+        for matrix in range(3):
+            rows = weights.at[matrix * width : (matrix + 1) * width]
+            load_att(quad, rows, sems.at[matrix], 8 * matrix, 8 * matrix + 8)
+        wait_whole(smalls, small_sem)
+        total = smalls[0].astype(F32)
+        for part in range(1, 4):
+            total = total + smalls[part].astype(F32)
+        small_ref[...] = total
+
+    small = small_ref[...]
+    stream = jnp.where(masked_ref[...] == 1, small[5:6], x_ref[...].astype(F32)).astype(BF)
+    stream_ref[...] = stream
+    for matrix in range(3):
+        rows = slice(matrix * width, (matrix + 1) * width)
+
+        @pl.when(pl.program_id(0) == 0)
+        def _():
+            wait_whole(weights.at[rows], sems.at[matrix])
+
+        product = dot_nn(stream, weights[rows])
+        if matrix == 0:
+            q_ref[...] = ((product + small[0:1]) * 0.125).astype(BF)
+        elif matrix == 1:
+            k_ref[...] = product.astype(BF)
+        else:
+            v_ref[...] = (product + small[1:2]).astype(BF)
+
+
+def project(block_input, masked_col, quad):
+    tok, width = block_input.shape
+    rows = 2 * TILE
+    tile = lambda cols: pl.BlockSpec((rows, cols), lambda s: (s, 0))
+    bf = jax.ShapeDtypeStruct((tok, width), BF)
+    return pl.pallas_call(
+        project_kernel,
+        grid=(tok // rows,),
+        out_shape=(bf, bf, bf, bf, jax.ShapeDtypeStruct((EXTRA, width), F32)),
+        in_specs=[tile(width), tile(1)] + [spec_any()] * 4,
+        out_specs=(tile(width),) * 4 + (spec_whole((EXTRA, width)),),
+        scratch_shapes=[
+            pltpu.VMEM((3 * width, width), BF),
+            pltpu.VMEM((4, EXTRA, width), BF),
+            pltpu.SemaphoreType.DMA((3,)),
+            pltpu.SemaphoreType.DMA,
+        ],
+        compiler_params=params(BIG),
+        cost_estimate=pl.CostEstimate(
+            flops=6 * tok * width * width, bytes_accessed=16 * MIB, transcendentals=0
+        ),
+        name="project",
+    )(block_input, masked_col, *quad)
+
+
+def forward_kernel(held, q_ref, k_ref, v_ref, seg_col_ref, seg_row_ref, *refs):
+    ctx_ref, lse_ref = refs[held:]
+    left = head_mask(q_ref.shape[0])
+    same = seg_col_ref[...] == seg_row_ref[0]
+    queries = q_ref[...]
+    keys = k_ref[...]
+    values_t = v_ref[...].T
+    outs = []
+    for head in range(2):
+        keep = left if head == 0 else jnp.logical_not(left)
+        own = jnp.where(keep, queries, jnp.zeros_like(queries))
+        scores = jnp.where(same, dot_nt(keys, own), MASKED_SCORE)
+        top = jnp.max(scores, axis=0, keepdims=True)
+        exponent = jnp.exp(scores - top)
+        total = jnp.sum(exponent, axis=0, keepdims=True)
+        probs = (exponent * (1.0 / total)).astype(BF)
+        lse_ref[0, 0, head : head + 1, :] = top + jnp.log(total)
+        outs.append(dot_nn(values_t[head * HEAD_DIM : (head + 1) * HEAD_DIM], probs))
+    ctx_ref[...] = jnp.concatenate(outs).T.astype(BF)
+
+
+def sequence_specs(at, seq):
+    tile = lambda: pl.BlockSpec((seq, LANES), lambda i: (at, i))
+    col = lambda: pl.BlockSpec((seq, 1), lambda i: (at, 0))
+    row = lambda: pl.BlockSpec((1, 1, seq), lambda i: (at, 0, 0))
+    stat = lambda: pl.BlockSpec((1, 1, 2, seq), lambda i: (at, i, 0, 0))
+    return tile, col, row, stat
+
+
+def attention_forward(at, q, k, v, seg_col, seg_row, held=()):
+    tok, width = q.shape
+    seq_count, seq = seg_row.shape[0], seg_row.shape[2]
+    pairs = width // LANES
+    tile, col, row, stat = sequence_specs(at, seq)
+    return pl.pallas_call(
+        functools.partial(forward_kernel, len(held)),
+        grid=(pairs,),
+        out_shape=(
+            jax.ShapeDtypeStruct((tok, width), BF),
+            jax.ShapeDtypeStruct((seq_count, pairs, 2, seq), F32),
+        ),
+        in_specs=[tile(), tile(), tile(), col(), row()] + [spec_any() for _ in held],
+        out_specs=(tile(), stat()),
+        input_output_aliases={5 + i: i for i in range(len(held))},
+        compiler_params=params(BIG),
+        cost_estimate=pl.CostEstimate(
+            flops=16 * seq * seq * width,
+            bytes_accessed=4 * MIB,
+            transcendentals=seq * seq * width // HEAD_DIM,
+        ),
+        name="attention_forward",
+    )(q, k, v, seg_col, seg_row, *held)
+
+
+def norm_stats(pre_norm):
+    center = pre_norm - jnp.mean(pre_norm, axis=-1, keepdims=True)
+    scale = lax.rsqrt(jnp.mean(center * center, axis=-1, keepdims=True) + EPSILON)
+    return center * scale, scale
+
+
+def norm_back(grad, gain, normed, scale):
+    scaled = grad * gain
+    mean_one = jnp.mean(scaled, axis=-1, keepdims=True)
+    mean_two = jnp.mean(scaled * normed, axis=-1, keepdims=True)
+    return scale * (scaled - mean_one - normed * mean_two)
+
+
+def column_sum(array):
+    return jnp.sum(array, axis=0, keepdims=True)
+
+
+def gelu_pair(inputs):
+    phi_cdf = 0.5 + 0.5 * lax.erf(inputs * math.sqrt(0.5))
+    density = jnp.exp(inputs * inputs * -0.5) * (1.0 / math.sqrt(2.0 * math.pi))
+    return inputs * phi_cdf, phi_cdf + inputs * density
+
+
+def ffn_kernel(
+    stream_ref,
+    ctx_ref,
+    grad_ref,
+    small_ref,
+    *refs,
+):
+    att_quad, quad_a, quad_b = refs[0:4], refs[4:8], refs[8:12]
+    y_ref, x1_ref, hid_ref, dhid_ref, dfb_ref, dpre_ref, dob_ref, dctx_ref, sums_ref = refs[12:21]
+    w_in, w_out, w_o, slope, sem_in, sem_out, sem_o = refs[21:]
+    width = ctx_ref.shape[1]
+    blocks = FF // width
+    step = pl.program_id(0)
+
+    @pl.when(step == 0)
+    def _():
+        load_att(att_quad, w_o, sem_o, 24, 32)
+        load_ffn((quad_a, quad_b), w_in, w_out, sem_in, sem_out)
+        sums_ref[...] = jnp.zeros_like(sums_ref)
+
+    @pl.when(step == 0)
+    def _():
+        wait_whole(w_o, sem_o)
+
+    small = small_ref[...]
+    pre_one = stream_ref[...].astype(F32) + dot_nn(ctx_ref[...], w_o[...]) + small[2:3]
+    normed_one, scale_one = norm_stats(pre_one)
+    x_one = normed_one * small[3:4] + small[4:5]
+    x_low = x_one.astype(BF)
+    x1_ref[...] = x_low
+
+    total = x_one + small[10:11]
+    for block in range(blocks):
+        cols = slice(block * width, (block + 1) * width)
+
+        @pl.when(step == 0)
+        def _():
+            wait_whole(w_in.at[block], sem_in.at[block])
+            wait_whole(w_out.at[cols, :], sem_out.at[block])
+
+        hidden, gate = gelu_pair(dot_nn(x_low, w_in[block]) + small[6 + block : 7 + block])
+        hidden = hidden.astype(BF)
+        hid_ref[:, cols] = hidden
+        slope[block] = gate
+        total = total + dot_nn(hidden, w_out[cols, :])
+    normed_two, scale_two = norm_stats(total)
+    y_ref[...] = (normed_two * small[11:12] + small[12:13]).astype(BF)
+    grad_out = grad_ref[...].astype(F32)
+    grad_two = norm_back(grad_out, small[11:12], normed_two, scale_two)
+    grad_low = grad_two.astype(BF)
+    dfb_ref[...] = grad_low
+    sums_ref[10:11] += column_sum(grad_low.astype(F32))
+    sums_ref[11:12] += column_sum(grad_out * normed_two)
+    sums_ref[12:13] += column_sum(grad_out)
+    grad_one = grad_two
+    for block in range(blocks):
+        cols = slice(block * width, (block + 1) * width)
+        dhid = (dot_nt(grad_low, w_out[cols, :]) * slope[block]).astype(BF)
+        dhid_ref[:, cols] = dhid
+        sums_ref[6 + block : 7 + block] += column_sum(dhid.astype(F32))
+        grad_one = grad_one + dot_nt(dhid, w_in[block])
+    sums_ref[3:4] += column_sum(grad_one * normed_one)
+    sums_ref[4:5] += column_sum(grad_one)
+    grad_pre = norm_back(grad_one, small[3:4], normed_one, scale_one)
+    dpre_ref[...] = grad_pre
+    dob = grad_pre.astype(BF)
+    dob_ref[...] = dob
+    sums_ref[2:3] += column_sum(dob.astype(F32))
+    dctx_ref[...] = dot_nt(dob, w_o[...]).astype(BF)
+
+
+def feed_forward(stream, ctx, out_grad, small, att_quad, quad_a, quad_b):
+    tok, width = ctx.shape
+    tile = lambda cols: pl.BlockSpec((TILE, cols), lambda i: (i, 0))
+    bf = lambda cols: jax.ShapeDtypeStruct((tok, cols), BF)
+    return pl.pallas_call(
+        ffn_kernel,
+        grid=(tok // TILE,),
+        out_shape=(
+            bf(width),
+            bf(width),
+            bf(FF),
+            bf(FF),
+            bf(width),
+            jax.ShapeDtypeStruct((tok, width), F32),
+            bf(width),
+            bf(width),
+            jax.ShapeDtypeStruct((EXTRA, width), F32),
+        ),
+        in_specs=[tile(width)] * 3 + [spec_whole((EXTRA, width))] + [spec_any()] * 12,
+        out_specs=(
+            tile(width),
+            tile(width),
+            tile(FF),
+            tile(FF),
+            tile(width),
+            tile(width),
+            tile(width),
+            tile(width),
+            spec_whole((EXTRA, width)),
+        ),
+        scratch_shapes=[
+            pltpu.VMEM((FF // width, width, width), BF),
+            pltpu.VMEM((FF, width), BF),
+            pltpu.VMEM((width, width), BF),
+            pltpu.VMEM((FF // width, TILE, width), F32),
+            pltpu.SemaphoreType.DMA((FF // width,)),
+            pltpu.SemaphoreType.DMA((FF // width,)),
+            pltpu.SemaphoreType.DMA,
+        ],
+        compiler_params=params(BIG),
+        cost_estimate=pl.CostEstimate(
+            flops=8 * tok * width * FF, bytes_accessed=40 * MIB, transcendentals=2 * tok * FF
+        ),
+        name="feed_forward",
+    )(stream, ctx, out_grad, small, *att_quad, *quad_a, *quad_b)
+
+
+def send_slot(parts, far_core, slot, offset, src, sem):
+    at = pl.multiple_of(lax.bitwise_and(slot, 7) * SLOT + offset, 16)
+
+    def copy(ref):
+        pltpu.make_async_copy(src, ref.at[pl.ds(at, src.shape[0]), :], sem).start()
+
+    pick(2 * far_core + lax.shift_right_logical(slot, 3), parts, copy)
+
+
+def part_shapes(width, small):
+    rows = [8 * SLOT, 8 * SLOT, 8 * SLOT, 8 * SLOT + (EXTRA if small else 0)]
+    return tuple(jax.ShapeDtypeStruct((count, width), BF) for count in rows)
+
+
+def wait_reuse(stage, sems, buf, step):
+    @pl.when(step >= 2)
+    def _():
+        wait_whole(stage.at[buf], sems.at[buf])
+
+
+def wait_last(stage, sems, step, steps):
+    @pl.when(step == steps - 1)
+    def _():
+        for buf in range(2):
+            wait_whole(stage.at[buf], sems.at[buf])
+
+
+def send_in_blocks(parts, me, late, part, stage, buf, sem):
+    for chunk in range(16):
+        far_core, slot = slot_of(chunk, me, late)
+        src = stage.at[buf, chunk * 48 : (chunk + 1) * 48]
+        send_slot(parts, far_core, slot, part * 48, src, sem)
+
+
+def ffn_grad_kernel(x_ref, hid_ref, dhid_ref, dfb_ref, sums_ref, *refs):
+    parts_a, parts_b = refs[0:4], refs[4:8]
+    stage, small_stage, sems, small_sem = refs[8:]
+    me = lax.axis_index("fsdp")
+    step = pl.program_id(0)
+    buf = lax.rem(step, 2)
+    small_rows = parts_b[3].at[pl.ds(8 * SLOT, EXTRA), :]
+
+    @pl.when(step == 0)
+    def _():
+        small_stage[...] = sums_ref[...].astype(BF)
+        pltpu.make_async_copy(small_stage, small_rows, small_sem).start()
+
+    wait_reuse(stage, sems, buf, step)
+
+    @pl.when(step < 4)
+    def _():
+        stage[buf] = dot_tn(hid_ref[...], dfb_ref[...]).astype(BF)
+        for piece in range(8):
+            late = piece % 2 == 1
+            far_core, slot = slot_of(16 + 4 * step + piece // 2, me, late)
+            src = stage.at[buf, piece * SLOT : (piece + 1) * SLOT]
+            send_slot(parts_b if late else parts_a, far_core, slot, 0, src, sems.at[buf])
+
+    @pl.when(step >= 4)
+    def _():
+        stage[buf] = dot_tn(x_ref[...], dhid_ref[...]).astype(BF)
+        send_in_blocks(parts_b, me, True, step - 4, stage, buf, sems.at[buf])
+
+    @pl.when(step == 5)
+    def _():
+        wait_whole(small_stage, small_sem)
+
+    wait_last(stage, sems, step, 6)
+
+
+def ffn_grads(x_low, hidden, dhid, dfb, sums):
+    tok, width = x_low.shape
+    out = pl.pallas_call(
+        ffn_grad_kernel,
+        grid=(6,),
+        out_shape=part_shapes(width, False) + part_shapes(width, True),
+        in_specs=[
+            spec_whole((tok, width)),
+            pl.BlockSpec((tok, width), lambda i: (0, jnp.minimum(i, 3))),
+            pl.BlockSpec((tok, width), lambda i: (0, jnp.maximum(i - 2, 2))),
+            spec_whole((tok, width)),
+            spec_whole((EXTRA, width)),
+        ],
+        out_specs=(spec_any(),) * 8,
+        scratch_shapes=[
+            pltpu.VMEM((2, width, width), BF),
+            pltpu.VMEM((EXTRA, width), BF),
+            pltpu.SemaphoreType.DMA((2,)),
+            pltpu.SemaphoreType.DMA,
+        ],
+        compiler_params=params(BIG),
+        cost_estimate=pl.CostEstimate(
+            flops=3 * tok * width * FF, bytes_accessed=24 * MIB, transcendentals=0
+        ),
+        name="ffn_grads",
+    )(x_low, hidden, dhid, dfb, sums)
+    return out[0:4], out[4:8]
+
+
+def ffn_rest_kernel(x_ref, dhid_ref, *refs):
+    parts = refs[4:8]
+    stage, sems = refs[8:]
+    me = lax.axis_index("fsdp")
+    step = pl.program_id(0)
+    stage[step] = dot_tn(x_ref[...], dhid_ref[...]).astype(BF)
+    send_in_blocks(parts, me, False, step, stage, step, sems.at[step])
+    wait_last(stage, sems, step, 2)
+
+
+def ffn_rest(x_low, dhid, parts):
+    tok, width = x_low.shape
+    return pl.pallas_call(
+        ffn_rest_kernel,
+        grid=(2,),
+        out_shape=part_shapes(width, False),
+        in_specs=[spec_whole((tok, width)), pl.BlockSpec((tok, width), lambda i: (0, i))]
+        + [spec_any()] * 4,
+        out_specs=(spec_any(),) * 4,
+        input_output_aliases={2 + i: i for i in range(4)},
+        scratch_shapes=[pltpu.VMEM((2, width, width), BF), pltpu.SemaphoreType.DMA((2,))],
+        compiler_params=params(BIG),
+        cost_estimate=pl.CostEstimate(
+            flops=tok * width * FF, bytes_accessed=8 * MIB, transcendentals=0
+        ),
+        name="ffn_rest",
+    )(x_low, dhid, *parts)
+
+
+def backward_kernel(held, q_ref, k_ref, v_ref, dctx_ref, lse_ref, seg_col_ref, seg_row_ref, *refs):
+    dq_ref, dk_ref, dv_ref = refs[held:]
+    left = head_mask(q_ref.shape[0])
+    same = seg_col_ref[...] == seg_row_ref[0]
+    queries = q_ref[...]
+    keys = k_ref[...]
+    values = v_ref[...]
+    grads = dctx_ref[...]
+    keys_t = keys.T
+    grad_q = []
+    grad_k = None
+    grad_v = None
+    for head in range(2):
+        keep = left if head == 0 else jnp.logical_not(left)
+        own = jnp.where(keep, queries, jnp.zeros_like(queries))
+        own_grad = jnp.where(keep, grads, jnp.zeros_like(grads))
+        log_total = lse_ref[0, 0, head : head + 1, :]
+        scores = jnp.where(same, dot_nt(keys, own), MASKED_SCORE)
+        probs = jnp.exp(scores - log_total)
+        grad_probs = dot_nt(values, own_grad)
+        inner = jnp.sum(grad_probs * probs, axis=0, keepdims=True)
+        grad_scores = (probs * (grad_probs - inner)).astype(BF)
+        part_v = dot_nn(probs.astype(BF), own_grad)
+        part_k = dot_nn(grad_scores, own)
+        grad_v = part_v if head == 0 else grad_v + part_v
+        grad_k = part_k if head == 0 else grad_k + part_k
+        grad_q.append(dot_nn(keys_t[head * HEAD_DIM : (head + 1) * HEAD_DIM], grad_scores))
+    dq_ref[...] = (jnp.concatenate(grad_q).T.astype(BF) * 0.125).astype(BF)
+    dk_ref[...] = grad_k.astype(BF)
+    dv_ref[...] = grad_v.astype(BF)
+
+
+def attention_backward(at, q, k, v, dctx, lse, seg_col, seg_row, held=()):
+    tok, width = q.shape
+    seq = seg_row.shape[2]
+    tile, col, row, stat = sequence_specs(at, seq)
+    return pl.pallas_call(
+        functools.partial(backward_kernel, len(held)),
+        grid=(width // LANES,),
+        out_shape=(jax.ShapeDtypeStruct((tok, width), BF),) * 3,
+        in_specs=[tile(), tile(), tile(), tile(), stat(), col(), row()]
+        + [spec_any() for _ in held],
+        out_specs=(tile(), tile(), tile()),
+        input_output_aliases={7 + i: i for i in range(len(held))},
+        compiler_params=params(BIG),
+        cost_estimate=pl.CostEstimate(
+            flops=40 * seq * seq * width,
+            bytes_accessed=6 * MIB,
+            transcendentals=seq * seq * width // HEAD_DIM,
+        ),
+        name="attention_backward",
+    )(q, k, v, dctx, lse, seg_col, seg_row, *held)
+
+
+def input_grad_kernel(dq_ref, dk_ref, dv_ref, dpre_ref, masked_ref, *refs):
+    quad = refs[0:4]
+    dx_ref, small_ref, weights, sems = refs[4:]
+    width = dq_ref.shape[1]
+    step = pl.program_id(0)
+
+    @pl.when(step == 0)
+    def _():
+        for matrix in range(3):
+            rows = weights.at[matrix * width : (matrix + 1) * width]
+            load_att(quad, rows, sems.at[matrix], 8 * matrix, 8 * matrix + 8)
+        small_ref[...] = jnp.zeros_like(small_ref)
+
+    grad = dpre_ref[...]
+    for matrix in range(3):
+        rows = slice(matrix * width, (matrix + 1) * width)
+
+        @pl.when(step == 0)
+        def _():
+            wait_whole(weights.at[rows], sems.at[matrix])
+
+        grad = grad + dot_nt((dq_ref, dk_ref, dv_ref)[matrix][...], weights[rows])
+    chosen = masked_ref[...] == 1
+    dx_ref[...] = jnp.where(chosen, 0.0, grad)
+    small_ref[0:1] += column_sum(dq_ref[...].astype(F32))
+    small_ref[1:2] += column_sum(dv_ref[...].astype(F32))
+    small_ref[5:6] += column_sum(jnp.where(chosen, grad, 0.0))
+
+
+def input_grads(dq, dk, dv, dpre, masked_col, quad):
+    tok, width = dq.shape
+    rows = TILE
+    tile = lambda cols: pl.BlockSpec((rows, cols), lambda i: (i, 0))
+    whole = spec_whole((EXTRA, width))
+    return pl.pallas_call(
+        input_grad_kernel,
+        grid=(tok // rows,),
+        out_shape=(
+            jax.ShapeDtypeStruct((tok, width), F32),
+            jax.ShapeDtypeStruct((EXTRA, width), F32),
+        ),
+        in_specs=[tile(width)] * 4 + [tile(1)] + [spec_any()] * 4,
+        out_specs=(tile(width), whole),
+        scratch_shapes=[pltpu.VMEM((3 * width, width), BF), pltpu.SemaphoreType.DMA((3,))],
+        compiler_params=params(BIG),
+        cost_estimate=pl.CostEstimate(
+            flops=6 * tok * width * width, bytes_accessed=16 * MIB, transcendentals=0
+        ),
+        name="input_grads",
+    )(dq, dk, dv, dpre, masked_col, *quad)
+
+
+def att_grad_kernel(*refs):
+    sources, parts = refs[0:6], refs[6:10]
+    held, stage, load_sems, sems = refs[10:]
+    me = lax.axis_index("fsdp")
+    step = pl.program_id(0)
+    buf = lax.rem(step, 2)
+
+    @pl.when(step == 0)
+    def _():
+        for number in range(6):
+            pltpu.make_async_copy(sources[number], held.at[number], load_sems.at[number]).start()
+
+    wait_reuse(stage, sems, buf, step)
+    for matrix in range(4):
+
+        @pl.when(step == matrix)
+        def _():
+            for number in ((0, 1), (2, 3), (4,), (5,))[matrix]:
+                wait_whole(held.at[number], load_sems.at[number])
+            left = 0 if matrix == 0 else 2
+            right = 1 if matrix == 0 else 2 + matrix
+            stage[buf] = dot_tn(held[left], held[right]).astype(BF)
+
+    first = lax.rem(step + 3, 4) * 8
+    for piece in range(8):
+        far_core, slot = slot_of(first + piece, me)
+        src = stage.at[buf, piece * SLOT : (piece + 1) * SLOT]
+        send_slot(parts, far_core, slot, 0, src, sems.at[buf])
+    wait_last(stage, sems, step, 4)
+
+
+def att_grads(ctx, dob, stream, dq, dk, dv):
+    tok, width = stream.shape
+    return pl.pallas_call(
+        att_grad_kernel,
+        grid=(4,),
+        out_shape=part_shapes(width, False),
+        in_specs=[spec_any()] * 6,
+        out_specs=(spec_any(),) * 4,
+        scratch_shapes=[
+            pltpu.VMEM((6, tok, width), BF),
+            pltpu.VMEM((2, width, width), BF),
+            pltpu.SemaphoreType.DMA((6,)),
+            pltpu.SemaphoreType.DMA((2,)),
+        ],
+        compiler_params=params(BIG),
+        cost_estimate=pl.CostEstimate(
+            flops=8 * tok * width * width, bytes_accessed=16 * MIB, transcendentals=0
+        ),
+        name="att_grads",
+    )(ctx, dob, stream, dq, dk, dv)
+
+
+def flat_att_kernel(grad_ref, out_ref):
+    for part in range(6):
+        out_ref[pl.ds(part, SLOT, stride=6), :] = grad_ref[:, part * LANES : (part + 1) * LANES]
+
+
+def flat_ffn_kernel(a_ref, b_ref, out_ref):
+    first = lax.axis_index("fsdp") < 16
+
+    @pl.when(first)
+    def _():
+        for block in range(4):
+            source = a_ref if block < 2 else b_ref
+            rows = slice((block % 2) * 48, (block % 2) * 48 + 48)
+            for part in range(6):
+                cols = slice(part * LANES, (part + 1) * LANES)
+                out_ref[pl.ds(6 * block + part, 48, stride=24), :] = source[rows, cols]
+
+    @pl.when(jnp.logical_not(first))
+    def _():
+        for part in range(6):
+            cols = slice(part * LANES, (part + 1) * LANES)
+            out_ref[pl.ds(part, SLOT, stride=6), :] = a_ref[:, cols]
+            out_ref[pl.ds(6 * SLOT + part, SLOT, stride=6), :] = b_ref[:, cols]
+
+
+def flatten(kernel, rows, *pieces):
+    return pl.pallas_call(
+        kernel,
+        out_shape=jax.ShapeDtypeStruct((rows, LANES), F32),
+        in_specs=[spec_vmem()] * len(pieces),
+        out_specs=spec_vmem(),
+        compiler_params=params(16),
+        name="flatten",
+    )(*pieces)
+
+
+def update_kernel(last, small_at, rate, flat_ref, head_ref, small_ref, w_ref, m_ref, a_ref, w_out, m_out, a_out, low_out, buf):
+    me = lax.axis_index("fsdp")
+    aligned = flat_ref.shape[0]
+    own = w_ref.shape[0]
+    count = small_at[1]
+    buf[0:aligned, :] = flat_ref[...]
+    buf[aligned : aligned + 64, :] = head_ref[...]
+
+    @pl.when(me == last)
+    def _():
+        buf[aligned : aligned + 64, :] = jnp.zeros((64, LANES), F32)
+        for part in range(6):
+            cols = slice(part * LANES, (part + 1) * LANES)
+            buf[pl.ds(aligned + part, count, stride=6), :] = small_ref[
+                small_at[0] : small_at[0] + count, cols
+            ]
+
+    grad = buf[pl.ds(2 * me, own), :]
+    moment = 0.5 * m_ref[...] + grad
+    master = w_ref[...] - rate * (grad + 0.5 * moment)
+    m_out[...] = moment
+    w_out[...] = master
+    a_out[...] = 0.5 * a_ref[...] + 0.5 * master
+    low_out[...] = master.astype(BF)
+
+
+def update(flat, head, small, small_at, rate, devices, master, moment, average):
+    own = master.shape[0]
+    f32 = jax.ShapeDtypeStruct((own, LANES), F32)
+    body = functools.partial(update_kernel, devices - 1, small_at, rate)
+    return pl.pallas_call(
+        body,
+        out_shape=(f32, f32, f32, jax.ShapeDtypeStruct((own, LANES), BF)),
+        in_specs=[spec_vmem()] * 6,
+        out_specs=(spec_vmem(),) * 4,
+        scratch_shapes=[pltpu.VMEM((flat.shape[0] + 64, LANES), F32)],
+        compiler_params=params(16),
+        name="update",
+    )(flat, head, small, master, moment, average)
+
+
+def local_exchange(
+    block_input,
+    seg_ids,
+    masked,
+    out_grad,
+    att_master,
+    att_moment,
+    att_average,
+    ffn_master,
+    ffn_moment,
+    ffn_average,
+):
+    tok, width = block_input.shape
+    seq_count, seq = seg_ids.shape
+    devices = lax.axis_size("fsdp")
+    up = [(i, i + 1) for i in range(devices - 1)]
+    down = [(i + 1, i) for i in range(devices - 1)]
+    tails = lax.ppermute(jnp.concatenate([att_master[-64:], ffn_master[-64:]]), "fsdp", up)
+    masked_col = masked.reshape(tok, 1)
+    seg_col = seg_ids.reshape(tok, 1)
+    seg_row = seg_ids.reshape(seq_count, 1, seq)
+    att_chunk, small_chunk, chunk_a, chunk_b = prepare(att_master, ffn_master, tails, devices, width)
+    att = jnp.concatenate([att_chunk, small_chunk])
+    got, masked_col, seg_col, seg_row = phase(exchange(att, 0), masked_col, seg_col, seg_row)
+    att = widen_small(att, got)
+    got = exchange(att, 1)
+    att, unit_a = phase(widen_small(att, got), chunk_a)
+    got, got_a = phase(exchange(att, 2), exchange(unit_a, 0))
+    att, unit_a, unit_b = phase(widen_small(att, got), widen(unit_a, got_a), chunk_b)
+    att_next, att_far, got_a, got_b = phase(
+        exchange(att, 3), exchange(att, 4), exchange(unit_a, 1), exchange(unit_b, 0)
+    )
+    unit_a, unit_b, att_next = phase(widen(unit_a, got_a), widen(unit_b, got_b), att_next)
+    att_last, got_b, block_input = phase(exchange(att_next, 4), exchange(unit_b, 2), block_input)
+    att = (att, att_next, att_far, att_last)
+    unit_a, unit_b, block_input = phase(unit_a, widen(unit_b, got_b), block_input)
+    got_b = exchange(unit_b, 1)
+    stream, q, k, v, small = project(block_input, masked_col, att)
+    got_a, q = phase(exchange(unit_a, 2), q)
+    unit_a, q = phase(widen(unit_a, got_a), q)
+    held = attention_forward(0, q, k, v, seg_col, seg_row)
+    a_next, a_far, got_b, held = phase(exchange(unit_a, 3), exchange(unit_a, 4), got_b, held)
+    unit_b, a_next, held = phase(widen(unit_b, got_b), a_next, held)
+    ctx, lse = attention_forward(1, q, k, v, seg_col, seg_row, held)
+    b_next, b_far, a_last, ctx = phase(
+        exchange(unit_b, 3), exchange(unit_b, 4), exchange(a_next, 4), ctx
+    )
+    b_last = exchange(b_next, 4)
+    block_output, x_low, hidden, dhid, dfb, dpre, dob, dctx, sums = feed_forward(
+        stream,
+        ctx,
+        out_grad,
+        small,
+        att,
+        (unit_a, a_next, a_far, a_last),
+        (unit_b, b_next, b_far, b_last),
+    )
+    part_a, part_b = ffn_grads(x_low, hidden, dhid, dfb, sums)
+    part_b, dhid = phase(part_b, dhid)
+    part_a = ffn_rest(x_low, dhid, part_a)
+    high_b, low_b, part_a = phase(exchange(part_b[3], 4), exchange(part_b[2], 4), part_a)
+    small_sum = sums + high_b[8 * SLOT :].astype(F32)
+    high_b = add_small(total_of((part_b[1], high_b), 0, 8 * SLOT).astype(BF), small_sum)
+    high_b, part_a, dctx = phase(high_b, part_a, dctx)
+    held = attention_backward(0, q, k, v, dctx, lse, seg_col, seg_row)
+    got_b, high_a, low_a, held = phase(
+        exchange(high_b, 3), exchange(part_a[3], 4), exchange(part_a[2], 4), held
+    )
+    high_a = total_of((part_a[1], high_a), 0, 8 * SLOT).astype(BF)
+    small_sum = small_sum + got_b[8 * SLOT :].astype(F32)
+    kept_b, sent_b = halve(part_b[0], low_b, got_b[: 8 * SLOT])
+    high_a, sent_b, held = phase(high_a, add_small(sent_b, small_sum), held)
+    dq, dk, dv = attention_backward(1, q, k, v, dctx, lse, seg_col, seg_row, held)
+    got_a, got_b, dq = phase(exchange(high_a, 3), exchange(sent_b, 1), dq)
+    kept_a, sent_a = halve(part_a[0], low_a, got_a)
+    small_sum = small_sum + got_b[4 * SLOT :].astype(F32)
+    kept_b, sent_b = halve(kept_b, got_b[: 4 * SLOT])
+    sent_a, sent_b, dq = phase(sent_a, add_small(sent_b, small_sum), dq)
+    part = att_grads(ctx, dob, stream, dq, dk, dv)
+    got_a, got_b, part = phase(exchange(sent_a, 2), exchange(sent_b, 2), part)
+    kept_a, sent_a = halve(kept_a, got_a)
+    small_sum = small_sum + got_b[2 * SLOT :].astype(F32)
+    kept_b, sent_b = halve(kept_b, got_b[: 2 * SLOT])
+    sent_a, sent_b, part = phase(sent_a, add_small(sent_b, small_sum), part)
+    got_b = exchange(sent_b, 0)
+    high = exchange(part[3], 4)
+    high = total_of((part[1], high), 0, 8 * SLOT).astype(BF)
+    high, sent_a, dq = phase(high, sent_a, dq)
+    input_grad, late = input_grads(dq, dk, dv, dpre, masked_col, att)
+    got, low, got_a, got_b, late = phase(
+        exchange(high, 3), exchange(part[2], 4), exchange(sent_a, 1), got_b, late
+    )
+    kept, sent = halve(part[0], low, got)
+    kept_a, sent_a = halve(kept_a, got_a)
+    sent, sent_a, late = phase(sent, sent_a, late)
+    got, got_a, got_late = phase(exchange(sent, 2), exchange(sent_a, 0), exchange(late.astype(BF), 4))
+    kept, sent = halve(kept, got)
+    late = late + got_late.astype(F32)
+    sent, late, got_a = phase(sent, late, got_a)
+    got = exchange(sent, 1)
+    late = late + exchange(late.astype(BF), 2).astype(F32)
+    late = late + exchange(late.astype(BF), 3).astype(F32)
+    small_sum = small_sum + got_b[SLOT:].astype(F32)
+    grad_a = total_of((kept_a, got_a), 0, SLOT)
+    grad_b = total_of((kept_b, got_b), 0, SLOT)
+    ffn_flat = flatten(flat_ffn_kernel, 12 * SLOT, grad_a, grad_b)
+    kept, sent = halve(kept, got)
+    sent, late, ffn_flat, small_sum = phase(sent, late, ffn_flat, small_sum)
+    got = exchange(sent, 0)
+    late = late + exchange(late.astype(BF), 1).astype(F32)
+    ffn_head = lax.ppermute(ffn_flat[:64], "fsdp", down)
+    got, late, ffn_head = phase(got, late, ffn_head)
+    grad_att = total_of((kept, got), 0, SLOT)
+    att_flat = flatten(flat_att_kernel, 6 * SLOT, grad_att)
+    att_head = lax.ppermute(att_flat[:64], "fsdp", down)
+    late = late + exchange(late.astype(BF), 0).astype(F32)
+    rate = 0.05 / math.sqrt(tok * devices)
+    ffn_new = update(
+        ffn_flat, ffn_head, small_sum, (6, 7), rate, devices, ffn_master, ffn_moment, ffn_average
+    )
+    att_head, late, ffn_new = phase(att_head, late, ffn_new)
+    small_total = small_sum + late
+    att_new = update(
+        att_flat, att_head, small_total, (0, 6), rate, devices, att_master, att_moment, att_average
+    )
+    return (block_output, input_grad) + tuple(att_new) + tuple(ffn_new)
+
+
+def chunked(mesh):
+    return mesh.shape["fsdp"] == 32
+
+
 def solution(mesh):
     in_specs = (
         P("fsdp", None),
@@ -263,4 +1250,5 @@
         P("fsdp", None),
         P("fsdp", None),
     )
-    return jax.shard_map(local, mesh=mesh, in_specs=in_specs, out_specs=out_specs, check_vma=False)
+    body = local_exchange if chunked(mesh) else local
+    return jax.shard_map(body, mesh=mesh, in_specs=in_specs, out_specs=out_specs, check_vma=False)

time: 828 us -> 294 us (0.36); the launches traced: 813 us -> 293 us
  blocking collectives: 306 us -> 0 us
  local copies, waits for them, and re-layouts: 210 us -> 11.1 us
  matrix products: 168 us -> 0 us
  Pallas kernels: 0 us -> 141 us
  starting transfers between devices: 5.12 us -> 50.1 us
  other arithmetic: 44.2 us -> 11.2 us
  waiting for transfers between devices: 63.1 us -> 78 us
  between operations: 15.3 us -> 1.44 us
    unnamed x1 -> x0, blocking collectives: 306 us -> none
    dot_general x26 -> x0, matrix products: 168 us -> none  [the longest x1 37.3 us: local(): jnp.dot(normed_low, weight_in, preferred_element_type=jnp.float32) + bias_in]
    pallas_call x0 -> x15, Pallas kernels: none -> 141 us  [the longest x1 38.9 us: feed_forward(): pl.pallas_call(ffn_kernel, grid=(tok // TILE,), out_shape=(bf(width), bf(...]
    ppermute x0 -> x44, waiting for transfers between devices: none -> 78 us  [the longest x41 71.2 us: exchange(): return lax.ppermute(array, 'fsdp', stage_perm(stage))]
    unnamed x158 -> x68, local copies, waits for them, and re-layouts: 79.1 us -> 6.77 us
    all_gather x2 -> x0, waiting for transfers between devices: 61 us -> none  [the longest x1 61 us: local(): lax.all_gather(att_master.astype(jnp.bfloat16), 'fsdp', axis=0, tiled=True)]
    ppermute x0 -> x44, starting transfers between devices: none -> 50.1 us  [the longest x41 39.4 us: exchange(): return lax.ppermute(array, 'fsdp', stage_perm(stage))]
    reshape x6 -> x1, local copies, waits for them, and re-layouts: 40.2 us -> 0.6 us  [local_exchange(): seg_row = seg_ids.reshape(seq_count, 1, seq)]
  transfers between devices with their start and end apart: 4 -> 44, of which waited for: 2 -> 21; matrix products, arithmetic and copies ran while one was open for 12% -> 1% of each run, Pallas kernels for 0% -> 30%
where the time goes in v2:
time: 294 us; the launch traced here: 293 us
  Pallas kernels  141 us (48%)
  waiting for transfers between devices  78 us (27%)
  starting transfers between devices  50.1 us (17%)
  other arithmetic  11.2 us (4%)
  local copies, waits for them, and re-layouts  11.1 us (4%)
    ppermute x41, waiting for transfers between devices, exchange(): return lax.ppermute(array, 'fsdp', stage_perm(stage))  71.2 us
    ppermute x41, starting transfers between devices, exchange(): return lax.ppermute(array, 'fsdp', stage_perm(stage))  39.4 us
    pallas_call x1, Pallas kernels, feed_forward(): pl.pallas_call(ffn_kernel, grid=(tok // TILE,), out_shape=(bf(width), bf(...  38.9 us
    pallas_call x2, Pallas kernels, attention_backward(): pl.pallas_call(functools.partial(backward_kernel, len(held)), grid=(width...  29.3 us
    pallas_call x2, Pallas kernels, attention_forward(): pl.pallas_call(functools.partial(forward_kernel, len(held)), grid=(pairs,...  20.7 us
    pallas_call x1, Pallas kernels, ffn_grads(): pl.pallas_call(ffn_grad_kernel, grid=(6,), out_shape=part_shapes(width, F...  13.7 us
    pallas_call x1, Pallas kernels, input_grads(): pl.pallas_call(input_grad_kernel, grid=(tok // rows,), out_shape=(jax.Sha...  11.4 us
    pallas_call x1, Pallas kernels, project(): pl.pallas_call(project_kernel, grid=(tok // rows,), out_shape=(bf, bf, bf...  9.2 us
  transfers between devices with their start and end apart: 44, of which 21 were waited for; matrix products, arithmetic and copies ran while one was open for 1% of the time, Pallas kernels for 30%

profile of v2, /device:TPU:7, one launch (start us, length us, event | category | flops | bytes accessed | tf_op | source)
XLA Modules:
  0.0 293.3 jit_solution(2422496537930245071)
XLA Ops:
  2.2 3.7 %collective-permute-start = (f32[128,128]{1,0:T(8,128)S(1)}, f32[128,128]{1,0:T(8,128)S(1)}, u32[]{:S(2)}, u32[]{:S(2)}) collective-permute-start(f32[128,128]{1,0:T(8,128)S(1)} %pad_maximum_fusion.14), channel_id=1, source_target_pairs={{0,1},{1,2},{2,3},{3,4},{4,5},{5,6},{6,7},{7,8},{8,9},{9,10},{10,1... | collective-permute-start | bytes 196616 | tf_op jit(solution)/shard_map/ppermute | solution.py:1113
  5.9 1.3 collective-permute-done.tail_ref
  7.2 1.1 copy-done
  8.3 1.0 copy-done.2
  9.5 2.3 collective-permute-start.1
  12.4 7.0 %collective-permute-done.1 = bf16[112,768]{1,0:T(8,128)(2,1)S(1)} collective-permute-done((bf16[112,768]{1,0:T(8,128)(2,1)S(1)}, bf16[112,768]{1,0:T(8,128)(2,1)S(1)}, u32[]{:S(2)}, u32[]{:S(2)}) %collective-permute-start.1) | collective-permute-done | bytes 172064 | tf_op jit(solution)/shard_map/ppermute | solution.py:310
  19.5 7.4 %collective-permute-done.2 = bf16[208,768]{1,0:T(8,128)(2,1)S(1)} collective-permute-done((bf16[208,768]{1,0:T(8,128)(2,1)S(1)}, bf16[208,768]{1,0:T(8,128)(2,1)S(1)}, u32[]{:S(2)}, u32[]{:S(2)}) %collective-permute-start.2) | collective-permute-done | bytes 319520 | tf_op jit(solution)/shard_map/ppermute | solution.py:310
  27.7 4.2 %collective-permute-start.4 = (bf16[96,768]{1,0:T(8,128)(2,1)S(1)}, bf16[96,768]{1,0:T(8,128)(2,1)S(1)}, u32[]{:S(2)}, u32[]{:S(2)}) collective-permute-start(bf16[96,768]{1,0:T(8,128)(2,1)S(1)} %get-tuple-element.186), channel_id=1, source_target_pairs={{0,16},{1,17},{2,18},{3,19},{4,20},{5,21},{6,22},{7,23},{8,24},{9,... | collective-permute-start | bytes 442376 | tf_op jit(solution)/shard_map/ppermute | solution.py:310
  31.9 6.5 %collective-permute-done.4 = bf16[96,768]{1,0:T(8,128)(2,1)S(1)} collective-permute-done((bf16[96,768]{1,0:T(8,128)(2,1)S(1)}, bf16[96,768]{1,0:T(8,128)(2,1)S(1)}, u32[]{:S(2)}, u32[]{:S(2)}) %collective-permute-start.4) | collective-permute-done | bytes 147488 | tf_op jit(solution)/shard_map/ppermute | solution.py:310
  38.6 1.4 collective-permute-start.6
  40.8 3.1 %collective-permute-start.8 = (bf16[96,768]{1,0:T(8,128)(2,1)S(1)}, bf16[96,768]{1,0:T(8,128)(2,1)S(1)}, u32[]{:S(2)}, u32[]{:S(2)}) collective-permute-start(bf16[96,768]{1,0:T(8,128)(2,1)S(1)} %get-tuple-element.192), channel_id=1, source_target_pairs={{0,16},{1,17},{2,18},{3,19},{4,20},{5,21},{6,22},{7,23},{8,24},{9,... | collective-permute-start | bytes 442376 | tf_op jit(solution)/shard_map/ppermute | solution.py:310
  43.9 5.2 %collective-permute-done.8 = bf16[96,768]{1,0:T(8,128)(2,1)S(1)} collective-permute-done((bf16[96,768]{1,0:T(8,128)(2,1)S(1)}, bf16[96,768]{1,0:T(8,128)(2,1)S(1)}, u32[]{:S(2)}, u32[]{:S(2)}) %collective-permute-start.8) | collective-permute-done | bytes 147488 | tf_op jit(solution)/shard_map/ppermute | solution.py:310
  49.1 2.6 collective-permute-done.7
  51.7 4.0 %collective-permute-done.5.refs_1_ = bf16[784,768]{1,0:T(8,128)(2,1)S(1)} collective-permute-done((bf16[784,768]{1,0:T(8,128)(2,1)S(1)}, bf16[784,768]{1,0:T(8,128)(2,1)S(1)}, u32[]{:S(2)}, u32[]{:S(2)}) %collective-permute-start.5) | collective-permute-done | bytes 1204256 | tf_op jit(solution)/shard_map/ppermute | solution.py:310
  55.7 1.0 collective-permute-start.9
  56.9 5.7 %collective-permute-done.10 = bf16[192,768]{1,0:T(8,128)(2,1)S(1)} collective-permute-done((bf16[192,768]{1,0:T(8,128)(2,1)S(1)}, bf16[192,768]{1,0:T(8,128)(2,1)S(1)}, u32[]{:S(2)}, u32[]{:S(2)}) %collective-permute-start.10) | collective-permute-done | bytes 294944 | tf_op jit(solution)/shard_map/ppermute | solution.py:310
  62.7 1.0 copy-done.27
  63.8 1.0 copy.29.masked_ref
  64.8 9.2 %project.1 = (bf16[1024,768]{1,0:T(8,128)(2,1)}, bf16[1024,768]{1,0:T(8,128)(2,1)}, bf16[1024,768]{1,0:T(8,128)(2,1)}, bf16[1024,768]{1,0:T(8,128)(2,1)}, f32[16,768]{1,0:T(8,128)}) custom-call(bf16[1024,768]{1,0:T(8,128)(2,1)} %x_ref, s32[1024,1]{1,0:T(8,128)} %copy.29.masked_ref, bf16[784,768]{1,0:T(8,128)(2,1)} %copy-done.10, ...), custom_call_target="tpu_custom_call" | custom-call | flops 3623878656 | bytes 16777216 | tf_op jit(solution)/shard_map/project/pallas_call | solution.py:517
  74.2 1.3 collective-permute-start.13
  75.5 1.3 collective-permute-start.12
  77.1 1.0 copy.30.seg_col_ref
  78.1 10.3 %attention_forward.2 = (bf16[1024,768]{1,0:T(8,128)(2,1)}, f32[2,6,2,512]{3,2,1,0:T(2,128)}) custom-call(bf16[1024,768]{1,0:T(8,128)(2,1)} %get-tuple-element.212.q_ref, bf16[1024,768]{1,0:T(8,128)(2,1)} %get-tuple-element.213.k_ref, bf16[1024,768]{1,0:T(8,128)(2,1)} %get-tuple-element.214.v_ref, s32[1024,1]{1,0:T(8,128)} %copy.30.seg_col_ref, ...), custom_call_target="tpu_custom_call" | custom-call | flops 3221225472 | bytes 4194304 | tf_op jit(solution)/shard_map/attention_forward/pallas_call | solution.py:571
  88.5 3.6 %collective-permute-done.14 = bf16[384,768]{1,0:T(8,128)(2,1)S(1)} collective-permute-done((bf16[384,768]{1,0:T(8,128)(2,1)S(1)}, bf16[384,768]{1,0:T(8,128)(2,1)S(1)}, u32[]{:S(2)}, u32[]{:S(2)}) %collective-permute-start.14) | collective-permute-done | bytes 589856 | tf_op jit(solution)/shard_map/ppermute | solution.py:310
  93.3 10.4 %attention_forward.3 = (bf16[1024,768]{1,0:T(8,128)(2,1)}, f32[2,6,2,512]{3,2,1,0:T(2,128)}) custom-call(bf16[1024,768]{1,0:T(8,128)(2,1)} %get-tuple-element.212.q_ref, bf16[1024,768]{1,0:T(8,128)(2,1)} %get-tuple-element.213.k_ref, bf16[1024,768]{1,0:T(8,128)(2,1)} %get-tuple-element.214.v_ref, ...), custom_call_target="tpu_custom_call", output_to_operand_aliasing={{0}: (5, {}), {1}: (6, {})} | custom-call | flops 3221225472 | bytes 4194304 | tf_op jit(solution)/shard_map/attention_forward/pallas_call | solution.py:571
  103.8 4.3 %collective-permute-done.15.refs_9_ = bf16[768,768]{1,0:T(8,128)(2,1)S(1)} collective-permute-done((bf16[768,768]{1,0:T(8,128)(2,1)S(1)}, bf16[768,768]{1,0:T(8,128)(2,1)S(1)}, u32[]{:S(2)}, u32[]{:S(2)}) %collective-permute-start.15) | collective-permute-done | bytes 1179680 | tf_op jit(solution)/shard_map/ppermute | solution.py:310
  108.1 1.3 collective-permute-start.18
  109.3 2.5 collective-permute-done.18.refs_11_
  111.8 1.1 copy-done.32
  112.9 38.9 %feed_forward.1 = (bf16[1024,768]{1,0:T(8,128)(2,1)}, bf16[1024,768]{1,0:T(8,128)(2,1)}, bf16[1024,3072]{1,0:T(8,128)(2,1)}, bf16[1024,3072]{1,0:T(8,128)(2,1)},...) custom-call(bf16[1024,768]{1,0:T(8,128)(2,1)} %get-tuple-element.205, ...), custom_call_target="tpu_custom_call" | custom-call | flops 19327352832 | bytes 41943040 | tf_op jit(solution)/shard_map/feed_forward/pallas_call | solution.py:689
  151.8 13.7 %ffn_grads.1 = (bf16[768,768]{1,0:T(8,128)(2,1)}, bf16[768,768]{1,0:T(8,128)(2,1)}, bf16[768,768]{1,0:T(8,128)(2,1)}, bf16[768,768]{1,0:T(8,128)(2,1)}, bf16[768...) custom-call(bf16[1024,768]{1,0:T(8,128)(2,1)} %get-tuple-element.235.x_ref, ...), custom_call_target="tpu_custom_call" | custom-call | flops 7247757312 | bytes 25165824 | tf_op jit(solution)/shard_map/ffn_grads/pallas_call | solution.py:804
  166.0 6.1 %ffn_rest.1 = (bf16[768,768]{1,0:T(8,128)(2,1)}, bf16[768,768]{1,0:T(8,128)(2,1)}, bf16[768,768]{1,0:T(8,128)(2,1)}, bf16[768,768]{1,0:T(8,128)(2,1)}) custom-call(bf16[1024,768]{1,0:T(8,128)(2,1)} %get-tuple-element.235.x_ref, ...), custom_call_target="tpu_custom_call", output_to_operand_aliasing={{0}: (2, {}), {1}: (3, {}), {2}: (4, {}), {3}: (5, {})} | custom-call | flops 2415919104 | bytes 8388608 | tf_op jit(solution)/shard_map/ffn_rest/pallas_call | solution.py:843
  172.2 1.1 copy-done.18
  175.6 14.6 %attention_backward.2 = (bf16[1024,768]{1,0:T(8,128)(2,1)}, bf16[1024,768]{1,0:T(8,128)(2,1)}, bf16[1024,768]{1,0:T(8,128)(2,1)}) custom-call(bf16[1024,768]{1,0:T(8,128)(2,1)} %get-tuple-element.212.q_ref, bf16[1024,768]{1,0:T(8,128)(2,1)} %get-tuple-element.213.k_ref, bf16[1024,768]{1,0:T(8,128)(2,1)} %get-tuple-element.214.v_ref, ...), custom_call_target="tpu_custom_call" | custom-call | flops 8053063680 | bytes 6291456 | tf_op jit(solution)/shard_map/attention_backward/pallas_call | solution.py:896
  190.3 2.2 add_convert_fusion.5
  192.5 1.6 add_convert_fusion.1
  195.3 14.7 %attention_backward.3 = (bf16[1024,768]{1,0:T(8,128)(2,1)}, bf16[1024,768]{1,0:T(8,128)(2,1)}, bf16[1024,768]{1,0:T(8,128)(2,1)}) custom-call(bf16[1024,768]{1,0:T(8,128)(2,1)} %get-tuple-element.212.q_ref, bf16[1024,768]{1,0:T(8,128)(2,1)} %get-tuple-element.213.k_ref, ...), custom_call_target="tpu_custom_call", output_to_operand_aliasing={{0}: (7, {}), {1}: (8, {}), {2}: (9, {})} | custom-call | flops 8053063680 | bytes 6291456 | tf_op jit(solution)/shard_map/attention_backward/pallas_call | solution.py:896
  210.2 1.1 copy-done.9
  211.3 1.7 add_convert_fusion.6
  213.0 1.2 collective-permute-start.26
  214.5 9.2 %att_grads.1 = (bf16[768,768]{1,0:T(8,128)(2,1)}, bf16[768,768]{1,0:T(8,128)(2,1)}, bf16[768,768]{1,0:T(8,128)(2,1)}, bf16[768,768]{1,0:T(8,128)(2,1)}) custom-call(bf16[1024,768]{1,0:T(8,128)(2,1)} %get-tuple-element.228.ctx_ref.refs_0_, bf16[1024,768]{1,0:T(8,128)(2,1)} %get-tuple-element.291.refs_1_, ...), custom_call_target="tpu_custom_call" | custom-call | flops 4831838208 | bytes 16777216 | tf_op jit(solution)/shard_map/att_grads/pallas_call | solution.py:999
  223.7 1.8 collective-permute-done.27
  227.2 2.2 collective-permute-start.28
  229.4 3.4 %collective-permute-done.28 = bf16[768,768]{1,0:T(8,128)(2,1)S(1)} collective-permute-done((bf16[768,768]{1,0:T(8,128)(2,1)S(1)}, bf16[768,768]{1,0:T(8,128)(2,1)S(1)}, u32[]{:S(2)}, u32[]{:S(2)}) %collective-permute-start.28) | collective-permute-done | bytes 1179680 | tf_op jit(solution)/shard_map/ppermute | solution.py:310
  233.8 3.0 %collective-permute-start.32 = (bf16[112,768]{1,0:T(8,128)(2,1)}, bf16[112,768]{1,0:T(8,128)(2,1)S(1)}, u32[]{:S(2)}, u32[]{:S(2)}) collective-permute-start(bf16[112,768]{1,0:T(8,128)(2,1)} %pad_maximum_fusion.13), channel_id=1, source_target_pairs={{0,16},{1,17},{2,18},{3,19},{4,20},{5,21},{6,22},{7,23},{8,24},{9,... | collective-permute-start | bytes 516104 | tf_op jit(solution)/shard_map/ppermute | solution.py:310
  237.3 11.4 %input_grads.1 = (f32[1024,768]{1,0:T(8,128)}, f32[16,768]{1,0:T(8,128)}) custom-call(bf16[1024,768]{1,0:T(8,128)(2,1)} %get-tuple-element.308.refs_3_.dq_ref, bf16[1024,768]{1,0:T(8,128)(2,1)} %get-tuple-element.293.refs_4_.dk_ref, bf16[1024,768]{1,0:T(8,128)(2,1)} %get-tuple-element.294.refs_5_.dv_ref, f32[1024,768]{1,0:T(8,128)} %get-tuple-element.309.dpre_ref, ...), custom_call_target="tpu_custom_call" | custom-call | flops 3623878656 | bytes 16777216 | tf_op jit(solution)/shard_map/input_grads/pallas_call | solution.py:948
  248.8 0.9 add_convert_fusion.19
  250.2 1.1 collective-permute-start.33
  251.3 2.2 collective-permute-start.34
  253.5 2.0 collective-permute-start.35
  256.3 4.4 %collective-permute-done.34 = bf16[96,768]{1,0:T(8,128)(2,1)S(1)} collective-permute-done((bf16[96,768]{1,0:T(8,128)(2,1)S(1)}, bf16[96,768]{1,0:T(8,128)(2,1)S(1)}, u32[]{:S(2)}, u32[]{:S(2)}) %collective-permute-start.34) | collective-permute-done | bytes 147488 | tf_op jit(solution)/shard_map/ppermute | solution.py:310
  260.9 0.9 collective-permute-start.37
  261.9 1.7 collective-permute-done.37
  264.1 1.0 convert_add_fusion.1
  265.3 1.4 collective-permute-done.38
  266.7 2.6 collective-permute-done.36
  269.4 4.2 %collective-permute-start.41 = (f32[64,128]{1,0:T(8,128)S(1)}, f32[64,128]{1,0:T(8,128)S(1)}, u32[]{:S(2)}, u32[]{:S(2)}) collective-permute-start(f32[64,128]{1,0:T(8,128)S(1)} %slice.253), channel_id=1, source_target_pairs={{1,0},{2,1},{3,2},{4,3},{5,4},{6,5},{7,6},{8,7},{9,8},{10,9},{11,1... | collective-permute-start | bytes 98312 | tf_op jit(solution)/shard_map/ppermute | solution.py:1206
  273.7 2.3 collective-permute-start.39
  275.9 1.1 collective-permute-done.41.head_ref
  277.0 6.2 %collective-permute-done.39 = bf16[96,768]{1,0:T(8,128)(2,1)S(1)} collective-permute-done((bf16[96,768]{1,0:T(8,128)(2,1)S(1)}, bf16[96,768]{1,0:T(8,128)(2,1)S(1)}, u32[]{:S(2)}, u32[]{:S(2)}) %collective-permute-start.39) | collective-permute-done | bytes 147488 | tf_op jit(solution)/shard_map/ppermute | solution.py:310
  283.4 2.8 collective-permute-start.42
  286.3 1.5 update.2
  287.7 4.5 %collective-permute-done.42.head_ref = f32[64,128]{1,0:T(8,128)S(1)} collective-permute-done((f32[64,128]{1,0:T(8,128)S(1)}, f32[64,128]{1,0:T(8,128)S(1)}, u32[]{:S(2)}, u32[]{:S(2)}) %collective-permute-start.42) | collective-permute-done | bytes 32800 | tf_op jit(solution)/shard_map/ppermute | solution.py:1210
  292.2 1.1 update.3
  (165 shorter events, 16.7 us)
Async XLA Ops:
  0.6 11.2 %copy-start.24 = (s32[2,512]{1,0:T(2,128)S(1)}, s32[2,512]{1,0:T(2,128)}, u32[]{:S(2)}) copy-start(s32[2,512]{1,0:T(2,128)} %param.12) | copy-start | bytes 12292
  0.7 11.2 %copy-start.23 = (s32[2,512]{1,0:T(2,128)S(1)}, s32[2,512]{1,0:T(2,128)}, u32[]{:S(2)}) copy-start(s32[2,512]{1,0:T(2,128)} %param.11) | copy-start | bytes 12292
  2.2 5.0 %collective-permute-start = (f32[128,128]{1,0:T(8,128)S(1)}, f32[128,128]{1,0:T(8,128)S(1)}, u32[]{:S(2)}, u32[]{:S(2)}) collective-permute-start(f32[128,128]{1,0:T(8,128)S(1)} %pad_maximum_fusion.14), channel_id=1, source_target_pairs={{0,1},{1,2},{2,3},{3,4},{4,5},{5,6},{6,7},{7,8},{8,9},{9,10},{10,1... | collective-permute-start | bytes 196616 | tf_op jit(solution)/shard_map/ppermute | solution.py:1113
  9.5 9.9 %collective-permute-start.1 = (bf16[112,768]{1,0:T(8,128)(2,1)S(1)}, bf16[112,768]{1,0:T(8,128)(2,1)S(1)}, u32[]{:S(2)}, u32[]{:S(2)}) collective-permute-start(bf16[112,768]{1,0:T(8,128)(2,1)S(1)} %pad_maximum_fusion.12), channel_id=1, source_target_pairs={{0,16},{1,17},{2,18},{3,19},{4,20},{5,21},{6,22},{7,23},{8,24},{9,... | collective-permute-start | bytes 516104 | tf_op jit(solution)/shard_map/ppermute | solution.py:310
  19.5 7.5 %collective-permute-start.2 = (bf16[208,768]{1,0:T(8,128)(2,1)S(1)}, bf16[208,768]{1,0:T(8,128)(2,1)S(1)}, u32[]{:S(2)}, u32[]{:S(2)}) collective-permute-start(bf16[208,768]{1,0:T(8,128)(2,1)S(1)} %pad_maximum_fusion.8), channel_id=1, source_target_pairs={{0,8},{1,9},{2,10},{3,11},{4,12},{5,13},{6,14},{7,15},{8,0},{9,1},... | collective-permute-start | bytes 958472 | tf_op jit(solution)/shard_map/ppermute | solution.py:310
  27.1 11.4 %collective-permute-start.3 = (bf16[400,768]{1,0:T(8,128)(2,1)S(1)}, bf16[400,768]{1,0:T(8,128)(2,1)S(1)}, u32[]{:S(2)}, u32[]{:S(2)}) collective-permute-start(bf16[400,768]{1,0:T(8,128)(2,1)S(1)} %pad_maximum_fusion.4), channel_id=1, source_target_pairs={{0,2},{1,5},{2,0},{3,7},{4,6},{5,1},{6,4},{7,3},{8,10},{9,13},{10,... | collective-permute-start | bytes 1843208 | tf_op jit(solution)/shard_map/ppermute | solution.py:310
  27.7 10.7 %collective-permute-start.4 = (bf16[96,768]{1,0:T(8,128)(2,1)S(1)}, bf16[96,768]{1,0:T(8,128)(2,1)S(1)}, u32[]{:S(2)}, u32[]{:S(2)}) collective-permute-start(bf16[96,768]{1,0:T(8,128)(2,1)S(1)} %get-tuple-element.186), channel_id=1, source_target_pairs={{0,16},{1,17},{2,18},{3,19},{4,20},{5,21},{6,22},{7,23},{8,24},{9,... | collective-permute-start | bytes 442376 | tf_op jit(solution)/shard_map/ppermute | solution.py:310
  38.6 24.1 %copy-start.10 = (bf16[784,768]{1,0:T(8,128)(2,1)}, bf16[784,768]{1,0:T(8,128)(2,1)S(1)}, u32[]{:S(2)}) copy-start(bf16[784,768]{1,0:T(8,128)(2,1)S(1)} %pad_maximum_fusion.refs_0_) | copy-start | bytes 3612676
  38.6 13.1 %collective-permute-start.6 = (bf16[784,768]{1,0:T(8,128)(2,1)S(1)}, bf16[784,768]{1,0:T(8,128)(2,1)S(1)}, u32[]{:S(2)}, u32[]{:S(2)}) collective-permute-start(bf16[784,768]{1,0:T(8,128)(2,1)S(1)} %pad_maximum_fusion.refs_0_), channel_id=1, source_target_pairs={{0,1},{1,0},{2,3},{3,2},{4,5},{5,4},{6,7},{7,6},{8,9},{9,8},{10,11... | collective-permute-start | bytes 3612680 | tf_op jit(solution)/shard_map/ppermute | solution.py:310
  40.0 15.6 %collective-permute-start.5 = (bf16[784,768]{1,0:T(8,128)(2,1)S(1)}, bf16[784,768]{1,0:T(8,128)(2,1)S(1)}, u32[]{:S(2)}, u32[]{:S(2)}) collective-permute-start(bf16[784,768]{1,0:T(8,128)(2,1)S(1)} %pad_maximum_fusion.refs_0_), channel_id=1, source_target_pairs={{0,4},{1,3},{2,6},{3,1},{4,0},{5,7},{6,2},{7,5},{8,12},{9,11},{10,... | collective-permute-start | bytes 3612680 | tf_op jit(solution)/shard_map/ppermute | solution.py:310
  40.3 11.4 %collective-permute-start.7 = (bf16[192,768]{1,0:T(8,128)(2,1)S(1)}, bf16[192,768]{1,0:T(8,128)(2,1)S(1)}, u32[]{:S(2)}, u32[]{:S(2)}) collective-permute-start(bf16[192,768]{1,0:T(8,128)(2,1)S(1)} %pad_maximum_fusion.10), channel_id=1, source_target_pairs={{0,8},{1,9},{2,10},{3,11},{4,12},{5,13},{6,14},{7,15},{8,0},{9,1},... | collective-permute-start | bytes 884744 | tf_op jit(solution)/shard_map/ppermute | solution.py:310
  40.8 8.3 %collective-permute-start.8 = (bf16[96,768]{1,0:T(8,128)(2,1)S(1)}, bf16[96,768]{1,0:T(8,128)(2,1)S(1)}, u32[]{:S(2)}, u32[]{:S(2)}) collective-permute-start(bf16[96,768]{1,0:T(8,128)(2,1)S(1)} %get-tuple-element.192), channel_id=1, source_target_pairs={{0,16},{1,17},{2,18},{3,19},{4,20},{5,21},{6,22},{7,23},{8,24},{9,... | collective-permute-start | bytes 442376 | tf_op jit(solution)/shard_map/ppermute | solution.py:310
  51.7 10.9 %copy-start.25 = (bf16[784,768]{1,0:T(8,128)(2,1)}, bf16[784,768]{1,0:T(8,128)(2,1)S(1)}, u32[]{:S(2)}) copy-start(bf16[784,768]{1,0:T(8,128)(2,1)S(1)} %collective-permute-done.6.refs_2_) | copy-start | bytes 3612676
  55.7 7.0 %copy-start.26 = (bf16[784,768]{1,0:T(8,128)(2,1)}, bf16[784,768]{1,0:T(8,128)(2,1)S(1)}, u32[]{:S(2)}) copy-start(bf16[784,768]{1,0:T(8,128)(2,1)S(1)} %collective-permute-done.5.refs_1_) | copy-start | bytes 3612676
  55.7 6.9 %collective-permute-start.9 = (bf16[784,768]{1,0:T(8,128)(2,1)S(1)}, bf16[784,768]{1,0:T(8,128)(2,1)S(1)}, u32[]{:S(2)}, u32[]{:S(2)}) collective-permute-start(bf16[784,768]{1,0:T(8,128)(2,1)S(1)} %collective-permute-done.5.refs_1_), channel_id=1, source_target_pairs={{0,1},{1,0},{2,3},{3,2},{4,5},{5,4},{6,7},{7,6},{8,9},{9,8},{10,11... | collective-permute-start | bytes 3612680 | tf_op jit(solution)/shard_map/ppermute | solution.py:310
  56.7 5.9 %collective-permute-start.10 = (bf16[192,768]{1,0:T(8,128)(2,1)S(1)}, bf16[192,768]{1,0:T(8,128)(2,1)S(1)}, u32[]{:S(2)}, u32[]{:S(2)}) collective-permute-start(bf16[192,768]{1,0:T(8,128)(2,1)S(1)} %pad_maximum_fusion.11), channel_id=1, source_target_pairs={{0,2},{1,5},{2,0},{3,7},{4,6},{5,1},{6,4},{7,3},{8,10},{9,13},{10,... | collective-permute-start | bytes 884744 | tf_op jit(solution)/shard_map/ppermute | solution.py:310
  63.6 10.4 %collective-permute-start.11 = (bf16[384,768]{1,0:T(8,128)(2,1)S(1)}, bf16[384,768]{1,0:T(8,128)(2,1)S(1)}, u32[]{:S(2)}, u32[]{:S(2)}) collective-permute-start(bf16[384,768]{1,0:T(8,128)(2,1)S(1)} %pad_maximum_fusion.6), channel_id=1, source_target_pairs={{0,2},{1,5},{2,0},{3,7},{4,6},{5,1},{6,4},{7,3},{8,10},{9,13},{10,... | collective-permute-start | bytes 1769480 | tf_op jit(solution)/shard_map/ppermute | solution.py:310
  74.2 14.3 %copy-start.15 = (bf16[768,768]{1,0:T(8,128)(2,1)}, bf16[768,768]{1,0:T(8,128)(2,1)S(1)}, u32[]{:S(2)}) copy-start(bf16[768,768]{1,0:T(8,128)(2,1)S(1)} %pad_maximum_fusion.2.refs_4_) | copy-start | bytes 3538948
  74.2 17.9 %collective-permute-start.13 = (bf16[768,768]{1,0:T(8,128)(2,1)S(1)}, bf16[768,768]{1,0:T(8,128)(2,1)}, u32[]{:S(2)}, u32[]{:S(2)}) collective-permute-start(bf16[768,768]{1,0:T(8,128)(2,1)S(1)} %pad_maximum_fusion.2.refs_4_), channel_id=1, source_target_pairs={{0,1},{1,0},{2,3},{3,2},{4,5},{5,4},{6,7},{7,6},{8,9},{9,8},{10,11... | collective-permute-start | bytes 3538952 | tf_op jit(solution)/shard_map/ppermute | solution.py:310
  75.5 16.6 %collective-permute-start.12 = (bf16[768,768]{1,0:T(8,128)(2,1)S(1)}, bf16[768,768]{1,0:T(8,128)(2,1)}, u32[]{:S(2)}, u32[]{:S(2)}) collective-permute-start(bf16[768,768]{1,0:T(8,128)(2,1)S(1)} %pad_maximum_fusion.2.refs_4_), channel_id=1, source_target_pairs={{0,4},{1,3},{2,6},{3,1},{4,0},{5,7},{6,2},{7,5},{8,12},{9,11},{10,... | collective-permute-start | bytes 3538952 | tf_op jit(solution)/shard_map/ppermute | solution.py:310
  76.7 15.3 %collective-permute-start.14 = (bf16[384,768]{1,0:T(8,128)(2,1)S(1)}, bf16[384,768]{1,0:T(8,128)(2,1)S(1)}, u32[]{:S(2)}, u32[]{:S(2)}) collective-permute-start(bf16[384,768]{1,0:T(8,128)(2,1)S(1)} %pad_maximum_fusion.7), channel_id=1, source_target_pairs={{0,8},{1,9},{2,10},{3,11},{4,12},{5,13},{6,14},{7,15},{8,0},{9,1},... | collective-permute-start | bytes 1769480 | tf_op jit(solution)/shard_map/ppermute | solution.py:310
  92.1 11.6 %copy-start.16 = (bf16[768,768]{1,0:T(8,128)(2,1)}, bf16[768,768]{1,0:T(8,128)(2,1)S(1)}, u32[]{:S(2)}) copy-start(bf16[768,768]{1,0:T(8,128)(2,1)S(1)} %pad_maximum_fusion.3.refs_8_) | copy-start | bytes 3538948
  92.1 11.6 %collective-permute-start.17 = (bf16[768,768]{1,0:T(8,128)(2,1)}, bf16[768,768]{1,0:T(8,128)(2,1)S(1)}, u32[]{:S(2)}, u32[]{:S(2)}) collective-permute-start(bf16[768,768]{1,0:T(8,128)(2,1)} %collective-permute-done.12.refs_5_), channel_id=1, source_target_pairs={{0,1},{1,0},{2,3},{3,2},{4,5},{5,4},{6,7},{7,6},{8,9},{9,8},{10,11... | collective-permute-start | bytes 3538952 | tf_op jit(solution)/shard_map/ppermute | solution.py:310
  92.6 11.1 %collective-permute-start.16 = (bf16[768,768]{1,0:T(8,128)(2,1)S(1)}, bf16[768,768]{1,0:T(8,128)(2,1)S(1)}, u32[]{:S(2)}, u32[]{:S(2)}) collective-permute-start(bf16[768,768]{1,0:T(8,128)(2,1)S(1)} %pad_maximum_fusion.3.refs_8_), channel_id=1, source_target_pairs={{0,1},{1,0},{2,3},{3,2},{4,5},{5,4},{6,7},{7,6},{8,9},{9,8},{10,11... | collective-permute-start | bytes 3538952 | tf_op jit(solution)/shard_map/ppermute | solution.py:310
  92.7 15.3 %collective-permute-start.15 = (bf16[768,768]{1,0:T(8,128)(2,1)S(1)}, bf16[768,768]{1,0:T(8,128)(2,1)S(1)}, u32[]{:S(2)}, u32[]{:S(2)}) collective-permute-start(bf16[768,768]{1,0:T(8,128)(2,1)S(1)} %pad_maximum_fusion.3.refs_8_), channel_id=1, source_target_pairs={{0,4},{1,3},{2,6},{3,1},{4,0},{5,7},{6,2},{7,5},{8,12},{9,11},{10,... | collective-permute-start | bytes 3538952 | tf_op jit(solution)/shard_map/ppermute | solution.py:310
  103.8 8.1 %copy-start.28 = (bf16[768,768]{1,0:T(8,128)(2,1)}, bf16[768,768]{1,0:T(8,128)(2,1)S(1)}, u32[]{:S(2)}) copy-start(bf16[768,768]{1,0:T(8,128)(2,1)S(1)} %collective-permute-done.17.refs_7_) | copy-start | bytes 3538948
  103.8 8.0 %copy-start.29 = (bf16[768,768]{1,0:T(8,128)(2,1)}, bf16[768,768]{1,0:T(8,128)(2,1)S(1)}, u32[]{:S(2)}) copy-start(bf16[768,768]{1,0:T(8,128)(2,1)S(1)} %collective-permute-done.16.refs_10_) | copy-start | bytes 3538948
  108.1 3.8 %collective-permute-start.18 = (bf16[768,768]{1,0:T(8,128)(2,1)S(1)}, bf16[768,768]{1,0:T(8,128)(2,1)S(1)}, u32[]{:S(2)}, u32[]{:S(2)}) collective-permute-start(bf16[768,768]{1,0:T(8,128)(2,1)S(1)} %collective-permute-done.15.refs_9_), channel_id=1, source_target_pairs={{0,1},{1,0},{2,3},{3,2},{4,5},{5,4},{6,7},{7,6},{8,9},{9,8},{10,11... | collective-permute-start | bytes 3538952 | tf_op jit(solution)/shard_map/ppermute | solution.py:310
  165.4 6.8 %collective-permute-start.19 = (bf16[784,768]{1,0:T(8,128)(2,1)}, bf16[784,768]{1,0:T(8,128)(2,1)S(1)}, u32[]{:S(2)}, u32[]{:S(2)}) collective-permute-start(bf16[784,768]{1,0:T(8,128)(2,1)} %get-tuple-element.245), channel_id=1, source_target_pairs={{0,1},{1,0},{2,3},{3,2},{4,5},{5,4},{6,7},{7,6},{8,9},{9,8},{10,11... | collective-permute-start | bytes 3612680 | tf_op jit(solution)/shard_map/ppermute | solution.py:310
  165.9 6.3 %collective-permute-start.20 = (bf16[768,768]{1,0:T(8,128)(2,1)}, bf16[768,768]{1,0:T(8,128)(2,1)S(1)}, u32[]{:S(2)}, u32[]{:S(2)}) collective-permute-start(bf16[768,768]{1,0:T(8,128)(2,1)} %get-tuple-element.246), channel_id=1, source_target_pairs={{0,1},{1,0},{2,3},{3,2},{4,5},{5,4},{6,7},{7,6},{8,9},{9,8},{10,11... | collective-permute-start | bytes 3538952 | tf_op jit(solution)/shard_map/ppermute | solution.py:310
  166.0 6.2 %copy-start.21 = (f32[16,768]{1,0:T(8,128)S(1)}, f32[16,768]{1,0:T(8,128)}, u32[]{:S(2)}) copy-start(f32[16,768]{1,0:T(8,128)} %get-tuple-element.239.sums_ref) | copy-start | bytes 147460
  166.0 7.3 %copy-start.14 = (bf16[768,768]{1,0:T(8,128)(2,1)S(1)}, bf16[768,768]{1,0:T(8,128)(2,1)}, u32[]{:S(2)}) copy-start(bf16[768,768]{1,0:T(8,128)(2,1)} %get-tuple-element.244) | copy-start | bytes 3538948
  173.7 16.6 %collective-permute-start.21 = (bf16[784,768]{1,0:T(8,128)(2,1)S(1)}, bf16[784,768]{1,0:T(8,128)(2,1)S(1)}, u32[]{:S(2)}, u32[]{:S(2)}) collective-permute-start(bf16[784,768]{1,0:T(8,128)(2,1)S(1)} %pad_maximum_fusion.1), channel_id=1, source_target_pairs={{0,4},{1,3},{2,6},{3,1},{4,0},{5,7},{6,2},{7,5},{8,12},{9,11},{10,... | collective-permute-start | bytes 3612680 | tf_op jit(solution)/shard_map/ppermute | solution.py:310
  174.9 15.4 %collective-permute-start.22 = (bf16[768,768]{1,0:T(8,128)(2,1)S(1)}, bf16[768,768]{1,0:T(8,128)(2,1)}, u32[]{:S(2)}, u32[]{:S(2)}) collective-permute-start(bf16[768,768]{1,0:T(8,128)(2,1)S(1)} %copy-done.12), channel_id=1, source_target_pairs={{0,1},{1,0},{2,3},{3,2},{4,5},{5,4},{6,7},{7,6},{8,9},{9,8},{10,11... | collective-permute-start | bytes 3538952 | tf_op jit(solution)/shard_map/ppermute | solution.py:310
  175.3 15.0 %collective-permute-start.23 = (bf16[768,768]{1,0:T(8,128)(2,1)S(1)}, bf16[768,768]{1,0:T(8,128)(2,1)}, u32[]{:S(2)}, u32[]{:S(2)}) collective-permute-start(bf16[768,768]{1,0:T(8,128)(2,1)S(1)} %copy-done.11), channel_id=1, source_target_pairs={{0,1},{1,0},{2,3},{3,2},{4,5},{5,4},{6,7},{7,6},{8,9},{9,8},{10,11... | collective-permute-start | bytes 3538952 | tf_op jit(solution)/shard_map/ppermute | solution.py:310
  194.2 15.8 %collective-permute-start.24 = (bf16[768,768]{1,0:T(8,128)(2,1)S(1)}, bf16[768,768]{1,0:T(8,128)(2,1)S(1)}, u32[]{:S(2)}, u32[]{:S(2)}) collective-permute-start(bf16[768,768]{1,0:T(8,128)(2,1)S(1)} %add_convert_fusion.1), channel_id=1, source_target_pairs={{0,4},{1,3},{2,6},{3,1},{4,0},{5,7},{6,2},{7,5},{8,12},{9,11},{10,... | collective-permute-start | bytes 3538952 | tf_op jit(solution)/shard_map/ppermute | solution.py:310
  194.9 15.1 %collective-permute-start.25 = (bf16[400,768]{1,0:T(8,128)(2,1)S(1)}, bf16[400,768]{1,0:T(8,128)(2,1)S(1)}, u32[]{:S(2)}, u32[]{:S(2)}) collective-permute-start(bf16[400,768]{1,0:T(8,128)(2,1)S(1)} %pad_maximum_fusion.5), channel_id=1, source_target_pairs={{0,8},{1,9},{2,10},{3,11},{4,12},{5,13},{6,14},{7,15},{8,0},{9,1},... | collective-permute-start | bytes 1843208 | tf_op jit(solution)/shard_map/ppermute | solution.py:310
  213.0 12.5 %collective-permute-start.26 = (bf16[384,768]{1,0:T(8,128)(2,1)S(1)}, bf16[384,768]{1,0:T(8,128)(2,1)S(1)}, u32[]{:S(2)}, u32[]{:S(2)}) collective-permute-start(bf16[384,768]{1,0:T(8,128)(2,1)S(1)} %get-tuple-element.289), channel_id=1, source_target_pairs={{0,2},{1,5},{2,0},{3,7},{4,6},{5,1},{6,4},{7,3},{8,10},{9,13},{10,... | collective-permute-start | bytes 1769480 | tf_op jit(solution)/shard_map/ppermute | solution.py:310
  214.2 11.4 %collective-permute-start.27 = (bf16[208,768]{1,0:T(8,128)(2,1)S(1)}, bf16[208,768]{1,0:T(8,128)(2,1)S(1)}, u32[]{:S(2)}, u32[]{:S(2)}) collective-permute-start(bf16[208,768]{1,0:T(8,128)(2,1)S(1)} %pad_maximum_fusion.9), channel_id=1, source_target_pairs={{0,2},{1,5},{2,0},{3,7},{4,6},{5,1},{6,4},{7,3},{8,10},{9,13},{10,... | collective-permute-start | bytes 958472 | tf_op jit(solution)/shard_map/ppermute | solution.py:310
  225.6 7.3 %copy-start.13 = (bf16[768,768]{1,0:T(8,128)(2,1)S(1)}, bf16[768,768]{1,0:T(8,128)(2,1)}, u32[]{:S(2)}) copy-start(bf16[768,768]{1,0:T(8,128)(2,1)} %get-tuple-element.305) | copy-start | bytes 3538948
  227.2 5.7 %collective-permute-start.28 = (bf16[768,768]{1,0:T(8,128)(2,1)S(1)}, bf16[768,768]{1,0:T(8,128)(2,1)S(1)}, u32[]{:S(2)}, u32[]{:S(2)}) collective-permute-start(bf16[768,768]{1,0:T(8,128)(2,1)S(1)} %copy-done.31), channel_id=1, source_target_pairs={{0,1},{1,0},{2,3},{3,2},{4,5},{5,4},{6,7},{7,6},{8,9},{9,8},{10,11... | collective-permute-start | bytes 3538952 | tf_op jit(solution)/shard_map/ppermute | solution.py:310
  229.4 19.4 %collective-permute-start.30 = (bf16[768,768]{1,0:T(8,128)(2,1)}, bf16[768,768]{1,0:T(8,128)(2,1)S(1)}, u32[]{:S(2)}, u32[]{:S(2)}) collective-permute-start(bf16[768,768]{1,0:T(8,128)(2,1)} %get-tuple-element.313), channel_id=1, source_target_pairs={{0,1},{1,0},{2,3},{3,2},{4,5},{5,4},{6,7},{7,6},{8,9},{9,8},{10,11... | collective-permute-start | bytes 3538952 | tf_op jit(solution)/shard_map/ppermute | solution.py:310
  233.1 15.6 %collective-permute-start.29 = (bf16[768,768]{1,0:T(8,128)(2,1)S(1)}, bf16[768,768]{1,0:T(8,128)(2,1)S(1)}, u32[]{:S(2)}, u32[]{:S(2)}) collective-permute-start(bf16[768,768]{1,0:T(8,128)(2,1)S(1)} %add_convert_fusion), channel_id=1, source_target_pairs={{0,4},{1,3},{2,6},{3,1},{4,0},{5,7},{6,2},{7,5},{8,12},{9,11},{10,... | collective-permute-start | bytes 3538952 | tf_op jit(solution)/shard_map/ppermute | solution.py:310
  233.8 14.9 %collective-permute-start.32 = (bf16[112,768]{1,0:T(8,128)(2,1)}, bf16[112,768]{1,0:T(8,128)(2,1)S(1)}, u32[]{:S(2)}, u32[]{:S(2)}) collective-permute-start(bf16[112,768]{1,0:T(8,128)(2,1)} %pad_maximum_fusion.13), channel_id=1, source_target_pairs={{0,16},{1,17},{2,18},{3,19},{4,20},{5,21},{6,22},{7,23},{8,24},{9,... | collective-permute-start | bytes 516104 | tf_op jit(solution)/shard_map/ppermute | solution.py:310
  236.8 11.9 %collective-permute-start.31 = (bf16[192,768]{1,0:T(8,128)(2,1)}, bf16[192,768]{1,0:T(8,128)(2,1)}, u32[]{:S(2)}, u32[]{:S(2)}) collective-permute-start(bf16[192,768]{1,0:T(8,128)(2,1)} %get-tuple-element.314), channel_id=1, source_target_pairs={{0,8},{1,9},{2,10},{3,11},{4,12},{5,13},{6,14},{7,15},{8,0},{9,1},... | collective-permute-start | bytes 884744 | tf_op jit(solution)/shard_map/ppermute | solution.py:310
  237.3 12.4 %copy-start.17 = (bf16[768,768]{1,0:T(8,128)(2,1)S(1)}, bf16[768,768]{1,0:T(8,128)(2,1)}, u32[]{:S(2)}) copy-start(bf16[768,768]{1,0:T(8,128)(2,1)} %get-tuple-element.311) | copy-start | bytes 3538948
  250.2 11.7 %copy-start.20 = (bf16[208,768]{1,0:T(8,128)(2,1)S(1)}, bf16[208,768]{1,0:T(8,128)(2,1)}, u32[]{:S(2)}) copy-start(bf16[208,768]{1,0:T(8,128)(2,1)} %copy-done.19) | copy-start | bytes 958468
  250.2 10.5 %collective-permute-start.33 = (bf16[384,768]{1,0:T(8,128)(2,1)S(1)}, bf16[384,768]{1,0:T(8,128)(2,1)S(1)}, u32[]{:S(2)}, u32[]{:S(2)}) collective-permute-start(bf16[384,768]{1,0:T(8,128)(2,1)S(1)} %get-tuple-element.321), channel_id=1, source_target_pairs={{0,2},{1,5},{2,0},{3,7},{4,6},{5,1},{6,4},{7,3},{8,10},{9,13},{10,... | collective-permute-start | bytes 1769480 | tf_op jit(solution)/shard_map/ppermute | solution.py:310
  251.3 9.4 %collective-permute-start.34 = (bf16[96,768]{1,0:T(8,128)(2,1)S(1)}, bf16[96,768]{1,0:T(8,128)(2,1)S(1)}, u32[]{:S(2)}, u32[]{:S(2)}) collective-permute-start(bf16[96,768]{1,0:T(8,128)(2,1)S(1)} %add_convert_fusion.19), channel_id=1, source_target_pairs={{0,16},{1,17},{2,18},{3,19},{4,20},{5,21},{6,22},{7,23},{8,24},{9,... | collective-permute-start | bytes 442376 | tf_op jit(solution)/shard_map/ppermute | solution.py:310
  253.5 2.8 collective-permute-start.35
  260.9 2.7 collective-permute-start.37
  261.8 7.4 %collective-permute-start.36 = (bf16[192,768]{1,0:T(8,128)(2,1)S(1)}, bf16[192,768]{1,0:T(8,128)(2,1)S(1)}, u32[]{:S(2)}, u32[]{:S(2)}) collective-permute-start(bf16[192,768]{1,0:T(8,128)(2,1)S(1)} %get-tuple-element.327), channel_id=1, source_target_pairs={{0,8},{1,9},{2,10},{3,11},{4,12},{5,13},{6,14},{7,15},{8,0},{9,1},... | collective-permute-start | bytes 884744 | tf_op jit(solution)/shard_map/ppermute | solution.py:310
  263.6 3.0 %collective-permute-start.38 = (bf16[16,768]{1,0:T(8,128)(2,1)S(1)}, bf16[16,768]{1,0:T(8,128)(2,1)S(1)}, u32[]{:S(2)}, u32[]{:S(2)}) collective-permute-start(bf16[16,768]{1,0:T(8,128)(2,1)S(1)} %fusion.2), channel_id=1, source_target_pairs={{0,4},{1,3},{2,6},{3,1},{4,0},{5,7},{6,2},{7,5},{8,12},{9,11},{10,... | collective-permute-start | bytes 73736 | tf_op jit(solution)/shard_map/ppermute | solution.py:310
  265.3 21.0 %copy-start.1 = (f32[1154,128]{1,0:T(8,128)S(1)}, f32[1154,128]{1,0:T(8,128)}, u32[]{:S(2)}) copy-start(f32[1154,128]{1,0:T(8,128)} %w_ref.2) | copy-start | bytes 1772548
  265.3 21.0 %copy-start.4 = (f32[1154,128]{1,0:T(8,128)S(1)}, f32[1154,128]{1,0:T(8,128)}, u32[]{:S(2)}) copy-start(f32[1154,128]{1,0:T(8,128)} %m_ref.2) | copy-start | bytes 1772548
  265.3 21.0 %copy-start.5 = (f32[1154,128]{1,0:T(8,128)S(1)}, f32[1154,128]{1,0:T(8,128)}, u32[]{:S(2)}) copy-start(f32[1154,128]{1,0:T(8,128)} %a_ref.2) | copy-start | bytes 1772548
  269.4 6.6 %collective-permute-start.40 = (bf16[16,768]{1,0:T(8,128)(2,1)S(1)}, bf16[16,768]{1,0:T(8,128)(2,1)S(1)}, u32[]{:S(2)}, u32[]{:S(2)}) collective-permute-start(bf16[16,768]{1,0:T(8,128)(2,1)S(1)} %convert_element_type.371), channel_id=1, source_target_pairs={{0,8},{1,9},{2,10},{3,11},{4,12},{5,13},{6,14},{7,15},{8,0},{9,1},... | collective-permute-start | bytes 73736 | tf_op jit(solution)/shard_map/ppermute | solution.py:310
  269.4 7.6 %collective-permute-start.41 = (f32[64,128]{1,0:T(8,128)S(1)}, f32[64,128]{1,0:T(8,128)S(1)}, u32[]{:S(2)}, u32[]{:S(2)}) collective-permute-start(f32[64,128]{1,0:T(8,128)S(1)} %slice.253), channel_id=1, source_target_pairs={{1,0},{2,1},{3,2},{4,3},{5,4},{6,5},{7,6},{8,7},{9,8},{10,9},{11,1... | collective-permute-start | bytes 98312 | tf_op jit(solution)/shard_map/ppermute | solution.py:1206
  273.7 9.6 %collective-permute-start.39 = (bf16[96,768]{1,0:T(8,128)(2,1)S(1)}, bf16[96,768]{1,0:T(8,128)(2,1)S(1)}, u32[]{:S(2)}, u32[]{:S(2)}) collective-permute-start(bf16[96,768]{1,0:T(8,128)(2,1)S(1)} %add_convert_fusion.17), channel_id=1, source_target_pairs={{0,16},{1,17},{2,18},{3,19},{4,20},{5,21},{6,22},{7,23},{8,24},{9,... | collective-permute-start | bytes 442376 | tf_op jit(solution)/shard_map/ppermute | solution.py:310
  283.2 4.5 %collective-permute-start.43 = (bf16[16,768]{1,0:T(8,128)(2,1)S(1)}, bf16[16,768]{1,0:T(8,128)(2,1)S(1)}, u32[]{:S(2)}, u32[]{:S(2)}) collective-permute-start(bf16[16,768]{1,0:T(8,128)(2,1)S(1)} %convert_element_type.374), channel_id=1, source_target_pairs={{0,16},{1,17},{2,18},{3,19},{4,20},{5,21},{6,22},{7,23},{8,24},{9,... | collective-permute-start | bytes 73736 | tf_op jit(solution)/shard_map/ppermute | solution.py:310
  283.4 8.8 %copy-start.3 = (f32[578,128]{1,0:T(8,128)S(1)}, f32[578,128]{1,0:T(8,128)}, u32[]{:S(2)}) copy-start(f32[578,128]{1,0:T(8,128)} %w_ref.3) | copy-start | bytes 887812
  283.4 8.8 %copy-start.6 = (f32[578,128]{1,0:T(8,128)S(1)}, f32[578,128]{1,0:T(8,128)}, u32[]{:S(2)}) copy-start(f32[578,128]{1,0:T(8,128)} %m_ref.3) | copy-start | bytes 887812
  283.4 8.8 %copy-start.7 = (f32[578,128]{1,0:T(8,128)S(1)}, f32[578,128]{1,0:T(8,128)}, u32[]{:S(2)}) copy-start(f32[578,128]{1,0:T(8,128)} %a_ref.3) | copy-start | bytes 887812
  283.4 8.8 %collective-permute-start.42 = (f32[64,128]{1,0:T(8,128)S(1)}, f32[64,128]{1,0:T(8,128)S(1)}, u32[]{:S(2)}, u32[]{:S(2)}) collective-permute-start(f32[64,128]{1,0:T(8,128)S(1)} %slice.271), channel_id=1, source_target_pairs={{1,0},{2,1},{3,2},{4,3},{5,4},{6,5},{7,6},{8,7},{9,8},{10,9},{11,1... | collective-permute-start | bytes 98312 | tf_op jit(solution)/shard_map/ppermute | solution.py:1210
  (13 other events, 22.4 us)
